TPU v7x, 128 devices: a whole 4x4x4 slice. The times are simulated.
128 devices in a mesh: dp: 16 (over y, z), tensor: 8 (over x, core).
Axes of the slice: x: 4, y: 4, z: 4, core: 2. Of those that a mesh axis runs over, the one named last changes fastest.
Arguments:
- grads: bfloat16 [16, 1024, 28672], P('dp', None, 'tensor'), may hold values from -6 to 6
- errors: bfloat16 [16, 1024, 28672], P('dp', None, 'tensor'), may hold values from -4 to 4
- basis: float32 [28672, 32], P('tensor'), may hold values from -6 to 6
Outputs:
- new_errors: bfloat16 [16, 1024, 28672], P('dp', None, 'tensor')
- p_basis: float32 [1024, 32], P('tensor')
- q_basis: float32 [28672, 32], P('tensor')
All inputs are finite; a program needn't handle non-finite values.
Results may differ from a plain program's by a relative error of at most 0.014.
Values may be sent and summed in bfloat16 or wider, within the bound.
No kernel may reach another device: no remote copies, remote signals or barrier semaphores. Data moves between devices by JAX's collectives and lax.ppermute only.
A program may use at most 64 MiB of HBM per device.

v0:
```python
import jax
import jax.numpy as jnp
from jax import lax
from jax.sharding import PartitionSpec as P


def split_up(value, dim, count):
    before, after = (value.shape[:dim], value.shape[dim + 1 :])
    return jnp.moveaxis(value.reshape(*before, count, -1, *after), dim, 0)


def summed_on_arrival(value, axis, dim):
    count = lax.axis_size(axis)
    pieces = lax.all_to_all(split_up(value, dim, count), axis, 0, 0, tiled=True)
    return jnp.sum(pieces, axis=0)


def copy_for_each(value, axis):
    copies = jnp.broadcast_to(value, (lax.axis_size(axis), *value.shape))
    return lax.all_to_all(copies, axis, split_axis=0, concat_axis=0, tiled=True)


def of_everyone(value, axis):
    everything = copy_for_each(value, axis)
    return jnp.sum(everything, axis=0)


def joined_along(pieces, dim):
    pieces = jnp.moveaxis(pieces, 0, dim)
    dims = pieces.shape
    return pieces.reshape(*dims[:dim], dims[dim] * dims[dim + 1], *dims[dim + 2 :])


def gathered_copies(value, axis, dim):
    return joined_along(copy_for_each(value, axis), dim)


def filled_up(lines, count):
    spare = -lines.shape[0] % count
    if not spare:
        return lines
    return jnp.concatenate([lines, jnp.zeros((spare, *lines.shape[1:]), lines.dtype)])


def sent_and_summed(value, axis, dim):
    pieces = split_up(value, dim, lax.axis_size(axis))
    arrived = lax.all_to_all(pieces, axis, split_axis=0, concat_axis=0, tiled=True)
    return arrived.astype(jnp.float32).sum(axis=0)


def nested_sum(value, axes):
    lines = value.reshape(-1, value.shape[-1])
    padded = filled_up(lines, lax.axis_size(axes))
    whole = gathered_copies(sent_and_summed(padded, axes, 0).astype(jnp.bfloat16), axes, 0)
    return lax.slice_in_dim(whole, 0, len(lines)).reshape(value.shape).astype(jnp.float32)


def orthonormal(p_rows, gram):
    lower = jnp.linalg.cholesky(gram)
    return jax.scipy.linalg.solve_triangular(lower, p_rows.T, lower=True).T


def on_device(grads, errors, basis):
    matrix = (grads[0].astype(jnp.float32) + errors[0].astype(jnp.float32)).astype(jnp.bfloat16)
    partial_p = jnp.dot(matrix, basis.astype(jnp.bfloat16), preferred_element_type=jnp.float32)
    p_block = summed_on_arrival(partial_p, "tensor", 0)
    p_block = of_everyone(p_block, "dp")
    local_gram = jnp.dot(p_block.T, p_block, precision=lax.Precision.HIGHEST)
    gram = of_everyone(local_gram, "tensor")
    p_basis = orthonormal(p_block, gram)
    p_b = gathered_copies(p_basis.astype(jnp.bfloat16), "tensor", 0)
    local_q = lax.dot_general(
        matrix, p_b, (((0,), (0,)), ((), ())), preferred_element_type=jnp.float32
    )
    q_basis = nested_sum(local_q.astype(jnp.bfloat16), "dp") / lax.axis_size("dp")
    approx = jnp.dot(p_b, q_basis.astype(jnp.bfloat16).T, preferred_element_type=jnp.float32)
    new_errors = (matrix.astype(jnp.float32) - approx).astype(jnp.bfloat16)[None]
    return (new_errors, p_basis, q_basis)


def solution(mesh):
    return jax.shard_map(
        on_device,
        mesh=mesh,
        in_specs=(P("dp", None, "tensor"), P("dp", None, "tensor"), P("tensor", None)),
        out_specs=(P("dp", None, "tensor"), P("tensor", None), P("tensor", None)),
        check_vma=False,
    )
```

profile of v0, /device:TPU:0, one launch (start us, length us, event | category | flops | bytes accessed | tf_op | source)
XLA Modules:
  0.0 107.0 jit_solution(37508095320860198)
XLA Ops:
  0.6 10.2 %add_convert_fusion = bf16[1,1024,3584]{2,1,0:T(8,128)(2,1)} fusion(bf16[1,1024,3584]{2,1,0:T(8,128)(2,1)} %param.4, bf16[1,1024,3584]{2,1,0:T(8,128)(2,1)} %param.3), kind=kLoop, calls=%fused_computation.1 | loop fusion | flops 14680064 | bytes 22020096 | tf_op jit(solution)/shard_map/convert_element_type | solution.py:64
  10.9 5.3 %fusion.6 = f32[8,128,32]{1,2,0:T(8,128)S(1)} fusion(bf16[8,128,3584]{2,1,0:T(8,128)(2,1)} %bitcast.48, f32[3584,32]{0,1:T(8,128)S(1)} %copy-done), kind=kOutput, calls=%fused_computation.7 | convolution fusion | flops 234995712 | bytes 7929856 | tf_op jit(solution)/shard_map/dot_general | solution.py:65
  16.1 10.3 %all_to_all.30 = f32[8,128,32]{1,2,0:T(8,128)S(1)} all-to-all(f32[8,128,32]{1,2,0:T(8,128)S(1)} %fusion.6), channel_id=1, replica_groups=mesh['dp'=16,'tensor'=8] {'tensor'}, dimensions={0} | all-to-all | bytes 262144 | tf_op jit(solution)/shard_map/all_to_all | solution.py:14
  26.5 16.4 %all_to_all.31 = f32[16,128,32]{1,2,0:T(8,128)S(1)} all-to-all(f32[16,128,32]{1,2,0:T(8,128)S(1)} %broadcast_in_dim.17), channel_id=1, replica_groups=mesh['dp'=16,'tensor'=8] {'dp'}, dimensions={0} | all-to-all | bytes 524288 | tf_op jit(solution)/shard_map/all_to_all | solution.py:20
  42.9 0.1 fusion.19
  43.1 0.1 reshape.45
  43.2 7.8 %all_to_all.32 = f32[8,1,1024]{2,1,0:T(1,128)S(1)} all-to-all(f32[8,1,1024]{2,1,0:T(1,128)S(1)} %reshape.45), channel_id=1, replica_groups=mesh['dp'=16,'tensor'=8] {'tensor'}, dimensions={0} | all-to-all | bytes 65536 | tf_op jit(solution)/shard_map/all_to_all | solution.py:20
  51.0 0.5 broadcast.57
  51.5 0.7 reduce.7
  52.4 2.9 %cholesky.16 = f32[32,32]{1,0:T(8,128)S(1)} custom-call(f32[32,32]{1,0:T(8,128)S(1)} %fusion.17), custom_call_target="Cholesky" | custom-call | tf_op jit(solution)/shard_map/jit(cholesky)/cholesky | solution.py:59
  55.4 0.6 compare_reduce_fusion
  56.0 0.7 fusion.14
  56.7 2.4 %custom-call.7 = f32[1,32,32]{1,2,0:T(8,128)S(1)} custom-call(f32[1,32,32]{2,1,0:T(8,128)S(1)} %fusion.14), custom_call_target="InvertDiagBlocksLowerTriangular" | custom-call | tf_op jit(solution)/shard_map/jit(_solve_triangular)/triangular_solve | solution.py:60
  59.1 0.8 fusion.18
  60.0 8.0 %all_to_all.33 = bf16[8,128,32]{1,2,0:T(8,128)(2,1)S(1)} all-to-all(bf16[8,128,32]{1,2,0:T(8,128)(2,1)S(1)} %broadcast_in_dim.19), channel_id=1, replica_groups=mesh['dp'=16,'tensor'=8] {'tensor'}, dimensions={0} | all-to-all | bytes 131072 | tf_op jit(solution)/shard_map/all_to_all | solution.py:20
  68.0 4.4 %fusion.3 = bf16[3584,32]{0,1:T(8,128)(2,1)S(1)} fusion(bf16[1,1024,3584]{2,1,0:T(8,128)(2,1)} %add_convert_fusion, bf16[8,128,32]{1,2,0:T(8,128)(2,1)S(1)} %all_to_all.33), kind=kOutput, calls=%fused_computation.5 | convolution fusion | flops 234995712 | bytes 7634944 | tf_op jit(solution)/shard_map/dot_general | solution.py:72
  72.4 0.4 reshape.43
  72.9 11.9 %all_to_all.34 = bf16[16,224,32]{1,2,0:T(8,128)(2,1)S(1)} all-to-all(bf16[16,224,32]{1,2,0:T(8,128)(2,1)S(1)} %copy.22), channel_id=1, replica_groups=mesh['dp'=16,'tensor'=8] {'dp'}, dimensions={0} | all-to-all | bytes 458752 | tf_op jit(solution)/shard_map/all_to_all | solution.py:47
  84.9 11.9 %all_to_all.35 = bf16[16,224,32]{1,2,0:T(8,128)(2,1)S(1)} all-to-all(bf16[16,224,32]{1,2,0:T(8,128)(2,1)S(1)} %broadcast_in_dim.20), channel_id=1, replica_groups=mesh['dp'=16,'tensor'=8] {'dp'}, dimensions={0} | all-to-all | bytes 458752 | tf_op jit(solution)/shard_map/all_to_all | solution.py:20
  96.9 0.2 copy.23
  97.1 0.4 convert_element_type.65
  97.4 0.3 copy.24
  97.7 1.1 div.20
  98.8 8.2 %fusion.2 = bf16[1,1024,3584]{2,1,0:T(8,128)(2,1)} fusion(bf16[3584,32]{0,1:T(8,128)(2,1)S(1)} %convert_element_type.65, bf16[1,1024,3584]{2,1,0:T(8,128)(2,1)} %add_convert_fusion, bf16[8,128,32]{1,2,0:T(8,128)(2,1)S(1)} %all_to_all.33), kind=kOutput, calls=%fused_computation.4 | convolution fusion | flops 245891072 | bytes 14974976 | tf_op jit(solution)/shard_map/dot_general | solution.py:76
  (16 shorter events, 0.5 us)
Async XLA Ops:
  0.6 10.2 %copy-start = (f32[3584,32]{0,1:T(8,128)S(1)}, f32[3584,32]{0,1:T(8,128)}, u32[]{:S(2)}) copy-start(f32[3584,32]{0,1:T(8,128)} %param.5) | copy-start | bytes 1376260
where the time goes:
time: 108 us; the launch traced here: 107 us
  blocking collectives  66.3 us (61%)
  matrix products  18.9 us (17%)
  other arithmetic  17.8 us (16%)
  local copies, waits for them, and re-layouts  3.21 us (3%)
    all_to_all x4, blocking collectives, copy_for_each(): return lax.all_to_all(copies, axis, split_axis=0, concat_axis=0, tiled=True)  44.1 us
    all_to_all x1, blocking collectives, sent_and_summed(): lax.all_to_all(pieces, axis, split_axis=0, concat_axis=0, tiled=True)  11.9 us
    all_to_all x1, blocking collectives, summed_on_arrival(): pieces = lax.all_to_all(split_up(value, dim, count), axis, 0, 0, tiled=True)  10.3 us
    convert_element_type x1, other arithmetic, on_device(): (grads[0].astype(jnp.float32) + errors[0].astype(jnp.float32)).astype(jnp...  10.2 us
    dot_general x1, matrix products, on_device(): jnp.dot(p_b, q_basis.astype(jnp.bfloat16).T, preferred_element_type=jnp.f...  8.23 us
    dot_general x1, matrix products, on_device(): jnp.dot(matrix, basis.astype(jnp.bfloat16), preferred_element_type=jnp.fl...  5.29 us
    dot_general x1, matrix products, on_device(): lax.dot_general(matrix, p_b, (((0,), (0,)), ((), ())), preferred_element_...  4.43 us
    another operation x3, other arithmetic, orthonormal(): lower = jnp.linalg.cholesky(gram)  3.6 us

commit v1 on v0

v1 whole, which is shorter than its diff:
```python
import functools

import jax
import jax.numpy as jnp
from jax import lax
from jax.experimental import pallas as pl
from jax.experimental.pallas import tpu as pltpu
from jax.sharding import PartitionSpec as P

BF16, F32 = jnp.bfloat16, jnp.float32
HIGHEST = lax.Precision.HIGHEST
LAST_BY_LAST = (((1,), (1,)), ((), ()))
IN_VMEM = pl.BlockSpec(memory_space=pltpu.VMEM)
IN_HBM = pl.BlockSpec(memory_space=pltpu.HBM)
LANES = 128
CHUNKS = 8


def merge_kernel(grads, errors, basis_t, matrix, partial, held, basis, grad_sems, error_sems, basis_sem):
    rows = matrix.shape[0]
    step = rows // CHUNKS
    pltpu.make_async_copy(basis_t, basis, basis_sem).start()
    for i in range(CHUNKS):
        part = pl.ds(i * step, step)
        pltpu.make_async_copy(grads.at[0, part], matrix.at[part], grad_sems.at[i]).start()
        pltpu.make_async_copy(errors.at[0, part], held.at[part], error_sems.at[i]).start()
    pltpu.make_async_copy(basis_t, basis, basis_sem).wait()
    basis_b = basis[...].astype(BF16)
    for i in range(CHUNKS):
        part = pl.ds(i * step, step)
        pltpu.make_async_copy(grads.at[0, part], matrix.at[part], grad_sems.at[i]).wait()
        pltpu.make_async_copy(errors.at[0, part], held.at[part], error_sems.at[i]).wait()
        total = matrix[part, :] + held[part, :]
        matrix[part, :] = total
        product = lax.dot_general(total, basis_b, LAST_BY_LAST, preferred_element_type=F32)
        partial[i] = product.T


def merge(grads, errors, basis_t):
    rows, cols = grads.shape[1:]
    rank = basis_t.shape[0]
    return pl.pallas_call(
        merge_kernel,
        out_shape=(
            jax.ShapeDtypeStruct((rows, cols), BF16),
            jax.ShapeDtypeStruct((rows // LANES, rank, LANES), F32),
        ),
        in_specs=[IN_HBM] * 3,
        out_specs=(IN_VMEM, IN_VMEM),
        scratch_shapes=[
            pltpu.VMEM((rows, cols), BF16),
            pltpu.VMEM((rank, cols), F32),
            pltpu.SemaphoreType.DMA((CHUNKS,)),
            pltpu.SemaphoreType.DMA((CHUNKS,)),
            pltpu.SemaphoreType.DMA(()),
        ],
        compiler_params=pltpu.CompilerParams(vmem_limit_bytes=24 << 20),
        name="merge",
    )(grads, errors, basis_t)


def inverse_factor(gram):
    rank = gram.shape[0]
    row = lax.broadcasted_iota(jnp.int32, (rank, LANES), 0)
    lane = lax.broadcasted_iota(jnp.int32, (rank, LANES), 1)
    work = jnp.concatenate([gram, jnp.zeros((rank, LANES - rank), F32)], axis=1)
    work = work + jnp.where(lane == row + rank, 1.0, 0.0)
    scale = jnp.zeros((rank, LANES), F32)
    for k in range(rank):
        column = jnp.broadcast_to(work[:, k : k + 1], (rank, LANES))
        pivot_row = jnp.broadcast_to(work[k : k + 1, :], (rank, LANES))
        pivot = jnp.broadcast_to(column[k : k + 1, :], (rank, LANES))
        scale = jnp.where(row == k, pivot, scale)
        work = work - jnp.where(row > k, column / pivot, 0.0) * pivot_row
    return (work * lax.rsqrt(scale))[:, rank : 2 * rank]


def project_kernel(pieces, own, matrix, p_own, p_b, q_pieces, whole):
    blocks, rank, _ = pieces.shape
    for i in range(blocks):
        whole[:, i * LANES : (i + 1) * LANES] = pieces[i]
    p_sum = whole[...]
    gram = lax.dot_general(p_sum, p_sum, LAST_BY_LAST, precision=HIGHEST, preferred_element_type=F32)
    inverse = inverse_factor(gram)
    p_own[...] = jnp.dot(inverse, own[0], precision=HIGHEST, preferred_element_type=F32)
    rounded = jnp.dot(inverse, p_sum, precision=HIGHEST, preferred_element_type=F32).astype(BF16)
    p_b[...] = rounded
    count, height, width = q_pieces.shape
    for j in range(count * height // rank):
        q = jnp.dot(rounded, matrix[:, j * width : (j + 1) * width], preferred_element_type=F32).astype(BF16)
        for s in range(rank // height):
            q_pieces[j * (rank // height) + s] = q[s * height : (s + 1) * height]


def project(pieces, own, matrix, count):
    blocks, rank, _ = pieces.shape
    rows, cols = matrix.shape
    height = 8
    width = cols * rank // (count * height)
    return pl.pallas_call(
        project_kernel,
        out_shape=(
            jax.ShapeDtypeStruct((rank, LANES), F32),
            jax.ShapeDtypeStruct((rank, rows), BF16),
            jax.ShapeDtypeStruct((count, height, width), BF16),
        ),
        in_specs=[IN_VMEM] * 3,
        out_specs=(IN_VMEM,) * 3,
        scratch_shapes=[pltpu.VMEM((rank, rows), F32)],
        compiler_params=pltpu.CompilerParams(vmem_limit_bytes=24 << 20),
        name="project",
    )(pieces, own, matrix)


def subtract_kernel(mean, q_pieces, p_b, matrix, new_errors, q_out, out_buf, q_buf, sems, q_sem):
    rank = p_b.shape[0]
    count, height, width = q_pieces.shape
    rows, cols = matrix.shape
    per = rank // height
    step = rows // CHUNKS
    for j in range(count // per):
        for s in range(per):
            q_buf[s * height : (s + 1) * height, j * width : (j + 1) * width] = (
                q_pieces[j * per + s].astype(F32) * mean
            )
    pltpu.make_async_copy(q_buf, q_out, q_sem).start()
    q_b = q_buf[...].astype(BF16)
    left = p_b[...].T
    for i in range(CHUNKS):
        part = pl.ds(i * step, step)
        approx = jnp.dot(left[i * step : (i + 1) * step], q_b, preferred_element_type=F32)
        out_buf[part, :] = (matrix[part, :].astype(F32) - approx).astype(BF16)
        pltpu.make_async_copy(out_buf.at[part], new_errors.at[0, part], sems.at[i]).start()
    for i in range(CHUNKS):
        part = pl.ds(i * step, step)
        pltpu.make_async_copy(out_buf.at[part], new_errors.at[0, part], sems.at[i]).wait()
    pltpu.make_async_copy(q_buf, q_out, q_sem).wait()


def subtract(q_pieces, p_b, matrix):
    rows, cols = matrix.shape
    rank = p_b.shape[0]
    count = q_pieces.shape[0]
    return pl.pallas_call(
        functools.partial(subtract_kernel, 1.0 / count),
        out_shape=(
            jax.ShapeDtypeStruct((1, rows, cols), BF16),
            jax.ShapeDtypeStruct((rank, cols), F32),
        ),
        in_specs=[IN_VMEM] * 3,
        out_specs=(IN_HBM, IN_HBM),
        scratch_shapes=[
            pltpu.VMEM((rows, cols), BF16),
            pltpu.VMEM((rank, cols), F32),
            pltpu.SemaphoreType.DMA((CHUNKS,)),
            pltpu.SemaphoreType.DMA(()),
        ],
        compiler_params=pltpu.CompilerParams(vmem_limit_bytes=24 << 20),
        name="subtract",
    )(q_pieces, p_b, matrix)


def total_kernel(pieces, copies):
    total = pieces[0].astype(F32)
    for i in range(1, pieces.shape[0]):
        total = total + pieces[i].astype(F32)
    total = total.astype(copies.dtype)
    for i in range(copies.shape[0]):
        copies[i] = total


def summed_copies(pieces, count):
    return pl.pallas_call(
        total_kernel,
        out_shape=jax.ShapeDtypeStruct((count, *pieces.shape[1:]), pieces.dtype),
        in_specs=[IN_VMEM],
        out_specs=IN_VMEM,
        compiler_params=pltpu.CompilerParams(vmem_limit_bytes=4 << 20),
        name="summed_copies",
    )(pieces)


def exchanged(pieces, axis):
    return lax.all_to_all(pieces, axis, split_axis=0, concat_axis=0, tiled=True)


def on_device(grads, errors, basis):
    n_dp, n_tensor = lax.axis_size("dp"), lax.axis_size("tensor")
    matrix, partial = merge(grads, errors, basis.T)
    p_terms = exchanged(summed_copies(exchanged(partial, "tensor"), n_dp), "dp")
    p_copies = summed_copies(p_terms, n_tensor)
    p_own, p_b, q_pieces = project(exchanged(p_copies, "tensor"), p_copies, matrix, n_dp)
    q_sums = exchanged(summed_copies(exchanged(q_pieces, "dp"), n_dp), "dp")
    new_errors, q_out = subtract(q_sums, p_b, matrix)
    return new_errors, p_own.T, q_out.T


def solution(mesh):
    return jax.shard_map(
        on_device,
        mesh=mesh,
        in_specs=(P("dp", None, "tensor"), P("dp", None, "tensor"), P("tensor", None)),
        out_specs=(P("dp", None, "tensor"), P("tensor", None), P("tensor", None)),
        check_vma=False,
    )
```

time: 108 us -> 85.4 us (0.79)
  matrix products: 18.9 us -> 0 us
  Pallas kernels: 0 us -> 18.4 us
  other arithmetic: 17.8 us -> 0 us
  blocking collectives: 66.3 us -> 58.7 us
  local copies, waits for them, and re-layouts: 3.21 us -> 7.18 us
    pallas_call x0 -> x6, Pallas kernels: none -> 18.4 us  [the longest x1 9.1 us: merge(): pl.pallas_call(merge_kernel, out_shape=(jax.ShapeDtypeStruct((rows, cols)...]
    dot_general x4 -> x0, matrix products: 18.1 us -> none  [the longest x1 8.23 us: on_device(): jnp.dot(p_b, q_basis.astype(jnp.bfloat16).T, preferred_element_type=jnp.f...]
    convert_element_type x1 -> x0, other arithmetic: 10.2 us -> none  [on_device(): (grads[0].astype(jnp.float32) + errors[0].astype(jnp.float32)).astype(jnp...]
    all_to_all x6 -> x5, blocking collectives: 66.3 us -> 58.7 us  [exchanged(): return lax.all_to_all(pieces, axis, split_axis=0, concat_axis=0, tiled=True)]
    unnamed x4 -> x6, local copies, waits for them, and re-layouts: 0.21 us -> 7.18 us
    another operation x5 -> x0, other arithmetic: 6.68 us -> none  [the longest x3 3.6 us: orthonormal(): lower = jnp.linalg.cholesky(gram)]
    div x2 -> x0, local copies, waits for them, and re-layouts: 1.38 us -> none  [on_device(): nested_sum(local_q.astype(jnp.bfloat16), 'dp') / lax.axis_size('dp')]
where the time goes in v1:
time: 85.4 us; the launch traced here: 85 us
  blocking collectives  58.7 us (69%)
  Pallas kernels  18.4 us (22%)
  local copies, waits for them, and re-layouts  7.18 us (8%)
    all_to_all x5, blocking collectives, exchanged(): return lax.all_to_all(pieces, axis, split_axis=0, concat_axis=0, tiled=True)  58.7 us
    pallas_call x1, Pallas kernels, merge(): pl.pallas_call(merge_kernel, out_shape=(jax.ShapeDtypeStruct((rows, cols)...  9.1 us
    unnamed x6, local copies, waits for them, and re-layouts  7.18 us
    pallas_call x1, Pallas kernels, project(): pl.pallas_call(project_kernel, out_shape=(jax.ShapeDtypeStruct((rank, LAN...  5.62 us
    pallas_call x1, Pallas kernels, subtract(): pl.pallas_call(functools.partial(subtract_kernel, 1.0 / count), out_shape...  3.62 us

profile of v1, /device:TPU:0, one launch (start us, length us, event | category | flops | bytes accessed | tf_op | source)
XLA Modules:
  0.0 85.0 jit_solution(16696589417680721207)
XLA Ops:
  0.6 0.0 copy-start
  0.6 3.1 %copy-done = bf16[1,1024,3584]{2,1,0:T(8,128)(2,1)S(1)} copy-done((bf16[1,1024,3584]{2,1,0:T(8,128)(2,1)S(1)}, bf16[1,1024,3584]{2,1,0:T(8,128)(2,1)}, u32[]{:S(2)}) %copy-start) | copy-done | bytes 7340056
  3.7 0.0 copy-start.1
  3.7 3.1 %copy-done.1 = bf16[1,1024,3584]{2,1,0:T(8,128)(2,1)S(1)} copy-done((bf16[1,1024,3584]{2,1,0:T(8,128)(2,1)S(1)}, bf16[1,1024,3584]{2,1,0:T(8,128)(2,1)}, u32[]{:S(2)}) %copy-start.1) | copy-done | bytes 7340056
  6.8 0.0 copy-start.2
  6.8 1.0 %copy-done.2 = f32[3584,32]{0,1:T(8,128)S(1)} copy-done((f32[3584,32]{0,1:T(8,128)S(1)}, f32[3584,32]{0,1:T(8,128)}, u32[]{:S(2)}) %copy-start.2) | copy-done | bytes 458776
  7.8 9.1 %merge.1 = (bf16[1024,3584]{1,0:T(8,128)(2,1)S(1)}, f32[8,32,128]{2,1,0:T(8,128)S(1)}) custom-call(bf16[1,1024,3584]{2,1,0:T(8,128)(2,1)S(1)} %copy-done, bf16[1,1024,3584]{2,1,0:T(8,128)(2,1)S(1)} %copy-done.1, f32[32,3584]{1,0:T(8,128)S(1)} %bitcast.3), custom_call_target="tpu_custom_call" | custom-call | tf_op jit(solution)/shard_map/merge/pallas_call | solution.py:42
  16.9 10.3 %all_to_all.25.pieces = f32[8,32,128]{2,1,0:T(8,128)S(1)} all-to-all(f32[8,32,128]{2,1,0:T(8,128)S(1)} %get-tuple-element.10), channel_id=1, replica_groups=mesh['dp'=16,'tensor'=8] {'tensor'}, dimensions={0} | all-to-all | bytes 262144 | tf_op jit(solution)/shard_map/all_to_all | solution.py:184
  27.3 16.4 %all_to_all.26.pieces = f32[16,32,128]{2,1,0:T(8,128)S(1)} all-to-all(f32[16,32,128]{2,1,0:T(8,128)S(1)} %summed_copies.3), channel_id=1, replica_groups=mesh['dp'=16,'tensor'=8] {'dp'}, dimensions={0} | all-to-all | bytes 524288 | tf_op jit(solution)/shard_map/all_to_all | solution.py:184
  43.7 8.5 %all_to_all.27.pieces = f32[8,32,128]{2,1,0:T(8,128)S(1)} all-to-all(f32[8,32,128]{2,1,0:T(8,128)S(1)} %summed_copies.4.own), channel_id=1, replica_groups=mesh['dp'=16,'tensor'=8] {'tensor'}, dimensions={0} | all-to-all | bytes 262144 | tf_op jit(solution)/shard_map/all_to_all | solution.py:184
  52.2 5.6 %project.1 = (f32[32,128]{1,0:T(8,128)}, bf16[32,1024]{1,0:T(8,128)(2,1)S(1)}, bf16[16,8,896]{2,1,0:T(8,128)(2,1)S(1)}) custom-call(f32[8,32,128]{2,1,0:T(8,128)S(1)} %all_to_all.27.pieces, f32[8,32,128]{2,1,0:T(8,128)S(1)} %summed_copies.4.own, bf16[1024,3584]{1,0:T(8,128)(2,1)S(1)} %get-tuple-element.11.matrix), custom_call_target="tpu_custom_call" | custom-call | tf_op jit(solution)/shard_map/project/pallas_call | solution.py:100
  57.8 11.8 %all_to_all.28.pieces = bf16[16,8,896]{2,1,0:T(8,128)(2,1)S(1)} all-to-all(bf16[16,8,896]{2,1,0:T(8,128)(2,1)S(1)} %get-tuple-element.12), channel_id=1, replica_groups=mesh['dp'=16,'tensor'=8] {'dp'}, dimensions={0} | all-to-all | bytes 458752 | tf_op jit(solution)/shard_map/all_to_all | solution.py:184
  69.7 11.7 %all_to_all.29.q_pieces = bf16[16,8,896]{2,1,0:T(8,128)(2,1)S(1)} all-to-all(bf16[16,8,896]{2,1,0:T(8,128)(2,1)S(1)} %summed_copies.5), channel_id=1, replica_groups=mesh['dp'=16,'tensor'=8] {'dp'}, dimensions={0} | all-to-all | bytes 458752 | tf_op jit(solution)/shard_map/all_to_all | solution.py:184
  81.3 3.6 %subtract.1 = (bf16[1,1024,3584]{2,1,0:T(8,128)(2,1)}, f32[32,3584]{1,0:T(8,128)}) custom-call(bf16[16,8,896]{2,1,0:T(8,128)(2,1)S(1)} %all_to_all.29.q_pieces, bf16[32,1024]{1,0:T(8,128)(2,1)S(1)} %get-tuple-element.13.p_b, bf16[1024,3584]{1,0:T(8,128)(2,1)S(1)} %get-tuple-element.11.matrix), custom_call_target="tpu_custom_call" | custom-call | tf_op jit(solution)/shard_map/subtract/pallas_call | solution.py:144
  (3 shorter events, 0.1 us)
Async XLA Ops:
  0.6 3.1 %copy-start = (bf16[1,1024,3584]{2,1,0:T(8,128)(2,1)S(1)}, bf16[1,1024,3584]{2,1,0:T(8,128)(2,1)}, u32[]{:S(2)}) copy-start(bf16[1,1024,3584]{2,1,0:T(8,128)(2,1)} %grads.1) | copy-start | bytes 22020100
  3.7 3.1 %copy-start.1 = (bf16[1,1024,3584]{2,1,0:T(8,128)(2,1)S(1)}, bf16[1,1024,3584]{2,1,0:T(8,128)(2,1)}, u32[]{:S(2)}) copy-start(bf16[1,1024,3584]{2,1,0:T(8,128)(2,1)} %errors.1) | copy-start | bytes 22020100
  6.8 1.0 %copy-start.2 = (f32[3584,32]{0,1:T(8,128)S(1)}, f32[3584,32]{0,1:T(8,128)}, u32[]{:S(2)}) copy-start(f32[3584,32]{0,1:T(8,128)} %param.5) | copy-start | bytes 1376260

commit v2 on v1

--- a/solution.py
+++ b/solution.py
@@ -14,26 +14,32 @@
 IN_HBM = pl.BlockSpec(memory_space=pltpu.HBM)
 LANES = 128
 CHUNKS = 8
-
-
-def merge_kernel(grads, errors, basis_t, matrix, partial, held, basis, grad_sems, error_sems, basis_sem):
-    rows = matrix.shape[0]
-    step = rows // CHUNKS
-    pltpu.make_async_copy(basis_t, basis, basis_sem).start()
-    for i in range(CHUNKS):
-        part = pl.ds(i * step, step)
-        pltpu.make_async_copy(grads.at[0, part], matrix.at[part], grad_sems.at[i]).start()
-        pltpu.make_async_copy(errors.at[0, part], held.at[part], error_sems.at[i]).start()
-    pltpu.make_async_copy(basis_t, basis, basis_sem).wait()
-    basis_b = basis[...].astype(BF16)
-    for i in range(CHUNKS):
-        part = pl.ds(i * step, step)
-        pltpu.make_async_copy(grads.at[0, part], matrix.at[part], grad_sems.at[i]).wait()
-        pltpu.make_async_copy(errors.at[0, part], held.at[part], error_sems.at[i]).wait()
-        total = matrix[part, :] + held[part, :]
-        matrix[part, :] = total
-        product = lax.dot_general(total, basis_b, LAST_BY_LAST, preferred_element_type=F32)
-        partial[i] = product.T
+WIDTHS = (512, 512, 512, 512, 512, 512, 512)
+STARTS = tuple(sum(WIDTHS[:i]) for i in range(len(WIDTHS)))
+
+
+def merge_kernel(grads, errors, basis_t, matrix, partial, held, grad_sems, error_sems):
+    def copies(i):
+        part = (slice(None), pl.ds(STARTS[i], WIDTHS[i]))
+        return (
+            pltpu.make_async_copy(grads.at[(0, *part)], matrix.at[part], grad_sems.at[i]),
+            pltpu.make_async_copy(errors.at[(0, *part)], held.at[part], error_sems.at[i]),
+        )
+
+    for i in range(len(WIDTHS)):
+        for copy in copies(i):
+            copy.start()
+    basis_b = basis_t[...].astype(BF16)
+    for i in range(len(WIDTHS)):
+        for copy in copies(i):
+            copy.wait()
+        part = slice(STARTS[i], STARTS[i] + WIDTHS[i])
+        total = matrix[:, part] + held[:, part]
+        matrix[:, part] = total
+        product = lax.dot_general(basis_b[:, part], total, LAST_BY_LAST, preferred_element_type=F32)
+        for j in range(partial.shape[0]):
+            term = product[:, j * LANES : (j + 1) * LANES]
+            partial[j] = term if i == 0 else partial[j] + term
 
 
 def merge(grads, errors, basis_t):
@@ -45,16 +51,14 @@
             jax.ShapeDtypeStruct((rows, cols), BF16),
             jax.ShapeDtypeStruct((rows // LANES, rank, LANES), F32),
         ),
-        in_specs=[IN_HBM] * 3,
+        in_specs=[IN_HBM, IN_HBM, IN_VMEM],
         out_specs=(IN_VMEM, IN_VMEM),
         scratch_shapes=[
             pltpu.VMEM((rows, cols), BF16),
-            pltpu.VMEM((rank, cols), F32),
-            pltpu.SemaphoreType.DMA((CHUNKS,)),
-            pltpu.SemaphoreType.DMA((CHUNKS,)),
-            pltpu.SemaphoreType.DMA(()),
+            pltpu.SemaphoreType.DMA((len(WIDTHS),)),
+            pltpu.SemaphoreType.DMA((len(WIDTHS),)),
         ],
-        compiler_params=pltpu.CompilerParams(vmem_limit_bytes=24 << 20),
+        compiler_params=pltpu.CompilerParams(vmem_limit_bytes=44 << 20),
         name="merge",
     )(grads, errors, basis_t)
 

time: 85.4 us -> 75.9 us (0.89)
  local copies, waits for them, and re-layouts: 7.18 us -> 1.01 us
  Pallas kernels: 18.4 us -> 15.2 us
    unnamed x6 -> x2, local copies, waits for them, and re-layouts: 7.18 us -> 1.01 us
    pallas_call x1, Pallas kernels: 9.1 us -> 5.86 us  [merge(): pl.pallas_call(merge_kernel, out_shape=(jax.ShapeDtypeStruct((rows, cols)...]
where the time goes in v2:
time: 75.9 us; the launch traced here: 75.5 us
  blocking collectives  58.7 us (77%)
  Pallas kernels  15.2 us (20%)
  local copies, waits for them, and re-layouts  1.01 us (1%)
    all_to_all x5, blocking collectives, exchanged(): return lax.all_to_all(pieces, axis, split_axis=0, concat_axis=0, tiled=True)  58.7 us
    pallas_call x1, Pallas kernels, merge(): pl.pallas_call(merge_kernel, out_shape=(jax.ShapeDtypeStruct((rows, cols)...  5.86 us
    pallas_call x1, Pallas kernels, project(): pl.pallas_call(project_kernel, out_shape=(jax.ShapeDtypeStruct((rank, LAN...  5.62 us
    pallas_call x1, Pallas kernels, subtract(): pl.pallas_call(functools.partial(subtract_kernel, 1.0 / count), out_shape...  3.62 us

profile of v2, /device:TPU:0, one launch (start us, length us, event | category | flops | bytes accessed | tf_op | source)
XLA Modules:
  0.0 75.5 jit_solution(16592872494774015259)
XLA Ops:
  0.6 0.0 copy-start
  0.6 1.0 %copy-done = f32[3584,32]{0,1:T(8,128)S(1)} copy-done((f32[3584,32]{0,1:T(8,128)S(1)}, f32[3584,32]{0,1:T(8,128)}, u32[]{:S(2)}) %copy-start) | copy-done | bytes 458776
  1.6 5.9 %merge.1 = (bf16[1024,3584]{1,0:T(8,128)(2,1)S(1)}, f32[8,32,128]{2,1,0:T(8,128)S(1)}) custom-call(bf16[1,1024,3584]{2,1,0:T(8,128)(2,1)} %grads.1, bf16[1,1024,3584]{2,1,0:T(8,128)(2,1)} %errors.1, f32[32,3584]{1,0:T(8,128)S(1)} %bitcast.3), custom_call_target="tpu_custom_call" | custom-call | tf_op jit(solution)/shard_map/merge/pallas_call | solution.py:48
  7.5 10.3 %all_to_all.25.pieces = f32[8,32,128]{2,1,0:T(8,128)S(1)} all-to-all(f32[8,32,128]{2,1,0:T(8,128)S(1)} %get-tuple-element.10), channel_id=1, replica_groups=mesh['dp'=16,'tensor'=8] {'tensor'}, dimensions={0} | all-to-all | bytes 262144 | tf_op jit(solution)/shard_map/all_to_all | solution.py:188
  17.9 16.4 %all_to_all.26.pieces = f32[16,32,128]{2,1,0:T(8,128)S(1)} all-to-all(f32[16,32,128]{2,1,0:T(8,128)S(1)} %summed_copies.3), channel_id=1, replica_groups=mesh['dp'=16,'tensor'=8] {'dp'}, dimensions={0} | all-to-all | bytes 524288 | tf_op jit(solution)/shard_map/all_to_all | solution.py:188
  34.3 8.5 %all_to_all.27.pieces = f32[8,32,128]{2,1,0:T(8,128)S(1)} all-to-all(f32[8,32,128]{2,1,0:T(8,128)S(1)} %summed_copies.4.own), channel_id=1, replica_groups=mesh['dp'=16,'tensor'=8] {'tensor'}, dimensions={0} | all-to-all | bytes 262144 | tf_op jit(solution)/shard_map/all_to_all | solution.py:188
  42.8 5.6 %project.1 = (f32[32,128]{1,0:T(8,128)}, bf16[32,1024]{1,0:T(8,128)(2,1)S(1)}, bf16[16,8,896]{2,1,0:T(8,128)(2,1)S(1)}) custom-call(f32[8,32,128]{2,1,0:T(8,128)S(1)} %all_to_all.27.pieces, f32[8,32,128]{2,1,0:T(8,128)S(1)} %summed_copies.4.own, bf16[1024,3584]{1,0:T(8,128)(2,1)S(1)} %get-tuple-element.11.matrix), custom_call_target="tpu_custom_call" | custom-call | tf_op jit(solution)/shard_map/project/pallas_call | solution.py:104
  48.4 11.8 %all_to_all.28.pieces = bf16[16,8,896]{2,1,0:T(8,128)(2,1)S(1)} all-to-all(bf16[16,8,896]{2,1,0:T(8,128)(2,1)S(1)} %get-tuple-element.12), channel_id=1, replica_groups=mesh['dp'=16,'tensor'=8] {'dp'}, dimensions={0} | all-to-all | bytes 458752 | tf_op jit(solution)/shard_map/all_to_all | solution.py:188
  60.2 11.7 %all_to_all.29.q_pieces = bf16[16,8,896]{2,1,0:T(8,128)(2,1)S(1)} all-to-all(bf16[16,8,896]{2,1,0:T(8,128)(2,1)S(1)} %summed_copies.5), channel_id=1, replica_groups=mesh['dp'=16,'tensor'=8] {'dp'}, dimensions={0} | all-to-all | bytes 458752 | tf_op jit(solution)/shard_map/all_to_all | solution.py:188
  71.9 3.6 %subtract.1 = (bf16[1,1024,3584]{2,1,0:T(8,128)(2,1)}, f32[32,3584]{1,0:T(8,128)}) custom-call(bf16[16,8,896]{2,1,0:T(8,128)(2,1)S(1)} %all_to_all.29.q_pieces, bf16[32,1024]{1,0:T(8,128)(2,1)S(1)} %get-tuple-element.13.p_b, bf16[1024,3584]{1,0:T(8,128)(2,1)S(1)} %get-tuple-element.11.matrix), custom_call_target="tpu_custom_call" | custom-call | tf_op jit(solution)/shard_map/subtract/pallas_call | solution.py:148
  (3 shorter events, 0.1 us)
Async XLA Ops:
  0.6 1.0 %copy-start = (f32[3584,32]{0,1:T(8,128)S(1)}, f32[3584,32]{0,1:T(8,128)}, u32[]{:S(2)}) copy-start(f32[3584,32]{0,1:T(8,128)} %param.5) | copy-start | bytes 1376260

commit v3 on v2

--- a/solution.py
+++ b/solution.py
@@ -13,7 +13,8 @@
 IN_VMEM = pl.BlockSpec(memory_space=pltpu.VMEM)
 IN_HBM = pl.BlockSpec(memory_space=pltpu.HBM)
 LANES = 128
-CHUNKS = 8
+CHUNKS = 16
+BLOCK = 8
 WIDTHS = (512, 512, 512, 512, 512, 512, 512)
 STARTS = tuple(sum(WIDTHS[:i]) for i in range(len(WIDTHS)))
 
@@ -70,12 +71,22 @@
     work = jnp.concatenate([gram, jnp.zeros((rank, LANES - rank), F32)], axis=1)
     work = work + jnp.where(lane == row + rank, 1.0, 0.0)
     scale = jnp.zeros((rank, LANES), F32)
-    for k in range(rank):
-        column = jnp.broadcast_to(work[:, k : k + 1], (rank, LANES))
-        pivot_row = jnp.broadcast_to(work[k : k + 1, :], (rank, LANES))
-        pivot = jnp.broadcast_to(column[k : k + 1, :], (rank, LANES))
-        scale = jnp.where(row == k, pivot, scale)
-        work = work - jnp.where(row > k, column / pivot, 0.0) * pivot_row
+    for k in range(0, rank, BLOCK):
+        columns = [jnp.broadcast_to(work[:, k + p : k + p + 1], (rank, LANES)) for p in range(BLOCK)]
+        lines = [work[k + p : k + p + 1, :] for p in range(BLOCK)]
+        scaled = []
+        for p in range(BLOCK):
+            pivot = columns[p][k + p : k + p + 1, :]
+            inverse = 1.0 / pivot
+            for q in range(p + 1, BLOCK):
+                factor = columns[p][k + q : k + q + 1, :] * inverse
+                lines[q] = lines[q] - factor * lines[p]
+                columns[q] = columns[q] - factor * columns[p]
+            scale = jnp.where(row == k + p, pivot, scale)
+            work = jnp.where(row == k + p, lines[p], work)
+            scaled.append(lines[p] * inverse)
+        for p in range(BLOCK):
+            work = work - jnp.where(row >= k + BLOCK, columns[p], 0.0) * scaled[p]
     return (work * lax.rsqrt(scale))[:, rank : 2 * rank]
 
 

time: 75.9 us -> 72.4 us (0.954)
  Pallas kernels: 15.2 us -> 11.8 us
    pallas_call x1, Pallas kernels: 5.62 us -> 2.4 us  [project(): pl.pallas_call(project_kernel, out_shape=(jax.ShapeDtypeStruct((rank, LAN...]
where the time goes in v3:
time: 72.4 us; the launch traced here: 72.1 us
  blocking collectives  58.7 us (81%)
  Pallas kernels  11.8 us (16%)
  local copies, waits for them, and re-layouts  1.01 us (1%)
    all_to_all x5, blocking collectives, exchanged(): return lax.all_to_all(pieces, axis, split_axis=0, concat_axis=0, tiled=True)  58.7 us
    pallas_call x1, Pallas kernels, merge(): pl.pallas_call(merge_kernel, out_shape=(jax.ShapeDtypeStruct((rows, cols)...  5.86 us
    pallas_call x1, Pallas kernels, subtract(): pl.pallas_call(functools.partial(subtract_kernel, 1.0 / count), out_shape...  3.41 us
    pallas_call x1, Pallas kernels, project(): pl.pallas_call(project_kernel, out_shape=(jax.ShapeDtypeStruct((rank, LAN...  2.4 us

profile of v3, /device:TPU:0, one launch (start us, length us, event | category | flops | bytes accessed | tf_op | source)
XLA Modules:
  0.0 72.1 jit_solution(12136989913049448558)
XLA Ops:
  0.6 0.0 copy-start
  0.6 1.0 %copy-done = f32[3584,32]{0,1:T(8,128)S(1)} copy-done((f32[3584,32]{0,1:T(8,128)S(1)}, f32[3584,32]{0,1:T(8,128)}, u32[]{:S(2)}) %copy-start) | copy-done | bytes 458776
  1.6 5.9 %merge.1 = (bf16[1024,3584]{1,0:T(8,128)(2,1)S(1)}, f32[8,32,128]{2,1,0:T(8,128)S(1)}) custom-call(bf16[1,1024,3584]{2,1,0:T(8,128)(2,1)} %grads.1, bf16[1,1024,3584]{2,1,0:T(8,128)(2,1)} %errors.1, f32[32,3584]{1,0:T(8,128)S(1)} %bitcast.3), custom_call_target="tpu_custom_call" | custom-call | tf_op jit(solution)/shard_map/merge/pallas_call | solution.py:49
  7.5 10.3 %all_to_all.25.pieces = f32[8,32,128]{2,1,0:T(8,128)S(1)} all-to-all(f32[8,32,128]{2,1,0:T(8,128)S(1)} %get-tuple-element.10), channel_id=1, replica_groups=mesh['dp'=16,'tensor'=8] {'tensor'}, dimensions={0} | all-to-all | bytes 262144 | tf_op jit(solution)/shard_map/all_to_all | solution.py:199
  17.9 16.4 %all_to_all.26.pieces = f32[16,32,128]{2,1,0:T(8,128)S(1)} all-to-all(f32[16,32,128]{2,1,0:T(8,128)S(1)} %summed_copies.3), channel_id=1, replica_groups=mesh['dp'=16,'tensor'=8] {'dp'}, dimensions={0} | all-to-all | bytes 524288 | tf_op jit(solution)/shard_map/all_to_all | solution.py:199
  34.3 8.5 %all_to_all.27.pieces = f32[8,32,128]{2,1,0:T(8,128)S(1)} all-to-all(f32[8,32,128]{2,1,0:T(8,128)S(1)} %summed_copies.4.own), channel_id=1, replica_groups=mesh['dp'=16,'tensor'=8] {'tensor'}, dimensions={0} | all-to-all | bytes 262144 | tf_op jit(solution)/shard_map/all_to_all | solution.py:199
  42.8 2.4 %project.1 = (f32[32,128]{1,0:T(8,128)}, bf16[32,1024]{1,0:T(8,128)(2,1)S(1)}, bf16[16,8,896]{2,1,0:T(8,128)(2,1)S(1)}) custom-call(f32[8,32,128]{2,1,0:T(8,128)S(1)} %all_to_all.27.pieces, f32[8,32,128]{2,1,0:T(8,128)S(1)} %summed_copies.4.own, bf16[1024,3584]{1,0:T(8,128)(2,1)S(1)} %get-tuple-element.11.matrix), custom_call_target="tpu_custom_call" | custom-call | tf_op jit(solution)/shard_map/project/pallas_call | solution.py:115
  45.2 11.8 %all_to_all.28.pieces = bf16[16,8,896]{2,1,0:T(8,128)(2,1)S(1)} all-to-all(bf16[16,8,896]{2,1,0:T(8,128)(2,1)S(1)} %get-tuple-element.12), channel_id=1, replica_groups=mesh['dp'=16,'tensor'=8] {'dp'}, dimensions={0} | all-to-all | bytes 458752 | tf_op jit(solution)/shard_map/all_to_all | solution.py:199
  57.0 11.7 %all_to_all.29.q_pieces = bf16[16,8,896]{2,1,0:T(8,128)(2,1)S(1)} all-to-all(bf16[16,8,896]{2,1,0:T(8,128)(2,1)S(1)} %summed_copies.5), channel_id=1, replica_groups=mesh['dp'=16,'tensor'=8] {'dp'}, dimensions={0} | all-to-all | bytes 458752 | tf_op jit(solution)/shard_map/all_to_all | solution.py:199
  68.7 3.4 %subtract.1 = (bf16[1,1024,3584]{2,1,0:T(8,128)(2,1)}, f32[32,3584]{1,0:T(8,128)}) custom-call(bf16[16,8,896]{2,1,0:T(8,128)(2,1)S(1)} %all_to_all.29.q_pieces, bf16[32,1024]{1,0:T(8,128)(2,1)S(1)} %get-tuple-element.13.p_b, bf16[1024,3584]{1,0:T(8,128)(2,1)S(1)} %get-tuple-element.11.matrix), custom_call_target="tpu_custom_call" | custom-call | tf_op jit(solution)/shard_map/subtract/pallas_call | solution.py:159
  (3 shorter events, 0.1 us)
Async XLA Ops:
  0.6 1.0 %copy-start = (f32[3584,32]{0,1:T(8,128)S(1)}, f32[3584,32]{0,1:T(8,128)}, u32[]{:S(2)}) copy-start(f32[3584,32]{0,1:T(8,128)} %param.5) | copy-start | bytes 1376260

commit v4 on v3

--- a/solution.py
+++ b/solution.py
@@ -38,9 +38,11 @@
         total = matrix[:, part] + held[:, part]
         matrix[:, part] = total
         product = lax.dot_general(basis_b[:, part], total, LAST_BY_LAST, preferred_element_type=F32)
-        for j in range(partial.shape[0]):
+        rank = product.shape[0]
+        for j in range(product.shape[1] // LANES):
+            block = pl.ds(j * rank, rank)
             term = product[:, j * LANES : (j + 1) * LANES]
-            partial[j] = term if i == 0 else partial[j] + term
+            partial[block, :] = term if i == 0 else partial[block, :] + term
 
 
 def merge(grads, errors, basis_t):
@@ -50,7 +52,7 @@
         merge_kernel,
         out_shape=(
             jax.ShapeDtypeStruct((rows, cols), BF16),
-            jax.ShapeDtypeStruct((rows // LANES, rank, LANES), F32),
+            jax.ShapeDtypeStruct((rows // LANES * rank, LANES), F32),
         ),
         in_specs=[IN_HBM, IN_HBM, IN_VMEM],
         out_specs=(IN_VMEM, IN_VMEM),
@@ -90,14 +92,15 @@
     return (work * lax.rsqrt(scale))[:, rank : 2 * rank]
 
 
-def project_kernel(pieces, own, matrix, p_own, p_b, q_pieces, whole):
-    blocks, rank, _ = pieces.shape
-    for i in range(blocks):
-        whole[:, i * LANES : (i + 1) * LANES] = pieces[i]
+def project_kernel(lines, matrix, p_own, p_b, q_pieces, whole):
+    rank = whole.shape[0]
+    for i in range(lines.shape[0] // rank):
+        whole[:, i * LANES : (i + 1) * LANES] = lines[i * rank : (i + 1) * rank]
     p_sum = whole[...]
     gram = lax.dot_general(p_sum, p_sum, LAST_BY_LAST, precision=HIGHEST, preferred_element_type=F32)
     inverse = inverse_factor(gram)
-    p_own[...] = jnp.dot(inverse, own[0], precision=HIGHEST, preferred_element_type=F32)
+    own = lines[pl.ds(pl.multiple_of(lax.axis_index("tensor") * rank, rank), rank), :]
+    p_own[...] = jnp.dot(inverse, own, precision=HIGHEST, preferred_element_type=F32)
     rounded = jnp.dot(inverse, p_sum, precision=HIGHEST, preferred_element_type=F32).astype(BF16)
     p_b[...] = rounded
     count, height, width = q_pieces.shape
@@ -107,9 +110,9 @@
             q_pieces[j * (rank // height) + s] = q[s * height : (s + 1) * height]
 
 
-def project(pieces, own, matrix, count):
-    blocks, rank, _ = pieces.shape
+def project(lines, matrix, count):
     rows, cols = matrix.shape
+    rank = lines.size // rows
     height = 8
     width = cols * rank // (count * height)
     return pl.pallas_call(
@@ -119,12 +122,12 @@
             jax.ShapeDtypeStruct((rank, rows), BF16),
             jax.ShapeDtypeStruct((count, height, width), BF16),
         ),
-        in_specs=[IN_VMEM] * 3,
+        in_specs=[IN_VMEM] * 2,
         out_specs=(IN_VMEM,) * 3,
         scratch_shapes=[pltpu.VMEM((rank, rows), F32)],
         compiler_params=pltpu.CompilerParams(vmem_limit_bytes=24 << 20),
         name="project",
-    )(pieces, own, matrix)
+    )(lines, matrix)
 
 
 def subtract_kernel(mean, q_pieces, p_b, matrix, new_errors, q_out, out_buf, q_buf, sems, q_sem):
@@ -195,16 +198,43 @@
     )(pieces)
 
 
+def line_kernel(lines, copies):
+    count, lanes = lines.shape
+    total = lines[0:8, :]
+    for i in range(8, count, 8):
+        total = total + lines[i : i + 8, :]
+    total = total[0:4] + total[4:8]
+    total = total[0:2] + total[2:4]
+    total = jnp.concatenate([total] * 4, axis=0)
+    for i in range(0, count, 8):
+        copies[i : i + 8, :] = total
+
+
+def summed_lines(lines):
+    return pl.pallas_call(
+        line_kernel,
+        out_shape=jax.ShapeDtypeStruct(lines.shape, F32),
+        in_specs=[IN_VMEM],
+        out_specs=IN_VMEM,
+        compiler_params=pltpu.CompilerParams(vmem_limit_bytes=4 << 20),
+        name="summed_lines",
+    )(lines)
+
+
 def exchanged(pieces, axis):
     return lax.all_to_all(pieces, axis, split_axis=0, concat_axis=0, tiled=True)
 
 
+def exchanged_lines(lines):
+    axes = ("dp", "tensor")
+    return exchanged(lines.reshape(lax.axis_size(axes), -1, LANES), axes).reshape(lines.shape)
+
+
 def on_device(grads, errors, basis):
-    n_dp, n_tensor = lax.axis_size("dp"), lax.axis_size("tensor")
+    n_dp = lax.axis_size("dp")
     matrix, partial = merge(grads, errors, basis.T)
-    p_terms = exchanged(summed_copies(exchanged(partial, "tensor"), n_dp), "dp")
-    p_copies = summed_copies(p_terms, n_tensor)
-    p_own, p_b, q_pieces = project(exchanged(p_copies, "tensor"), p_copies, matrix, n_dp)
+    lines = exchanged_lines(summed_lines(exchanged_lines(partial)))
+    p_own, p_b, q_pieces = project(lines, matrix, n_dp)
     q_sums = exchanged(summed_copies(exchanged(q_pieces, "dp"), n_dp), "dp")
     new_errors, q_out = subtract(q_sums, p_b, matrix)
     return new_errors, p_own.T, q_out.T

time: 72.4 us -> 71.8 us (level)
    all_to_all x5 -> x4, blocking collectives: 58.7 us -> 58.1 us  [exchanged(): return lax.all_to_all(pieces, axis, split_axis=0, concat_axis=0, tiled=True)]
where the time goes in v4:
time: 71.8 us; the launch traced here: 71.5 us
  blocking collectives  58.1 us (81%)
  Pallas kernels  11.8 us (16%)
  local copies, waits for them, and re-layouts  1.01 us (1%)
    all_to_all x4, blocking collectives, exchanged(): return lax.all_to_all(pieces, axis, split_axis=0, concat_axis=0, tiled=True)  58.1 us
    pallas_call x1, Pallas kernels, merge(): pl.pallas_call(merge_kernel, out_shape=(jax.ShapeDtypeStruct((rows, cols)...  5.86 us
    pallas_call x1, Pallas kernels, subtract(): pl.pallas_call(functools.partial(subtract_kernel, 1.0 / count), out_shape...  3.41 us
    pallas_call x1, Pallas kernels, project(): pl.pallas_call(project_kernel, out_shape=(jax.ShapeDtypeStruct((rank, LAN...  2.4 us

profile of v4, /device:TPU:0, one launch (start us, length us, event | category | flops | bytes accessed | tf_op | source)
XLA Modules:
  0.0 71.5 jit_solution(8399898473232098832)
XLA Ops:
  0.6 0.0 copy-start
  0.6 1.0 %copy-done = f32[3584,32]{0,1:T(8,128)S(1)} copy-done((f32[3584,32]{0,1:T(8,128)S(1)}, f32[3584,32]{0,1:T(8,128)}, u32[]{:S(2)}) %copy-start) | copy-done | bytes 458776
  1.6 5.9 %merge.1 = (bf16[1024,3584]{1,0:T(8,128)(2,1)S(1)}, f32[256,128]{1,0:T(8,128)S(1)}) custom-call(bf16[1,1024,3584]{2,1,0:T(8,128)(2,1)} %grads.1, bf16[1,1024,3584]{2,1,0:T(8,128)(2,1)} %errors.1, f32[32,3584]{1,0:T(8,128)S(1)} %bitcast.10), custom_call_target="tpu_custom_call" | custom-call | tf_op jit(solution)/shard_map/merge/pallas_call | solution.py:51
  7.5 20.6 %all_to_all.20 = f32[128,2,128]{2,1,0:T(2,128)S(1)} all-to-all(f32[128,2,128]{2,1,0:T(2,128)S(1)} %bitcast.11), channel_id=1, replica_groups=mesh['dp'=16,'tensor'=8] {'dp','tensor'}, dimensions={0} | all-to-all | bytes 262144 | tf_op jit(solution)/shard_map/all_to_all | solution.py:225
  28.2 14.3 %all_to_all.21 = f32[128,2,128]{2,1,0:T(2,128)S(1)} all-to-all(f32[128,2,128]{2,1,0:T(2,128)S(1)} %bitcast.9), channel_id=1, replica_groups=mesh['dp'=16,'tensor'=8] {'dp','tensor'}, dimensions={0} | all-to-all | bytes 262144 | tf_op jit(solution)/shard_map/all_to_all | solution.py:225
  42.5 2.4 %project.1 = (f32[32,128]{1,0:T(8,128)}, bf16[32,1024]{1,0:T(8,128)(2,1)S(1)}, bf16[16,8,896]{2,1,0:T(8,128)(2,1)S(1)}) custom-call(f32[256,128]{1,0:T(8,128)S(1)} %bitcast.7, bf16[1024,3584]{1,0:T(8,128)(2,1)S(1)} %get-tuple-element.11.matrix), custom_call_target="tpu_custom_call" | custom-call | tf_op jit(solution)/shard_map/project/pallas_call | solution.py:118
  44.9 11.6 %all_to_all.22.pieces = bf16[16,8,896]{2,1,0:T(8,128)(2,1)S(1)} all-to-all(bf16[16,8,896]{2,1,0:T(8,128)(2,1)S(1)} %get-tuple-element.12), channel_id=1, replica_groups=mesh['dp'=16,'tensor'=8] {'dp'}, dimensions={0} | all-to-all | bytes 458752 | tf_op jit(solution)/shard_map/all_to_all | solution.py:225
  56.5 11.7 %all_to_all.23.q_pieces = bf16[16,8,896]{2,1,0:T(8,128)(2,1)S(1)} all-to-all(bf16[16,8,896]{2,1,0:T(8,128)(2,1)S(1)} %summed_copies.1), channel_id=1, replica_groups=mesh['dp'=16,'tensor'=8] {'dp'}, dimensions={0} | all-to-all | bytes 458752 | tf_op jit(solution)/shard_map/all_to_all | solution.py:225
  68.1 3.4 %subtract.1 = (bf16[1,1024,3584]{2,1,0:T(8,128)(2,1)}, f32[32,3584]{1,0:T(8,128)}) custom-call(bf16[16,8,896]{2,1,0:T(8,128)(2,1)S(1)} %all_to_all.23.q_pieces, bf16[32,1024]{1,0:T(8,128)(2,1)S(1)} %get-tuple-element.13.p_b, bf16[1024,3584]{1,0:T(8,128)(2,1)S(1)} %get-tuple-element.11.matrix), custom_call_target="tpu_custom_call" | custom-call | tf_op jit(solution)/shard_map/subtract/pallas_call | solution.py:162
  (2 shorter events, 0.1 us)
Async XLA Ops:
  0.6 1.0 %copy-start = (f32[3584,32]{0,1:T(8,128)S(1)}, f32[3584,32]{0,1:T(8,128)}, u32[]{:S(2)}) copy-start(f32[3584,32]{0,1:T(8,128)} %param.5) | copy-start | bytes 1376260

commit v5 on v3

--- a/solution.py
+++ b/solution.py
@@ -14,12 +14,16 @@
 IN_HBM = pl.BlockSpec(memory_space=pltpu.HBM)
 LANES = 128
 CHUNKS = 16
-BLOCK = 8
-WIDTHS = (512, 512, 512, 512, 512, 512, 512)
+BLOCK = 16
+WIDTHS = (768, 768, 768, 512, 512, 256)
 STARTS = tuple(sum(WIDTHS[:i]) for i in range(len(WIDTHS)))
 
 
-def merge_kernel(grads, errors, basis_t, matrix, partial, held, grad_sems, error_sems):
+def on_first_core():
+    return lax.rem(lax.axis_index("tensor"), 2) == 0
+
+
+def merge_kernel(grads, errors, basis_t, matrix, kept, sent, held, partial, grad_sems, error_sems):
     def copies(i):
         part = (slice(None), pl.ds(STARTS[i], WIDTHS[i]))
         return (
@@ -31,6 +35,8 @@
         for copy in copies(i):
             copy.start()
     basis_b = basis_t[...].astype(BF16)
+    half = kept.shape[1]
+    first = on_first_core()
     for i in range(len(WIDTHS)):
         for copy in copies(i):
             copy.wait()
@@ -38,9 +44,12 @@
         total = matrix[:, part] + held[:, part]
         matrix[:, part] = total
         product = lax.dot_general(basis_b[:, part], total, LAST_BY_LAST, preferred_element_type=F32)
-        for j in range(partial.shape[0]):
-            term = product[:, j * LANES : (j + 1) * LANES]
-            partial[j] = term if i == 0 else partial[j] + term
+        if i:
+            product = partial[...] + product
+        if i < len(WIDTHS) - 1:
+            partial[...] = product
+    kept[...] = jnp.where(first, product[:, :half], product[:, half:])
+    sent[...] = jnp.where(first, product[:, half:], product[:, :half])
 
 
 def merge(grads, errors, basis_t):
@@ -50,12 +59,14 @@
         merge_kernel,
         out_shape=(
             jax.ShapeDtypeStruct((rows, cols), BF16),
-            jax.ShapeDtypeStruct((rows // LANES, rank, LANES), F32),
+            jax.ShapeDtypeStruct((rank, rows // 2), F32),
+            jax.ShapeDtypeStruct((rank, rows // 2), F32),
         ),
         in_specs=[IN_HBM, IN_HBM, IN_VMEM],
-        out_specs=(IN_VMEM, IN_VMEM),
+        out_specs=(IN_VMEM,) * 3,
         scratch_shapes=[
             pltpu.VMEM((rows, cols), BF16),
+            pltpu.VMEM((rank, rows), F32),
             pltpu.SemaphoreType.DMA((len(WIDTHS),)),
             pltpu.SemaphoreType.DMA((len(WIDTHS),)),
         ],
@@ -90,14 +101,16 @@
     return (work * lax.rsqrt(scale))[:, rank : 2 * rank]
 
 
-def project_kernel(pieces, own, matrix, p_own, p_b, q_pieces, whole):
-    blocks, rank, _ = pieces.shape
-    for i in range(blocks):
-        whole[:, i * LANES : (i + 1) * LANES] = pieces[i]
+def project_kernel(mine, other, matrix, p_own, p_b, q_pieces, whole):
+    rank, half = mine.shape
+    first = on_first_core()
+    whole[:, :half] = jnp.where(first, mine[...], other[...])
+    whole[:, half:] = jnp.where(first, other[...], mine[...])
     p_sum = whole[...]
     gram = lax.dot_general(p_sum, p_sum, LAST_BY_LAST, precision=HIGHEST, preferred_element_type=F32)
     inverse = inverse_factor(gram)
-    p_own[...] = jnp.dot(inverse, own[0], precision=HIGHEST, preferred_element_type=F32)
+    own = whole[:, pl.ds(pl.multiple_of(lax.axis_index("tensor") * LANES, LANES), LANES)]
+    p_own[...] = jnp.dot(inverse, own, precision=HIGHEST, preferred_element_type=F32)
     rounded = jnp.dot(inverse, p_sum, precision=HIGHEST, preferred_element_type=F32).astype(BF16)
     p_b[...] = rounded
     count, height, width = q_pieces.shape
@@ -107,8 +120,8 @@
             q_pieces[j * (rank // height) + s] = q[s * height : (s + 1) * height]
 
 
-def project(pieces, own, matrix, count):
-    blocks, rank, _ = pieces.shape
+def project(mine, other, matrix, count):
+    rank = mine.shape[0]
     rows, cols = matrix.shape
     height = 8
     width = cols * rank // (count * height)
@@ -124,7 +137,7 @@
         scratch_shapes=[pltpu.VMEM((rank, rows), F32)],
         compiler_params=pltpu.CompilerParams(vmem_limit_bytes=24 << 20),
         name="project",
-    )(pieces, own, matrix)
+    )(mine, other, matrix)
 
 
 def subtract_kernel(mean, q_pieces, p_b, matrix, new_errors, q_out, out_buf, q_buf, sems, q_sem):
@@ -195,16 +208,45 @@
     )(pieces)
 
 
+def added_kernel(*refs):
+    terms = [ref[...] for ref in refs[:-1]]
+    while len(terms) > 1:
+        terms = [terms[i] + terms[i + 1] for i in range(0, len(terms), 2)]
+    refs[-1][...] = terms[0]
+
+
+def added(*terms):
+    return pl.pallas_call(
+        added_kernel,
+        out_shape=jax.ShapeDtypeStruct(terms[0].shape, terms[0].dtype),
+        in_specs=[IN_VMEM] * len(terms),
+        out_specs=IN_VMEM,
+        compiler_params=pltpu.CompilerParams(vmem_limit_bytes=4 << 20),
+        name="added",
+    )(*terms)
+
+
+def swapped(value, axis, stride, distance):
+    return lax.ppermute(value, axis, [(i, i ^ (distance * stride)) for i in range(lax.axis_size(axis))])
+
+
+def summed_over_four(value, axis, stride):
+    one, three, two = (swapped(value, axis, stride, distance) for distance in (1, 3, 2))
+    return added(value, one, two, three)
+
+
 def exchanged(pieces, axis):
     return lax.all_to_all(pieces, axis, split_axis=0, concat_axis=0, tiled=True)
 
 
 def on_device(grads, errors, basis):
-    n_dp, n_tensor = lax.axis_size("dp"), lax.axis_size("tensor")
-    matrix, partial = merge(grads, errors, basis.T)
-    p_terms = exchanged(summed_copies(exchanged(partial, "tensor"), n_dp), "dp")
-    p_copies = summed_copies(p_terms, n_tensor)
-    p_own, p_b, q_pieces = project(exchanged(p_copies, "tensor"), p_copies, matrix, n_dp)
+    matrix, kept, sent = merge(grads, errors, basis.T)
+    mine = added(kept, swapped(sent, "tensor", 1, 1))
+    mine = summed_over_four(mine, "tensor", 2)
+    mine = summed_over_four(mine, "dp", 4)
+    mine = summed_over_four(mine, "dp", 1)
+    n_dp = lax.axis_size("dp")
+    p_own, p_b, q_pieces = project(mine, swapped(mine, "tensor", 1, 1), matrix, n_dp)
     q_sums = exchanged(summed_copies(exchanged(q_pieces, "dp"), n_dp), "dp")
     new_errors, q_out = subtract(q_sums, p_b, matrix)
     return new_errors, p_own.T, q_out.T

time: 72.4 us -> 68.7 us (0.949)
  blocking collectives: 58.7 us -> 24.8 us
  waiting for transfers between devices: 0 us -> 16.8 us
  starting transfers between devices: 0 us -> 13.6 us
    all_to_all x5 -> x2, blocking collectives: 58.7 us -> 24.8 us  [exchanged(): return lax.all_to_all(pieces, axis, split_axis=0, concat_axis=0, tiled=True)]
    ppermute x0 -> x11, waiting for transfers between devices: none -> 16.8 us  [swapped(): lax.ppermute(value, axis, [(i, i ^ distance * stride) for i in range(lax....]
    ppermute x0 -> x11, starting transfers between devices: none -> 13.6 us  [swapped(): lax.ppermute(value, axis, [(i, i ^ distance * stride) for i in range(lax....]
  transfers between devices with their start and end apart: 0 -> 11, of which waited for: 0 -> 8; matrix products, arithmetic and copies ran while one was open for 0% -> 0% of each run, Pallas kernels for 0% -> 0%
where the time goes in v5:
time: 68.7 us; the launch traced here: 68.5 us
  blocking collectives  24.8 us (36%)
  waiting for transfers between devices  16.8 us (24%)
  starting transfers between devices  13.6 us (20%)
  Pallas kernels  11.5 us (17%)
  local copies, waits for them, and re-layouts  1.01 us (1%)
  between operations  0.7 us (1%)
    all_to_all x2, blocking collectives, exchanged(): return lax.all_to_all(pieces, axis, split_axis=0, concat_axis=0, tiled=True)  24.8 us
    ppermute x11, waiting for transfers between devices, swapped(): lax.ppermute(value, axis, [(i, i ^ distance * stride) for i in range(lax....  16.8 us
    ppermute x11, starting transfers between devices, swapped(): lax.ppermute(value, axis, [(i, i ^ distance * stride) for i in range(lax....  13.6 us
    pallas_call x1, Pallas kernels, merge(): pl.pallas_call(merge_kernel, out_shape=(jax.ShapeDtypeStruct((rows, cols)...  5.68 us
    pallas_call x1, Pallas kernels, subtract(): pl.pallas_call(functools.partial(subtract_kernel, 1.0 / count), out_shape...  3.41 us
    pallas_call x1, Pallas kernels, project(): pl.pallas_call(project_kernel, out_shape=(jax.ShapeDtypeStruct((rank, LAN...  2.32 us
  transfers between devices with their start and end apart: 11, of which 8 were waited for; matrix products, arithmetic and copies ran while one was open for 0% of the time, Pallas kernels for 0%

profile of v5, /device:TPU:0, one launch (start us, length us, event | category | flops | bytes accessed | tf_op | source)
XLA Modules:
  0.0 68.5 jit_solution(9044570278069001901)
XLA Ops:
  0.6 1.0 %copy-done = f32[3584,32]{0,1:T(8,128)S(1)} copy-done((f32[3584,32]{0,1:T(8,128)S(1)}, f32[3584,32]{0,1:T(8,128)}, u32[]{:S(2)}) %copy-start) | copy-done | bytes 458776
  1.6 5.7 %merge.1 = (bf16[1024,3584]{1,0:T(8,128)(2,1)S(1)}, f32[32,512]{1,0:T(8,128)S(1)}, f32[32,512]{1,0:T(8,128)S(1)}) custom-call(bf16[1,1024,3584]{2,1,0:T(8,128)(2,1)} %grads.1, bf16[1,1024,3584]{2,1,0:T(8,128)(2,1)} %errors.1, f32[32,3584]{1,0:T(8,128)S(1)} %bitcast.3), custom_call_target="tpu_custom_call" | custom-call | tf_op jit(solution)/shard_map/merge/pallas_call | solution.py:58
  7.3 0.1 collective-permute-start
  7.4 1.2 %collective-permute-done.refs_1_ = f32[32,512]{1,0:T(8,128)S(1)} collective-permute-done((f32[32,512]{1,0:T(8,128)S(1)}, f32[32,512]{1,0:T(8,128)S(1)}, u32[]{:S(2)}, u32[]{:S(2)}) %collective-permute-start) | collective-permute-done | bytes 65568 | tf_op jit(solution)/shard_map/ppermute | solution.py:230
  8.7 2.9 %collective-permute-start.3 = (f32[32,512]{1,0:T(8,128)S(1)}, f32[32,512]{1,0:T(8,128)S(1)}, u32[]{:S(2)}, u32[]{:S(2)}) collective-permute-start(f32[32,512]{1,0:T(8,128)S(1)} %added.4.refs_0_), channel_id=1, source_target_pairs={{0,6},{1,7},{2,4},{3,5},{4,2},{5,3},{6,0},{7,1},{8,14},{9,15},{10,... | collective-permute-start | bytes 196616 | tf_op jit(solution)/shard_map/ppermute | solution.py:230
  11.6 0.8 %collective-permute-start.2 = (f32[32,512]{1,0:T(8,128)S(1)}, f32[32,512]{1,0:T(8,128)S(1)}, u32[]{:S(2)}, u32[]{:S(2)}) collective-permute-start(f32[32,512]{1,0:T(8,128)S(1)} %added.4.refs_0_), channel_id=1, source_target_pairs={{0,4},{1,5},{2,6},{3,7},{4,0},{5,1},{6,2},{7,3},{8,12},{9,13},{10,... | collective-permute-start | bytes 196616 | tf_op jit(solution)/shard_map/ppermute | solution.py:230
  12.4 0.5 collective-permute-start.1
  12.9 1.8 %collective-permute-done.3.refs_3_ = f32[32,512]{1,0:T(8,128)S(1)} collective-permute-done((f32[32,512]{1,0:T(8,128)S(1)}, f32[32,512]{1,0:T(8,128)S(1)}, u32[]{:S(2)}, u32[]{:S(2)}) %collective-permute-start.3) | collective-permute-done | bytes 65568 | tf_op jit(solution)/shard_map/ppermute | solution.py:230
  14.6 3.0 %collective-permute-done.2.refs_2_ = f32[32,512]{1,0:T(8,128)S(1)} collective-permute-done((f32[32,512]{1,0:T(8,128)S(1)}, f32[32,512]{1,0:T(8,128)S(1)}, u32[]{:S(2)}, u32[]{:S(2)}) %collective-permute-start.2) | collective-permute-done | bytes 65568 | tf_op jit(solution)/shard_map/ppermute | solution.py:230
  17.7 3.1 %collective-permute-start.6 = (f32[32,512]{1,0:T(8,128)S(1)}, f32[32,512]{1,0:T(8,128)S(1)}, u32[]{:S(2)}, u32[]{:S(2)}) collective-permute-start(f32[32,512]{1,0:T(8,128)S(1)} %added.5.refs_0_), channel_id=1, source_target_pairs={{0,96},{8,104},{16,112},{24,120},{32,64},{40,72},{48,80},{56,88},{... | collective-permute-start | bytes 196616 | tf_op jit(solution)/shard_map/ppermute | solution.py:230
  20.8 0.6 collective-permute-start.5
  21.4 0.5 collective-permute-start.4
  21.9 2.1 %collective-permute-done.6.refs_3_ = f32[32,512]{1,0:T(8,128)S(1)} collective-permute-done((f32[32,512]{1,0:T(8,128)S(1)}, f32[32,512]{1,0:T(8,128)S(1)}, u32[]{:S(2)}, u32[]{:S(2)}) %collective-permute-start.6) | collective-permute-done | bytes 65568 | tf_op jit(solution)/shard_map/ppermute | solution.py:230
  24.0 2.6 %collective-permute-done.5.refs_2_ = f32[32,512]{1,0:T(8,128)S(1)} collective-permute-done((f32[32,512]{1,0:T(8,128)S(1)}, f32[32,512]{1,0:T(8,128)S(1)}, u32[]{:S(2)}, u32[]{:S(2)}) %collective-permute-start.5) | collective-permute-done | bytes 65568 | tf_op jit(solution)/shard_map/ppermute | solution.py:230
  26.6 4.1 %collective-permute-start.9 = (f32[32,512]{1,0:T(8,128)S(1)}, f32[32,512]{1,0:T(8,128)S(1)}, u32[]{:S(2)}, u32[]{:S(2)}) collective-permute-start(f32[32,512]{1,0:T(8,128)S(1)} %added.6.refs_0_), channel_id=1, source_target_pairs={{0,24},{8,16},{16,8},{24,0},{32,56},{40,48},{48,40},{56,32},{64,88... | collective-permute-start | bytes 196616 | tf_op jit(solution)/shard_map/ppermute | solution.py:230
  30.7 0.9 %collective-permute-start.7 = (f32[32,512]{1,0:T(8,128)S(1)}, f32[32,512]{1,0:T(8,128)S(1)}, u32[]{:S(2)}, u32[]{:S(2)}) collective-permute-start(f32[32,512]{1,0:T(8,128)S(1)} %added.6.refs_0_), channel_id=1, source_target_pairs={{0,8},{8,0},{16,24},{24,16},{32,40},{40,32},{48,56},{56,48},{64,72... | collective-permute-start | bytes 196616 | tf_op jit(solution)/shard_map/ppermute | solution.py:230
  31.7 1.6 %collective-permute-done.9.refs_3_ = f32[32,512]{1,0:T(8,128)S(1)} collective-permute-done((f32[32,512]{1,0:T(8,128)S(1)}, f32[32,512]{1,0:T(8,128)S(1)}, u32[]{:S(2)}, u32[]{:S(2)}) %collective-permute-start.9) | collective-permute-done | bytes 65568 | tf_op jit(solution)/shard_map/ppermute | solution.py:230
  33.2 3.3 %collective-permute-done.8.refs_2_ = f32[32,512]{1,0:T(8,128)S(1)} collective-permute-done((f32[32,512]{1,0:T(8,128)S(1)}, f32[32,512]{1,0:T(8,128)S(1)}, u32[]{:S(2)}, u32[]{:S(2)}) %collective-permute-start.8) | collective-permute-done | bytes 65568 | tf_op jit(solution)/shard_map/ppermute | solution.py:230
  36.5 0.1 collective-permute-start.10
  36.6 1.2 %collective-permute-done.10.other = f32[32,512]{1,0:T(8,128)S(1)} collective-permute-done((f32[32,512]{1,0:T(8,128)S(1)}, f32[32,512]{1,0:T(8,128)S(1)}, u32[]{:S(2)}, u32[]{:S(2)}) %collective-permute-start.10) | collective-permute-done | bytes 65568 | tf_op jit(solution)/shard_map/ppermute | solution.py:230
  37.8 2.3 %project.1 = (f32[32,128]{1,0:T(8,128)}, bf16[32,1024]{1,0:T(8,128)(2,1)S(1)}, bf16[16,8,896]{2,1,0:T(8,128)(2,1)S(1)}) custom-call(f32[32,512]{1,0:T(8,128)S(1)} %added.7.mine, f32[32,512]{1,0:T(8,128)S(1)} %collective-permute-done.10.other, bf16[1024,3584]{1,0:T(8,128)(2,1)S(1)} %get-tuple-element.13.matrix), custom_call_target="tpu_custom_call" | custom-call | tf_op jit(solution)/shard_map/project/pallas_call | solution.py:128
  40.2 13.2 %all_to_all.10.pieces = bf16[16,8,896]{2,1,0:T(8,128)(2,1)S(1)} all-to-all(bf16[16,8,896]{2,1,0:T(8,128)(2,1)S(1)} %get-tuple-element.14), channel_id=1, replica_groups=mesh['dp'=16,'tensor'=8] {'dp'}, dimensions={0} | all-to-all | bytes 458752 | tf_op jit(solution)/shard_map/all_to_all | solution.py:239
  53.4 11.7 %all_to_all.11.q_pieces = bf16[16,8,896]{2,1,0:T(8,128)(2,1)S(1)} all-to-all(bf16[16,8,896]{2,1,0:T(8,128)(2,1)S(1)} %summed_copies.1), channel_id=1, replica_groups=mesh['dp'=16,'tensor'=8] {'dp'}, dimensions={0} | all-to-all | bytes 458752 | tf_op jit(solution)/shard_map/all_to_all | solution.py:239
  65.1 3.4 %subtract.1 = (bf16[1,1024,3584]{2,1,0:T(8,128)(2,1)}, f32[32,3584]{1,0:T(8,128)}) custom-call(bf16[16,8,896]{2,1,0:T(8,128)(2,1)S(1)} %all_to_all.11.q_pieces, bf16[32,1024]{1,0:T(8,128)(2,1)S(1)} %get-tuple-element.15.p_b, bf16[1024,3584]{1,0:T(8,128)(2,1)S(1)} %get-tuple-element.13.matrix), custom_call_target="tpu_custom_call" | custom-call | tf_op jit(solution)/shard_map/subtract/pallas_call | solution.py:172
  (10 shorter events, 0.1 us)
Async XLA Ops:
  0.6 1.0 %copy-start = (f32[3584,32]{0,1:T(8,128)S(1)}, f32[3584,32]{0,1:T(8,128)}, u32[]{:S(2)}) copy-start(f32[3584,32]{0,1:T(8,128)} %param.5) | copy-start | bytes 1376260
  7.3 1.3 %collective-permute-start = (f32[32,512]{1,0:T(8,128)S(1)}, f32[32,512]{1,0:T(8,128)S(1)}, u32[]{:S(2)}, u32[]{:S(2)}) collective-permute-start(f32[32,512]{1,0:T(8,128)S(1)} %get-tuple-element.12), channel_id=1, source_target_pairs={{0,1},{1,0},{2,3},{3,2},{4,5},{5,4},{6,7},{7,6},{8,9},{9,8},{10,11... | collective-permute-start | bytes 196616 | tf_op jit(solution)/shard_map/ppermute | solution.py:230
  8.7 6.0 %collective-permute-start.3 = (f32[32,512]{1,0:T(8,128)S(1)}, f32[32,512]{1,0:T(8,128)S(1)}, u32[]{:S(2)}, u32[]{:S(2)}) collective-permute-start(f32[32,512]{1,0:T(8,128)S(1)} %added.4.refs_0_), channel_id=1, source_target_pairs={{0,6},{1,7},{2,4},{3,5},{4,2},{5,3},{6,0},{7,1},{8,14},{9,15},{10,... | collective-permute-start | bytes 196616 | tf_op jit(solution)/shard_map/ppermute | solution.py:230
  11.6 6.1 %collective-permute-start.2 = (f32[32,512]{1,0:T(8,128)S(1)}, f32[32,512]{1,0:T(8,128)S(1)}, u32[]{:S(2)}, u32[]{:S(2)}) collective-permute-start(f32[32,512]{1,0:T(8,128)S(1)} %added.4.refs_0_), channel_id=1, source_target_pairs={{0,4},{1,5},{2,6},{3,7},{4,0},{5,1},{6,2},{7,3},{8,12},{9,13},{10,... | collective-permute-start | bytes 196616 | tf_op jit(solution)/shard_map/ppermute | solution.py:230
  12.4 5.3 %collective-permute-start.1 = (f32[32,512]{1,0:T(8,128)S(1)}, f32[32,512]{1,0:T(8,128)S(1)}, u32[]{:S(2)}, u32[]{:S(2)}) collective-permute-start(f32[32,512]{1,0:T(8,128)S(1)} %added.4.refs_0_), channel_id=1, source_target_pairs={{0,2},{1,3},{2,0},{3,1},{4,6},{5,7},{6,4},{7,5},{8,10},{9,11},{10,... | collective-permute-start | bytes 196616 | tf_op jit(solution)/shard_map/ppermute | solution.py:230
  17.7 6.3 %collective-permute-start.6 = (f32[32,512]{1,0:T(8,128)S(1)}, f32[32,512]{1,0:T(8,128)S(1)}, u32[]{:S(2)}, u32[]{:S(2)}) collective-permute-start(f32[32,512]{1,0:T(8,128)S(1)} %added.5.refs_0_), channel_id=1, source_target_pairs={{0,96},{8,104},{16,112},{24,120},{32,64},{40,72},{48,80},{56,88},{... | collective-permute-start | bytes 196616 | tf_op jit(solution)/shard_map/ppermute | solution.py:230
  20.8 5.8 %collective-permute-start.5 = (f32[32,512]{1,0:T(8,128)S(1)}, f32[32,512]{1,0:T(8,128)S(1)}, u32[]{:S(2)}, u32[]{:S(2)}) collective-permute-start(f32[32,512]{1,0:T(8,128)S(1)} %added.5.refs_0_), channel_id=1, source_target_pairs={{0,64},{8,72},{16,80},{24,88},{32,96},{40,104},{48,112},{56,120},{... | collective-permute-start | bytes 196616 | tf_op jit(solution)/shard_map/ppermute | solution.py:230
  21.4 5.1 %collective-permute-start.4 = (f32[32,512]{1,0:T(8,128)S(1)}, f32[32,512]{1,0:T(8,128)S(1)}, u32[]{:S(2)}, u32[]{:S(2)}) collective-permute-start(f32[32,512]{1,0:T(8,128)S(1)} %added.5.refs_0_), channel_id=1, source_target_pairs={{0,32},{8,40},{16,48},{24,56},{32,0},{40,8},{48,16},{56,24},{64,96... | collective-permute-start | bytes 196616 | tf_op jit(solution)/shard_map/ppermute | solution.py:230
  26.6 6.6 %collective-permute-start.9 = (f32[32,512]{1,0:T(8,128)S(1)}, f32[32,512]{1,0:T(8,128)S(1)}, u32[]{:S(2)}, u32[]{:S(2)}) collective-permute-start(f32[32,512]{1,0:T(8,128)S(1)} %added.6.refs_0_), channel_id=1, source_target_pairs={{0,24},{8,16},{16,8},{24,0},{32,56},{40,48},{48,40},{56,32},{64,88... | collective-permute-start | bytes 196616 | tf_op jit(solution)/shard_map/ppermute | solution.py:230
  30.7 5.8 %collective-permute-start.8 = (f32[32,512]{1,0:T(8,128)S(1)}, f32[32,512]{1,0:T(8,128)S(1)}, u32[]{:S(2)}, u32[]{:S(2)}) collective-permute-start(f32[32,512]{1,0:T(8,128)S(1)} %added.6.refs_0_), channel_id=1, source_target_pairs={{0,16},{8,24},{16,0},{24,8},{32,48},{40,56},{48,32},{56,40},{64,80... | collective-permute-start | bytes 196616 | tf_op jit(solution)/shard_map/ppermute | solution.py:230
  30.7 5.8 %collective-permute-start.7 = (f32[32,512]{1,0:T(8,128)S(1)}, f32[32,512]{1,0:T(8,128)S(1)}, u32[]{:S(2)}, u32[]{:S(2)}) collective-permute-start(f32[32,512]{1,0:T(8,128)S(1)} %added.6.refs_0_), channel_id=1, source_target_pairs={{0,8},{8,0},{16,24},{24,16},{32,40},{40,32},{48,56},{56,48},{64,72... | collective-permute-start | bytes 196616 | tf_op jit(solution)/shard_map/ppermute | solution.py:230
  36.5 1.3 %collective-permute-start.10 = (f32[32,512]{1,0:T(8,128)S(1)}, f32[32,512]{1,0:T(8,128)S(1)}, u32[]{:S(2)}, u32[]{:S(2)}) collective-permute-start(f32[32,512]{1,0:T(8,128)S(1)} %added.7.mine), channel_id=1, source_target_pairs={{0,1},{1,0},{2,3},{3,2},{4,5},{5,4},{6,7},{7,6},{8,9},{9,8},{10,11... | collective-permute-start | bytes 196616 | tf_op jit(solution)/shard_map/ppermute | solution.py:230

commit v6 on v5

--- a/solution.py
+++ b/solution.py
@@ -232,7 +232,7 @@
 
 def summed_over_four(value, axis, stride):
     one, three, two = (swapped(value, axis, stride, distance) for distance in (1, 3, 2))
-    return added(value, one, two, three)
+    return added(value, one, three, two)
 
 
 def exchanged(pieces, axis):

time: 68.7 us -> 67.8 us (0.987)
  waiting for transfers between devices: 16.8 us -> 15.7 us
    ppermute x11, waiting for transfers between devices: 16.8 us -> 15.7 us  [swapped(): lax.ppermute(value, axis, [(i, i ^ distance * stride) for i in range(lax....]
where the time goes in v6:
time: 67.8 us; the launch traced here: 67.6 us
  blocking collectives  24.8 us (37%)
  waiting for transfers between devices  15.7 us (23%)
  starting transfers between devices  13.8 us (20%)
  Pallas kernels  11.5 us (17%)
  local copies, waits for them, and re-layouts  1.01 us (1%)
  between operations  0.7 us (1%)
    all_to_all x2, blocking collectives, exchanged(): return lax.all_to_all(pieces, axis, split_axis=0, concat_axis=0, tiled=True)  24.8 us
    ppermute x11, waiting for transfers between devices, swapped(): lax.ppermute(value, axis, [(i, i ^ distance * stride) for i in range(lax....  15.7 us
    ppermute x11, starting transfers between devices, swapped(): lax.ppermute(value, axis, [(i, i ^ distance * stride) for i in range(lax....  13.8 us
    pallas_call x1, Pallas kernels, merge(): pl.pallas_call(merge_kernel, out_shape=(jax.ShapeDtypeStruct((rows, cols)...  5.68 us
    pallas_call x1, Pallas kernels, subtract(): pl.pallas_call(functools.partial(subtract_kernel, 1.0 / count), out_shape...  3.41 us
    pallas_call x1, Pallas kernels, project(): pl.pallas_call(project_kernel, out_shape=(jax.ShapeDtypeStruct((rank, LAN...  2.32 us
  transfers between devices with their start and end apart: 11, of which 8 were waited for; matrix products, arithmetic and copies ran while one was open for 0% of the time, Pallas kernels for 0%

profile of v6, /device:TPU:0, one launch (start us, length us, event | category | flops | bytes accessed | tf_op | source)
XLA Modules:
  0.0 67.6 jit_solution(3634078243536347620)
XLA Ops:
  0.6 1.0 %copy-done = f32[3584,32]{0,1:T(8,128)S(1)} copy-done((f32[3584,32]{0,1:T(8,128)S(1)}, f32[3584,32]{0,1:T(8,128)}, u32[]{:S(2)}) %copy-start) | copy-done | bytes 458776
  1.6 5.7 %merge.1 = (bf16[1024,3584]{1,0:T(8,128)(2,1)S(1)}, f32[32,512]{1,0:T(8,128)S(1)}, f32[32,512]{1,0:T(8,128)S(1)}) custom-call(bf16[1,1024,3584]{2,1,0:T(8,128)(2,1)} %grads.1, bf16[1,1024,3584]{2,1,0:T(8,128)(2,1)} %errors.1, f32[32,3584]{1,0:T(8,128)S(1)} %bitcast.3), custom_call_target="tpu_custom_call" | custom-call | tf_op jit(solution)/shard_map/merge/pallas_call | solution.py:58
  7.3 0.1 collective-permute-start
  7.4 1.2 %collective-permute-done.refs_1_ = f32[32,512]{1,0:T(8,128)S(1)} collective-permute-done((f32[32,512]{1,0:T(8,128)S(1)}, f32[32,512]{1,0:T(8,128)S(1)}, u32[]{:S(2)}, u32[]{:S(2)}) %collective-permute-start) | collective-permute-done | bytes 65568 | tf_op jit(solution)/shard_map/ppermute | solution.py:230
  8.7 3.2 %collective-permute-start.3 = (f32[32,512]{1,0:T(8,128)S(1)}, f32[32,512]{1,0:T(8,128)S(1)}, u32[]{:S(2)}, u32[]{:S(2)}) collective-permute-start(f32[32,512]{1,0:T(8,128)S(1)} %added.4.refs_0_), channel_id=1, source_target_pairs={{0,4},{1,5},{2,6},{3,7},{4,0},{5,1},{6,2},{7,3},{8,12},{9,13},{10,... | collective-permute-start | bytes 196616 | tf_op jit(solution)/shard_map/ppermute | solution.py:230
  11.9 1.1 %collective-permute-start.2 = (f32[32,512]{1,0:T(8,128)S(1)}, f32[32,512]{1,0:T(8,128)S(1)}, u32[]{:S(2)}, u32[]{:S(2)}) collective-permute-start(f32[32,512]{1,0:T(8,128)S(1)} %added.4.refs_0_), channel_id=1, source_target_pairs={{0,6},{1,7},{2,4},{3,5},{4,2},{5,3},{6,0},{7,1},{8,14},{9,15},{10,... | collective-permute-start | bytes 196616 | tf_op jit(solution)/shard_map/ppermute | solution.py:230
  13.0 1.5 %collective-permute-done.3.refs_3_ = f32[32,512]{1,0:T(8,128)S(1)} collective-permute-done((f32[32,512]{1,0:T(8,128)S(1)}, f32[32,512]{1,0:T(8,128)S(1)}, u32[]{:S(2)}, u32[]{:S(2)}) %collective-permute-start.3) | collective-permute-done | bytes 65568 | tf_op jit(solution)/shard_map/ppermute | solution.py:230
  14.5 2.8 %collective-permute-done.2.refs_2_ = f32[32,512]{1,0:T(8,128)S(1)} collective-permute-done((f32[32,512]{1,0:T(8,128)S(1)}, f32[32,512]{1,0:T(8,128)S(1)}, u32[]{:S(2)}, u32[]{:S(2)}) %collective-permute-start.2) | collective-permute-done | bytes 65568 | tf_op jit(solution)/shard_map/ppermute | solution.py:230
  17.4 0.0 collective-permute-done.1.refs_1_
  17.4 3.3 %collective-permute-start.6 = (f32[32,512]{1,0:T(8,128)S(1)}, f32[32,512]{1,0:T(8,128)S(1)}, u32[]{:S(2)}, u32[]{:S(2)}) collective-permute-start(f32[32,512]{1,0:T(8,128)S(1)} %added.5.refs_0_), channel_id=1, source_target_pairs={{0,64},{8,72},{16,80},{24,88},{32,96},{40,104},{48,112},{56,120},{... | collective-permute-start | bytes 196616 | tf_op jit(solution)/shard_map/ppermute | solution.py:230
  20.6 1.1 %collective-permute-start.5 = (f32[32,512]{1,0:T(8,128)S(1)}, f32[32,512]{1,0:T(8,128)S(1)}, u32[]{:S(2)}, u32[]{:S(2)}) collective-permute-start(f32[32,512]{1,0:T(8,128)S(1)} %added.5.refs_0_), channel_id=1, source_target_pairs={{0,96},{8,104},{16,112},{24,120},{32,64},{40,72},{48,80},{56,88},{... | collective-permute-start | bytes 196616 | tf_op jit(solution)/shard_map/ppermute | solution.py:230
  21.7 1.5 %collective-permute-done.6.refs_3_ = f32[32,512]{1,0:T(8,128)S(1)} collective-permute-done((f32[32,512]{1,0:T(8,128)S(1)}, f32[32,512]{1,0:T(8,128)S(1)}, u32[]{:S(2)}, u32[]{:S(2)}) %collective-permute-start.6) | collective-permute-done | bytes 65568 | tf_op jit(solution)/shard_map/ppermute | solution.py:230
  23.3 2.9 %collective-permute-done.5.refs_2_ = f32[32,512]{1,0:T(8,128)S(1)} collective-permute-done((f32[32,512]{1,0:T(8,128)S(1)}, f32[32,512]{1,0:T(8,128)S(1)}, u32[]{:S(2)}, u32[]{:S(2)}) %collective-permute-start.5) | collective-permute-done | bytes 65568 | tf_op jit(solution)/shard_map/ppermute | solution.py:230
  26.1 4.0 %collective-permute-start.9 = (f32[32,512]{1,0:T(8,128)S(1)}, f32[32,512]{1,0:T(8,128)S(1)}, u32[]{:S(2)}, u32[]{:S(2)}) collective-permute-start(f32[32,512]{1,0:T(8,128)S(1)} %added.6.refs_0_), channel_id=1, source_target_pairs={{0,16},{8,24},{16,0},{24,8},{32,48},{40,56},{48,32},{56,40},{64,80... | collective-permute-start | bytes 196616 | tf_op jit(solution)/shard_map/ppermute | solution.py:230
  30.1 0.7 %collective-permute-start.8 = (f32[32,512]{1,0:T(8,128)S(1)}, f32[32,512]{1,0:T(8,128)S(1)}, u32[]{:S(2)}, u32[]{:S(2)}) collective-permute-start(f32[32,512]{1,0:T(8,128)S(1)} %added.6.refs_0_), channel_id=1, source_target_pairs={{0,24},{8,16},{16,8},{24,0},{32,56},{40,48},{48,40},{56,32},{64,88... | collective-permute-start | bytes 196616 | tf_op jit(solution)/shard_map/ppermute | solution.py:230
  30.8 0.3 collective-permute-start.7
  31.1 1.3 %collective-permute-done.9.refs_3_ = f32[32,512]{1,0:T(8,128)S(1)} collective-permute-done((f32[32,512]{1,0:T(8,128)S(1)}, f32[32,512]{1,0:T(8,128)S(1)}, u32[]{:S(2)}, u32[]{:S(2)}) %collective-permute-start.9) | collective-permute-done | bytes 65568 | tf_op jit(solution)/shard_map/ppermute | solution.py:230
  32.5 3.1 %collective-permute-done.8.refs_2_ = f32[32,512]{1,0:T(8,128)S(1)} collective-permute-done((f32[32,512]{1,0:T(8,128)S(1)}, f32[32,512]{1,0:T(8,128)S(1)}, u32[]{:S(2)}, u32[]{:S(2)}) %collective-permute-start.8) | collective-permute-done | bytes 65568 | tf_op jit(solution)/shard_map/ppermute | solution.py:230
  35.6 0.1 collective-permute-start.10
  35.7 1.2 %collective-permute-done.10.other = f32[32,512]{1,0:T(8,128)S(1)} collective-permute-done((f32[32,512]{1,0:T(8,128)S(1)}, f32[32,512]{1,0:T(8,128)S(1)}, u32[]{:S(2)}, u32[]{:S(2)}) %collective-permute-start.10) | collective-permute-done | bytes 65568 | tf_op jit(solution)/shard_map/ppermute | solution.py:230
  36.9 2.3 %project.1 = (f32[32,128]{1,0:T(8,128)}, bf16[32,1024]{1,0:T(8,128)(2,1)S(1)}, bf16[16,8,896]{2,1,0:T(8,128)(2,1)S(1)}) custom-call(f32[32,512]{1,0:T(8,128)S(1)} %added.7.mine, f32[32,512]{1,0:T(8,128)S(1)} %collective-permute-done.10.other, bf16[1024,3584]{1,0:T(8,128)(2,1)S(1)} %get-tuple-element.13.matrix), custom_call_target="tpu_custom_call" | custom-call | tf_op jit(solution)/shard_map/project/pallas_call | solution.py:128
  39.3 13.2 %all_to_all.10.pieces = bf16[16,8,896]{2,1,0:T(8,128)(2,1)S(1)} all-to-all(bf16[16,8,896]{2,1,0:T(8,128)(2,1)S(1)} %get-tuple-element.14), channel_id=1, replica_groups=mesh['dp'=16,'tensor'=8] {'dp'}, dimensions={0} | all-to-all | bytes 458752 | tf_op jit(solution)/shard_map/all_to_all | solution.py:239
  52.5 11.7 %all_to_all.11.q_pieces = bf16[16,8,896]{2,1,0:T(8,128)(2,1)S(1)} all-to-all(bf16[16,8,896]{2,1,0:T(8,128)(2,1)S(1)} %summed_copies.1), channel_id=1, replica_groups=mesh['dp'=16,'tensor'=8] {'dp'}, dimensions={0} | all-to-all | bytes 458752 | tf_op jit(solution)/shard_map/all_to_all | solution.py:239
  64.2 3.4 %subtract.1 = (bf16[1,1024,3584]{2,1,0:T(8,128)(2,1)}, f32[32,3584]{1,0:T(8,128)}) custom-call(bf16[16,8,896]{2,1,0:T(8,128)(2,1)S(1)} %all_to_all.11.q_pieces, bf16[32,1024]{1,0:T(8,128)(2,1)S(1)} %get-tuple-element.15.p_b, bf16[1024,3584]{1,0:T(8,128)(2,1)S(1)} %get-tuple-element.13.matrix), custom_call_target="tpu_custom_call" | custom-call | tf_op jit(solution)/shard_map/subtract/pallas_call | solution.py:172
  (10 shorter events, 0.1 us)
Async XLA Ops:
  0.6 1.0 %copy-start = (f32[3584,32]{0,1:T(8,128)S(1)}, f32[3584,32]{0,1:T(8,128)}, u32[]{:S(2)}) copy-start(f32[3584,32]{0,1:T(8,128)} %param.5) | copy-start | bytes 1376260
  7.3 1.3 %collective-permute-start = (f32[32,512]{1,0:T(8,128)S(1)}, f32[32,512]{1,0:T(8,128)S(1)}, u32[]{:S(2)}, u32[]{:S(2)}) collective-permute-start(f32[32,512]{1,0:T(8,128)S(1)} %get-tuple-element.12), channel_id=1, source_target_pairs={{0,1},{1,0},{2,3},{3,2},{4,5},{5,4},{6,7},{7,6},{8,9},{9,8},{10,11... | collective-permute-start | bytes 196616 | tf_op jit(solution)/shard_map/ppermute | solution.py:230
  8.7 5.8 %collective-permute-start.3 = (f32[32,512]{1,0:T(8,128)S(1)}, f32[32,512]{1,0:T(8,128)S(1)}, u32[]{:S(2)}, u32[]{:S(2)}) collective-permute-start(f32[32,512]{1,0:T(8,128)S(1)} %added.4.refs_0_), channel_id=1, source_target_pairs={{0,4},{1,5},{2,6},{3,7},{4,0},{5,1},{6,2},{7,3},{8,12},{9,13},{10,... | collective-permute-start | bytes 196616 | tf_op jit(solution)/shard_map/ppermute | solution.py:230
  11.9 5.5 %collective-permute-start.2 = (f32[32,512]{1,0:T(8,128)S(1)}, f32[32,512]{1,0:T(8,128)S(1)}, u32[]{:S(2)}, u32[]{:S(2)}) collective-permute-start(f32[32,512]{1,0:T(8,128)S(1)} %added.4.refs_0_), channel_id=1, source_target_pairs={{0,6},{1,7},{2,4},{3,5},{4,2},{5,3},{6,0},{7,1},{8,14},{9,15},{10,... | collective-permute-start | bytes 196616 | tf_op jit(solution)/shard_map/ppermute | solution.py:230
  13.0 4.3 %collective-permute-start.1 = (f32[32,512]{1,0:T(8,128)S(1)}, f32[32,512]{1,0:T(8,128)S(1)}, u32[]{:S(2)}, u32[]{:S(2)}) collective-permute-start(f32[32,512]{1,0:T(8,128)S(1)} %added.4.refs_0_), channel_id=1, source_target_pairs={{0,2},{1,3},{2,0},{3,1},{4,6},{5,7},{6,4},{7,5},{8,10},{9,11},{10,... | collective-permute-start | bytes 196616 | tf_op jit(solution)/shard_map/ppermute | solution.py:230
  17.4 5.9 %collective-permute-start.6 = (f32[32,512]{1,0:T(8,128)S(1)}, f32[32,512]{1,0:T(8,128)S(1)}, u32[]{:S(2)}, u32[]{:S(2)}) collective-permute-start(f32[32,512]{1,0:T(8,128)S(1)} %added.5.refs_0_), channel_id=1, source_target_pairs={{0,64},{8,72},{16,80},{24,88},{32,96},{40,104},{48,112},{56,120},{... | collective-permute-start | bytes 196616 | tf_op jit(solution)/shard_map/ppermute | solution.py:230
  20.6 5.5 %collective-permute-start.5 = (f32[32,512]{1,0:T(8,128)S(1)}, f32[32,512]{1,0:T(8,128)S(1)}, u32[]{:S(2)}, u32[]{:S(2)}) collective-permute-start(f32[32,512]{1,0:T(8,128)S(1)} %added.5.refs_0_), channel_id=1, source_target_pairs={{0,96},{8,104},{16,112},{24,120},{32,64},{40,72},{48,80},{56,88},{... | collective-permute-start | bytes 196616 | tf_op jit(solution)/shard_map/ppermute | solution.py:230
  21.7 4.4 %collective-permute-start.4 = (f32[32,512]{1,0:T(8,128)S(1)}, f32[32,512]{1,0:T(8,128)S(1)}, u32[]{:S(2)}, u32[]{:S(2)}) collective-permute-start(f32[32,512]{1,0:T(8,128)S(1)} %added.5.refs_0_), channel_id=1, source_target_pairs={{0,32},{8,40},{16,48},{24,56},{32,0},{40,8},{48,16},{56,24},{64,96... | collective-permute-start | bytes 196616 | tf_op jit(solution)/shard_map/ppermute | solution.py:230
  26.1 6.3 %collective-permute-start.9 = (f32[32,512]{1,0:T(8,128)S(1)}, f32[32,512]{1,0:T(8,128)S(1)}, u32[]{:S(2)}, u32[]{:S(2)}) collective-permute-start(f32[32,512]{1,0:T(8,128)S(1)} %added.6.refs_0_), channel_id=1, source_target_pairs={{0,16},{8,24},{16,0},{24,8},{32,48},{40,56},{48,32},{56,40},{64,80... | collective-permute-start | bytes 196616 | tf_op jit(solution)/shard_map/ppermute | solution.py:230
  30.1 5.5 %collective-permute-start.8 = (f32[32,512]{1,0:T(8,128)S(1)}, f32[32,512]{1,0:T(8,128)S(1)}, u32[]{:S(2)}, u32[]{:S(2)}) collective-permute-start(f32[32,512]{1,0:T(8,128)S(1)} %added.6.refs_0_), channel_id=1, source_target_pairs={{0,24},{8,16},{16,8},{24,0},{32,56},{40,48},{48,40},{56,32},{64,88... | collective-permute-start | bytes 196616 | tf_op jit(solution)/shard_map/ppermute | solution.py:230
  30.8 4.8 %collective-permute-start.7 = (f32[32,512]{1,0:T(8,128)S(1)}, f32[32,512]{1,0:T(8,128)S(1)}, u32[]{:S(2)}, u32[]{:S(2)}) collective-permute-start(f32[32,512]{1,0:T(8,128)S(1)} %added.6.refs_0_), channel_id=1, source_target_pairs={{0,8},{8,0},{16,24},{24,16},{32,40},{40,32},{48,56},{56,48},{64,72... | collective-permute-start | bytes 196616 | tf_op jit(solution)/shard_map/ppermute | solution.py:230
  35.6 1.3 %collective-permute-start.10 = (f32[32,512]{1,0:T(8,128)S(1)}, f32[32,512]{1,0:T(8,128)S(1)}, u32[]{:S(2)}, u32[]{:S(2)}) collective-permute-start(f32[32,512]{1,0:T(8,128)S(1)} %added.7.mine), channel_id=1, source_target_pairs={{0,1},{1,0},{2,3},{3,2},{4,5},{5,4},{6,7},{7,6},{8,9},{9,8},{10,11... | collective-permute-start | bytes 196616 | tf_op jit(solution)/shard_map/ppermute | solution.py:230

commit v7 on v6

--- a/solution.py
+++ b/solution.py
@@ -13,8 +13,10 @@
 IN_VMEM = pl.BlockSpec(memory_space=pltpu.VMEM)
 IN_HBM = pl.BlockSpec(memory_space=pltpu.HBM)
 LANES = 128
-CHUNKS = 16
+CHUNKS = 4
 BLOCK = 16
+RING = 4
+FAR_FIRST = (2, 3, 1, 0)
 WIDTHS = (768, 768, 768, 512, 512, 256)
 STARTS = tuple(sum(WIDTHS[:i]) for i in range(len(WIDTHS)))
 
@@ -101,7 +103,8 @@
     return (work * lax.rsqrt(scale))[:, rank : 2 * rank]
 
 
-def project_kernel(mine, other, matrix, p_own, p_b, q_pieces, whole):
+def project_kernel(mine, other, matrix, p_own, p_b, *refs):
+    *q_parts, whole = refs
     rank, half = mine.shape
     first = on_first_core()
     whole[:, :half] = jnp.where(first, mine[...], other[...])
@@ -113,106 +116,85 @@
     p_own[...] = jnp.dot(inverse, own, precision=HIGHEST, preferred_element_type=F32)
     rounded = jnp.dot(inverse, p_sum, precision=HIGHEST, preferred_element_type=F32).astype(BF16)
     p_b[...] = rounded
-    count, height, width = q_pieces.shape
-    for j in range(count * height // rank):
-        q = jnp.dot(rounded, matrix[:, j * width : (j + 1) * width], preferred_element_type=F32).astype(BF16)
-        for s in range(rank // height):
-            q_pieces[j * (rank // height) + s] = q[s * height : (s + 1) * height]
-
-
-def project(mine, other, matrix, count):
+    width = q_parts[0].shape[1]
+    position = lax.rem(lax.axis_index("dp"), RING)
+    for distance in FAR_FIRST:
+        cols = pl.ds(pl.multiple_of((position ^ distance) * width, LANES), width)
+        product = jnp.dot(rounded, matrix[:, cols], preferred_element_type=F32)
+        q_parts[distance][...] = product.astype(BF16)
+
+
+def project(mine, other, matrix):
     rank = mine.shape[0]
     rows, cols = matrix.shape
-    height = 8
-    width = cols * rank // (count * height)
     return pl.pallas_call(
         project_kernel,
         out_shape=(
             jax.ShapeDtypeStruct((rank, LANES), F32),
             jax.ShapeDtypeStruct((rank, rows), BF16),
-            jax.ShapeDtypeStruct((count, height, width), BF16),
+            *[jax.ShapeDtypeStruct((rank, cols // RING), BF16)] * RING,
         ),
         in_specs=[IN_VMEM] * 3,
-        out_specs=(IN_VMEM,) * 3,
+        out_specs=(IN_VMEM,) * (2 + RING),
         scratch_shapes=[pltpu.VMEM((rank, rows), F32)],
         compiler_params=pltpu.CompilerParams(vmem_limit_bytes=24 << 20),
         name="project",
     )(mine, other, matrix)
 
 
-def subtract_kernel(mean, q_pieces, p_b, matrix, new_errors, q_out, out_buf, q_buf, sems, q_sem):
-    rank = p_b.shape[0]
-    count, height, width = q_pieces.shape
-    rows, cols = matrix.shape
-    per = rank // height
+def subtract_kernel(mean, distance, q_part, p_b, matrix, *refs):
+    new_errors, q_out, out_buf, q_buf, sems, q_sem = refs[-6:]
+    width = q_part.shape[1]
+    rows = matrix.shape[0]
     step = rows // CHUNKS
-    for j in range(count // per):
-        for s in range(per):
-            q_buf[s * height : (s + 1) * height, j * width : (j + 1) * width] = (
-                q_pieces[j * per + s].astype(F32) * mean
-            )
-    pltpu.make_async_copy(q_buf, q_out, q_sem).start()
+    position = lax.rem(lax.axis_index("dp"), RING)
+    cols = pl.ds(pl.multiple_of((position ^ distance) * width, LANES), width)
+    q_buf[...] = q_part[...].astype(F32) * mean
+    q_copy = pltpu.make_async_copy(q_buf, q_out.at[:, cols], q_sem)
+    q_copy.start()
     q_b = q_buf[...].astype(BF16)
     left = p_b[...].T
+    copies = []
     for i in range(CHUNKS):
         part = pl.ds(i * step, step)
         approx = jnp.dot(left[i * step : (i + 1) * step], q_b, preferred_element_type=F32)
-        out_buf[part, :] = (matrix[part, :].astype(F32) - approx).astype(BF16)
-        pltpu.make_async_copy(out_buf.at[part], new_errors.at[0, part], sems.at[i]).start()
-    for i in range(CHUNKS):
-        part = pl.ds(i * step, step)
-        pltpu.make_async_copy(out_buf.at[part], new_errors.at[0, part], sems.at[i]).wait()
-    pltpu.make_async_copy(q_buf, q_out, q_sem).wait()
-
-
-def subtract(q_pieces, p_b, matrix):
+        out_buf[part, :] = (matrix[part, cols].astype(F32) - approx).astype(BF16)
+        copies.append(pltpu.make_async_copy(out_buf.at[part], new_errors.at[0, part, cols], sems.at[i]))
+        copies[-1].start()
+    for copy in copies:
+        copy.wait()
+    q_copy.wait()
+
+
+def subtract(q_part, p_b, matrix, mean, distance, earlier):
     rows, cols = matrix.shape
-    rank = p_b.shape[0]
-    count = q_pieces.shape[0]
-    return pl.pallas_call(
-        functools.partial(subtract_kernel, 1.0 / count),
+    rank, width = q_part.shape
+    return pl.pallas_call(
+        functools.partial(subtract_kernel, mean, distance),
         out_shape=(
             jax.ShapeDtypeStruct((1, rows, cols), BF16),
             jax.ShapeDtypeStruct((rank, cols), F32),
         ),
-        in_specs=[IN_VMEM] * 3,
+        in_specs=[IN_VMEM] * 3 + [IN_HBM] * len(earlier),
         out_specs=(IN_HBM, IN_HBM),
         scratch_shapes=[
-            pltpu.VMEM((rows, cols), BF16),
-            pltpu.VMEM((rank, cols), F32),
+            pltpu.VMEM((rows, width), BF16),
+            pltpu.VMEM((rank, width), F32),
             pltpu.SemaphoreType.DMA((CHUNKS,)),
             pltpu.SemaphoreType.DMA(()),
         ],
-        compiler_params=pltpu.CompilerParams(vmem_limit_bytes=24 << 20),
+        input_output_aliases={3: 0, 4: 1} if earlier else {},
+        compiler_params=pltpu.CompilerParams(vmem_limit_bytes=12 << 20),
+        cost_estimate=pl.CostEstimate(flops=2 * rows * width * rank, bytes_accessed=2 * rows * width, transcendentals=0),
         name="subtract",
-    )(q_pieces, p_b, matrix)
-
-
-def total_kernel(pieces, copies):
-    total = pieces[0].astype(F32)
-    for i in range(1, pieces.shape[0]):
-        total = total + pieces[i].astype(F32)
-    total = total.astype(copies.dtype)
-    for i in range(copies.shape[0]):
-        copies[i] = total
-
-
-def summed_copies(pieces, count):
-    return pl.pallas_call(
-        total_kernel,
-        out_shape=jax.ShapeDtypeStruct((count, *pieces.shape[1:]), pieces.dtype),
-        in_specs=[IN_VMEM],
-        out_specs=IN_VMEM,
-        compiler_params=pltpu.CompilerParams(vmem_limit_bytes=4 << 20),
-        name="summed_copies",
-    )(pieces)
+    )(q_part, p_b, matrix, *earlier)
 
 
 def added_kernel(*refs):
-    terms = [ref[...] for ref in refs[:-1]]
+    terms = [ref[...].astype(F32) for ref in refs[:-1]]
     while len(terms) > 1:
         terms = [terms[i] + terms[i + 1] for i in range(0, len(terms), 2)]
-    refs[-1][...] = terms[0]
+    refs[-1][...] = terms[0].astype(refs[-1].dtype)
 
 
 def added(*terms):
@@ -232,11 +214,7 @@
 
 def summed_over_four(value, axis, stride):
     one, three, two = (swapped(value, axis, stride, distance) for distance in (1, 3, 2))
-    return added(value, one, three, two)
-
-
-def exchanged(pieces, axis):
-    return lax.all_to_all(pieces, axis, split_axis=0, concat_axis=0, tiled=True)
+    return added(two, three, one, value)
 
 
 def on_device(grads, errors, basis):
@@ -245,10 +223,14 @@
     mine = summed_over_four(mine, "tensor", 2)
     mine = summed_over_four(mine, "dp", 4)
     mine = summed_over_four(mine, "dp", 1)
-    n_dp = lax.axis_size("dp")
-    p_own, p_b, q_pieces = project(mine, swapped(mine, "tensor", 1, 1), matrix, n_dp)
-    q_sums = exchanged(summed_copies(exchanged(q_pieces, "dp"), n_dp), "dp")
-    new_errors, q_out = subtract(q_sums, p_b, matrix)
+    p_own, p_b, *q_parts = project(mine, swapped(mine, "tensor", 1, 1), matrix)
+    one, three, two = (swapped(q_parts[distance], "dp", 1, distance) for distance in (1, 3, 2))
+    q_sum = summed_over_four(added(two, three, one, q_parts[0]), "dp", 4)
+    mean, earlier = 1.0 / lax.axis_size("dp"), ()
+    for distance in (0, 2, 1, 3):
+        q_part = swapped(q_sum, "dp", 1, distance) if distance else q_sum
+        earlier = subtract(q_part, p_b, matrix, mean, distance, earlier)
+    new_errors, q_out = earlier
     return new_errors, p_own.T, q_out.T
 
 

time: 67.8 us -> 64.5 us (0.951)
  blocking collectives: 24.8 us -> 0 us
  starting transfers between devices: 13.8 us -> 25.1 us
  waiting for transfers between devices: 15.7 us -> 22.9 us
  Pallas kernels: 11.5 us -> 14.5 us
    all_to_all x2 -> x0, blocking collectives: 24.8 us -> none  [exchanged(): return lax.all_to_all(pieces, axis, split_axis=0, concat_axis=0, tiled=True)]
    ppermute x11 -> x20, starting transfers between devices: 13.8 us -> 25.1 us  [swapped(): lax.ppermute(value, axis, [(i, i ^ distance * stride) for i in range(lax....]
    ppermute x11 -> x20, waiting for transfers between devices: 15.7 us -> 22.9 us  [swapped(): lax.ppermute(value, axis, [(i, i ^ distance * stride) for i in range(lax....]
    pallas_call x2 -> x4, Pallas kernels: 3.46 us -> 6.39 us  [subtract(): pl.pallas_call(functools.partial(subtract_kernel, mean, distance), out_sh...]
  transfers between devices with their start and end apart: 11 -> 20, of which waited for: 8 -> 12; matrix products, arithmetic and copies ran while one was open for 0% -> 0% of each run, Pallas kernels for 0% -> 7%
where the time goes in v7:
time: 64.5 us; the launch traced here: 64.3 us
  starting transfers between devices  25.1 us (39%)
  waiting for transfers between devices  22.9 us (36%)
  Pallas kernels  14.5 us (22%)
  local copies, waits for them, and re-layouts  1.01 us (2%)
  between operations  0.76 us (1%)
    ppermute x20, starting transfers between devices, swapped(): lax.ppermute(value, axis, [(i, i ^ distance * stride) for i in range(lax....  25.1 us
    ppermute x20, waiting for transfers between devices, swapped(): lax.ppermute(value, axis, [(i, i ^ distance * stride) for i in range(lax....  22.9 us
    pallas_call x4, Pallas kernels, subtract(): pl.pallas_call(functools.partial(subtract_kernel, mean, distance), out_sh...  6.39 us
    pallas_call x1, Pallas kernels, merge(): pl.pallas_call(merge_kernel, out_shape=(jax.ShapeDtypeStruct((rows, cols)...  5.68 us
    pallas_call x1, Pallas kernels, project(): pl.pallas_call(project_kernel, out_shape=(jax.ShapeDtypeStruct((rank, LAN...  2.33 us
  transfers between devices with their start and end apart: 20, of which 12 were waited for; matrix products, arithmetic and copies ran while one was open for 0% of the time, Pallas kernels for 7%

profile of v7, /device:TPU:0, one launch (start us, length us, event | category | flops | bytes accessed | tf_op | source)
XLA Modules:
  0.0 64.3 jit_solution(7489766963064097480)
XLA Ops:
  1.6 5.7 %merge.1 = (bf16[1024,3584]{1,0:T(8,128)(2,1)S(1)}, f32[32,512]{1,0:T(8,128)S(1)}, f32[32,512]{1,0:T(8,128)S(1)}) custom-call(bf16[1,1024,3584]{2,1,0:T(8,128)(2,1)} %grads.1, bf16[1,1024,3584]{2,1,0:T(8,128)(2,1)} %errors.1, f32[32,3584]{1,0:T(8,128)S(1)} %bitcast.3), custom_call_target="tpu_custom_call" | custom-call | tf_op jit(solution)/shard_map/merge/pallas_call | solution.py:60
  7.4 1.2 %collective-permute-done.refs_1_ = f32[32,512]{1,0:T(8,128)S(1)} collective-permute-done((f32[32,512]{1,0:T(8,128)S(1)}, f32[32,512]{1,0:T(8,128)S(1)}, u32[]{:S(2)}, u32[]{:S(2)}) %collective-permute-start) | collective-permute-done | bytes 65568 | tf_op jit(solution)/shard_map/ppermute | solution.py:212
  8.7 3.2 %collective-permute-start.1 = (f32[32,512]{1,0:T(8,128)S(1)}, f32[32,512]{1,0:T(8,128)S(1)}, u32[]{:S(2)}, u32[]{:S(2)}) collective-permute-start(f32[32,512]{1,0:T(8,128)S(1)} %added.6.refs_3_), channel_id=1, source_target_pairs={{0,4},{1,5},{2,6},{3,7},{4,0},{5,1},{6,2},{7,3},{8,12},{9,13},{10,... | collective-permute-start | bytes 196616 | tf_op jit(solution)/shard_map/ppermute | solution.py:212
  13.0 1.5 %collective-permute-done.1.refs_0_ = f32[32,512]{1,0:T(8,128)S(1)} collective-permute-done((f32[32,512]{1,0:T(8,128)S(1)}, f32[32,512]{1,0:T(8,128)S(1)}, u32[]{:S(2)}, u32[]{:S(2)}) %collective-permute-start.1) | collective-permute-done | bytes 65568 | tf_op jit(solution)/shard_map/ppermute | solution.py:212
  14.5 2.8 %collective-permute-done.2.refs_1_ = f32[32,512]{1,0:T(8,128)S(1)} collective-permute-done((f32[32,512]{1,0:T(8,128)S(1)}, f32[32,512]{1,0:T(8,128)S(1)}, u32[]{:S(2)}, u32[]{:S(2)}) %collective-permute-start.2) | collective-permute-done | bytes 65568 | tf_op jit(solution)/shard_map/ppermute | solution.py:212
  17.4 3.3 %collective-permute-start.4 = (f32[32,512]{1,0:T(8,128)S(1)}, f32[32,512]{1,0:T(8,128)S(1)}, u32[]{:S(2)}, u32[]{:S(2)}) collective-permute-start(f32[32,512]{1,0:T(8,128)S(1)} %added.7.refs_3_), channel_id=1, source_target_pairs={{0,64},{8,72},{16,80},{24,88},{32,96},{40,104},{48,112},{56,120},{... | collective-permute-start | bytes 196616 | tf_op jit(solution)/shard_map/ppermute | solution.py:212
  21.7 1.5 %collective-permute-done.4.refs_0_ = f32[32,512]{1,0:T(8,128)S(1)} collective-permute-done((f32[32,512]{1,0:T(8,128)S(1)}, f32[32,512]{1,0:T(8,128)S(1)}, u32[]{:S(2)}, u32[]{:S(2)}) %collective-permute-start.4) | collective-permute-done | bytes 65568 | tf_op jit(solution)/shard_map/ppermute | solution.py:212
  23.3 2.9 %collective-permute-done.5.refs_1_ = f32[32,512]{1,0:T(8,128)S(1)} collective-permute-done((f32[32,512]{1,0:T(8,128)S(1)}, f32[32,512]{1,0:T(8,128)S(1)}, u32[]{:S(2)}, u32[]{:S(2)}) %collective-permute-start.5) | collective-permute-done | bytes 65568 | tf_op jit(solution)/shard_map/ppermute | solution.py:212
  26.1 4.0 %collective-permute-start.7 = (f32[32,512]{1,0:T(8,128)S(1)}, f32[32,512]{1,0:T(8,128)S(1)}, u32[]{:S(2)}, u32[]{:S(2)}) collective-permute-start(f32[32,512]{1,0:T(8,128)S(1)} %added.8.refs_3_), channel_id=1, source_target_pairs={{0,16},{8,24},{16,0},{24,8},{32,48},{40,56},{48,32},{56,40},{64,80... | collective-permute-start | bytes 196616 | tf_op jit(solution)/shard_map/ppermute | solution.py:212
  31.1 1.3 %collective-permute-done.7.refs_0_ = f32[32,512]{1,0:T(8,128)S(1)} collective-permute-done((f32[32,512]{1,0:T(8,128)S(1)}, f32[32,512]{1,0:T(8,128)S(1)}, u32[]{:S(2)}, u32[]{:S(2)}) %collective-permute-start.7) | collective-permute-done | bytes 65568 | tf_op jit(solution)/shard_map/ppermute | solution.py:212
  32.5 3.1 %collective-permute-done.8.refs_1_ = f32[32,512]{1,0:T(8,128)S(1)} collective-permute-done((f32[32,512]{1,0:T(8,128)S(1)}, f32[32,512]{1,0:T(8,128)S(1)}, u32[]{:S(2)}, u32[]{:S(2)}) %collective-permute-start.8) | collective-permute-done | bytes 65568 | tf_op jit(solution)/shard_map/ppermute | solution.py:212
  35.7 1.2 %collective-permute-done.10.other = f32[32,512]{1,0:T(8,128)S(1)} collective-permute-done((f32[32,512]{1,0:T(8,128)S(1)}, f32[32,512]{1,0:T(8,128)S(1)}, u32[]{:S(2)}, u32[]{:S(2)}) %collective-permute-start.10) | collective-permute-done | bytes 65568 | tf_op jit(solution)/shard_map/ppermute | solution.py:212
  36.9 2.3 %project.1 = (f32[32,128]{1,0:T(8,128)}, bf16[32,1024]{1,0:T(8,128)(2,1)S(1)}, bf16[32,896]{1,0:T(8,128)(2,1)S(1)}, bf16[32,896]{1,0:T(8,128)(2,1)S(1)}, bf16[32...) custom-call(f32[32,512]{1,0:T(8,128)S(1)} %added.9.mine, f32[32,512]{1,0:T(8,128)S(1)} %collective-permute-done.10.other, ...), custom_call_target="tpu_custom_call" | custom-call | tf_op jit(solution)/shard_map/project/pallas_call | solution.py:130
  39.3 1.9 %collective-permute-start.11 = (bf16[32,896]{1,0:T(8,128)(2,1)S(1)}, bf16[32,896]{1,0:T(8,128)(2,1)S(1)}, u32[]{:S(2)}, u32[]{:S(2)}) collective-permute-start(bf16[32,896]{1,0:T(8,128)(2,1)S(1)} %get-tuple-element.23), channel_id=1, source_target_pairs={{0,16},{8,24},{16,0},{24,8},{32,48},{40,56},{48,32},{56,40},{64,80... | collective-permute-start | bytes 172040 | tf_op jit(solution)/shard_map/ppermute | solution.py:212
  42.8 2.2 %collective-permute-done.11.refs_0_ = bf16[32,896]{1,0:T(8,128)(2,1)S(1)} collective-permute-done((bf16[32,896]{1,0:T(8,128)(2,1)S(1)}, bf16[32,896]{1,0:T(8,128)(2,1)S(1)}, u32[]{:S(2)}, u32[]{:S(2)}) %collective-permute-start.11) | collective-permute-done | bytes 57376 | tf_op jit(solution)/shard_map/ppermute | solution.py:212
  45.1 1.6 %collective-permute-done.12.refs_1_ = bf16[32,896]{1,0:T(8,128)(2,1)S(1)} collective-permute-done((bf16[32,896]{1,0:T(8,128)(2,1)S(1)}, bf16[32,896]{1,0:T(8,128)(2,1)S(1)}, u32[]{:S(2)}, u32[]{:S(2)}) %collective-permute-start.12) | collective-permute-done | bytes 57376 | tf_op jit(solution)/shard_map/ppermute | solution.py:212
  46.7 1.6 %collective-permute-start.14 = (bf16[32,896]{1,0:T(8,128)(2,1)S(1)}, bf16[32,896]{1,0:T(8,128)(2,1)S(1)}, u32[]{:S(2)}, u32[]{:S(2)}) collective-permute-start(bf16[32,896]{1,0:T(8,128)(2,1)S(1)} %added.10.refs_3_), channel_id=1, source_target_pairs={{0,64},{8,72},{16,80},{24,88},{32,96},{40,104},{48,112},{56,120},{... | collective-permute-start | bytes 172040 | tf_op jit(solution)/shard_map/ppermute | solution.py:212
  50.2 2.8 %collective-permute-done.14.refs_0_ = bf16[32,896]{1,0:T(8,128)(2,1)S(1)} collective-permute-done((bf16[32,896]{1,0:T(8,128)(2,1)S(1)}, bf16[32,896]{1,0:T(8,128)(2,1)S(1)}, u32[]{:S(2)}, u32[]{:S(2)}) %collective-permute-start.14) | collective-permute-done | bytes 57376 | tf_op jit(solution)/shard_map/ppermute | solution.py:212
  53.7 1.9 %collective-permute-start.19 = (bf16[32,896]{1,0:T(8,128)(2,1)S(1)}, bf16[32,896]{1,0:T(8,128)(2,1)S(1)}, u32[]{:S(2)}, u32[]{:S(2)}) collective-permute-start(bf16[32,896]{1,0:T(8,128)(2,1)S(1)} %added.11.q_part), channel_id=1, source_target_pairs={{0,16},{8,24},{16,0},{24,8},{32,48},{40,56},{48,32},{56,40},{64,80... | collective-permute-start | bytes 172040 | tf_op jit(solution)/shard_map/ppermute | solution.py:212
  56.7 1.2 %collective-permute-start.17 = (bf16[32,896]{1,0:T(8,128)(2,1)S(1)}, bf16[32,896]{1,0:T(8,128)(2,1)S(1)}, u32[]{:S(2)}, u32[]{:S(2)}) collective-permute-start(bf16[32,896]{1,0:T(8,128)(2,1)S(1)} %added.11.q_part), channel_id=1, source_target_pairs={{0,24},{8,16},{16,8},{24,0},{32,56},{40,48},{48,40},{56,32},{64,88... | collective-permute-start | bytes 172040 | tf_op jit(solution)/shard_map/ppermute | solution.py:212
  57.9 1.6 %subtract.4 = (bf16[1,1024,3584]{2,1,0:T(8,128)(2,1)}, f32[32,3584]{1,0:T(8,128)}) custom-call(bf16[32,896]{1,0:T(8,128)(2,1)S(1)} %added.11.q_part, bf16[32,1024]{1,0:T(8,128)(2,1)S(1)} %get-tuple-element.27.p_b, bf16[1024,3584]{1,0:T(8,128)(2,1)S(1)} %get-tuple-element.22.matrix), custom_call_target="tpu_custom_call" | custom-call | flops 58720256 | bytes 1835008 | tf_op jit(solution)/shard_map/subtract/pallas_call | solution.py:172
  59.5 1.6 %subtract.5 = (bf16[1,1024,3584]{2,1,0:T(8,128)(2,1)}, f32[32,3584]{1,0:T(8,128)}) custom-call(bf16[32,896]{1,0:T(8,128)(2,1)S(1)} %collective-permute-done.19.q_part, bf16[32,1024]{1,0:T(8,128)(2,1)S(1)} %get-tuple-element.27.p_b, bf16[1024,3584]{1,0:T(8,128)(2,1)S(1)} %get-tuple-element.22.matrix, ...), custom_call_target="tpu_custom_call", output_to_operand_aliasing={{0}: (3, {}), {1}: (4, {})} | custom-call | flops 58720256 | bytes 1835008 | tf_op jit(solution)/shard_map/subtract/pallas_call | solution.py:172
  61.1 1.6 %subtract.6 = (bf16[1,1024,3584]{2,1,0:T(8,128)(2,1)}, f32[32,3584]{1,0:T(8,128)}) custom-call(bf16[32,896]{1,0:T(8,128)(2,1)S(1)} %collective-permute-done.18.q_part, bf16[32,1024]{1,0:T(8,128)(2,1)S(1)} %get-tuple-element.27.p_b, bf16[1024,3584]{1,0:T(8,128)(2,1)S(1)} %get-tuple-element.22.matrix, ...), custom_call_target="tpu_custom_call", output_to_operand_aliasing={{0}: (3, {}), {1}: (4, {})} | custom-call | flops 58720256 | bytes 1835008 | tf_op jit(solution)/shard_map/subtract/pallas_call | solution.py:172
  62.7 1.6 %subtract.7 = (bf16[1,1024,3584]{2,1,0:T(8,128)(2,1)}, f32[32,3584]{1,0:T(8,128)}) custom-call(bf16[32,896]{1,0:T(8,128)(2,1)S(1)} %collective-permute-done.17.q_part, bf16[32,1024]{1,0:T(8,128)(2,1)S(1)} %get-tuple-element.27.p_b, bf16[1024,3584]{1,0:T(8,128)(2,1)S(1)} %get-tuple-element.22.matrix, ...), custom_call_target="tpu_custom_call", output_to_operand_aliasing={{0}: (3, {}), {1}: (4, {})} | custom-call | flops 58720256 | bytes 1835008 | tf_op jit(solution)/shard_map/subtract/pallas_call | solution.py:172
  (30 shorter events, 9.8 us)
Async XLA Ops:
  0.6 1.0 %copy-start = (f32[3584,32]{0,1:T(8,128)S(1)}, f32[3584,32]{0,1:T(8,128)}, u32[]{:S(2)}) copy-start(f32[3584,32]{0,1:T(8,128)} %param.5) | copy-start | bytes 1376260
  7.3 1.3 %collective-permute-start = (f32[32,512]{1,0:T(8,128)S(1)}, f32[32,512]{1,0:T(8,128)S(1)}, u32[]{:S(2)}, u32[]{:S(2)}) collective-permute-start(f32[32,512]{1,0:T(8,128)S(1)} %get-tuple-element.21), channel_id=1, source_target_pairs={{0,1},{1,0},{2,3},{3,2},{4,5},{5,4},{6,7},{7,6},{8,9},{9,8},{10,11... | collective-permute-start | bytes 196616 | tf_op jit(solution)/shard_map/ppermute | solution.py:212
  8.7 5.8 %collective-permute-start.1 = (f32[32,512]{1,0:T(8,128)S(1)}, f32[32,512]{1,0:T(8,128)S(1)}, u32[]{:S(2)}, u32[]{:S(2)}) collective-permute-start(f32[32,512]{1,0:T(8,128)S(1)} %added.6.refs_3_), channel_id=1, source_target_pairs={{0,4},{1,5},{2,6},{3,7},{4,0},{5,1},{6,2},{7,3},{8,12},{9,13},{10,... | collective-permute-start | bytes 196616 | tf_op jit(solution)/shard_map/ppermute | solution.py:212
  11.9 5.5 %collective-permute-start.2 = (f32[32,512]{1,0:T(8,128)S(1)}, f32[32,512]{1,0:T(8,128)S(1)}, u32[]{:S(2)}, u32[]{:S(2)}) collective-permute-start(f32[32,512]{1,0:T(8,128)S(1)} %added.6.refs_3_), channel_id=1, source_target_pairs={{0,6},{1,7},{2,4},{3,5},{4,2},{5,3},{6,0},{7,1},{8,14},{9,15},{10,... | collective-permute-start | bytes 196616 | tf_op jit(solution)/shard_map/ppermute | solution.py:212
  13.0 4.3 %collective-permute-start.3 = (f32[32,512]{1,0:T(8,128)S(1)}, f32[32,512]{1,0:T(8,128)S(1)}, u32[]{:S(2)}, u32[]{:S(2)}) collective-permute-start(f32[32,512]{1,0:T(8,128)S(1)} %added.6.refs_3_), channel_id=1, source_target_pairs={{0,2},{1,3},{2,0},{3,1},{4,6},{5,7},{6,4},{7,5},{8,10},{9,11},{10,... | collective-permute-start | bytes 196616 | tf_op jit(solution)/shard_map/ppermute | solution.py:212
  17.4 5.9 %collective-permute-start.4 = (f32[32,512]{1,0:T(8,128)S(1)}, f32[32,512]{1,0:T(8,128)S(1)}, u32[]{:S(2)}, u32[]{:S(2)}) collective-permute-start(f32[32,512]{1,0:T(8,128)S(1)} %added.7.refs_3_), channel_id=1, source_target_pairs={{0,64},{8,72},{16,80},{24,88},{32,96},{40,104},{48,112},{56,120},{... | collective-permute-start | bytes 196616 | tf_op jit(solution)/shard_map/ppermute | solution.py:212
  20.6 5.5 %collective-permute-start.5 = (f32[32,512]{1,0:T(8,128)S(1)}, f32[32,512]{1,0:T(8,128)S(1)}, u32[]{:S(2)}, u32[]{:S(2)}) collective-permute-start(f32[32,512]{1,0:T(8,128)S(1)} %added.7.refs_3_), channel_id=1, source_target_pairs={{0,96},{8,104},{16,112},{24,120},{32,64},{40,72},{48,80},{56,88},{... | collective-permute-start | bytes 196616 | tf_op jit(solution)/shard_map/ppermute | solution.py:212
  21.7 4.4 %collective-permute-start.6 = (f32[32,512]{1,0:T(8,128)S(1)}, f32[32,512]{1,0:T(8,128)S(1)}, u32[]{:S(2)}, u32[]{:S(2)}) collective-permute-start(f32[32,512]{1,0:T(8,128)S(1)} %added.7.refs_3_), channel_id=1, source_target_pairs={{0,32},{8,40},{16,48},{24,56},{32,0},{40,8},{48,16},{56,24},{64,96... | collective-permute-start | bytes 196616 | tf_op jit(solution)/shard_map/ppermute | solution.py:212
  26.1 6.3 %collective-permute-start.7 = (f32[32,512]{1,0:T(8,128)S(1)}, f32[32,512]{1,0:T(8,128)S(1)}, u32[]{:S(2)}, u32[]{:S(2)}) collective-permute-start(f32[32,512]{1,0:T(8,128)S(1)} %added.8.refs_3_), channel_id=1, source_target_pairs={{0,16},{8,24},{16,0},{24,8},{32,48},{40,56},{48,32},{56,40},{64,80... | collective-permute-start | bytes 196616 | tf_op jit(solution)/shard_map/ppermute | solution.py:212
  30.1 5.5 %collective-permute-start.8 = (f32[32,512]{1,0:T(8,128)S(1)}, f32[32,512]{1,0:T(8,128)S(1)}, u32[]{:S(2)}, u32[]{:S(2)}) collective-permute-start(f32[32,512]{1,0:T(8,128)S(1)} %added.8.refs_3_), channel_id=1, source_target_pairs={{0,24},{8,16},{16,8},{24,0},{32,56},{40,48},{48,40},{56,32},{64,88... | collective-permute-start | bytes 196616 | tf_op jit(solution)/shard_map/ppermute | solution.py:212
  30.8 4.8 %collective-permute-start.9 = (f32[32,512]{1,0:T(8,128)S(1)}, f32[32,512]{1,0:T(8,128)S(1)}, u32[]{:S(2)}, u32[]{:S(2)}) collective-permute-start(f32[32,512]{1,0:T(8,128)S(1)} %added.8.refs_3_), channel_id=1, source_target_pairs={{0,8},{8,0},{16,24},{24,16},{32,40},{40,32},{48,56},{56,48},{64,72... | collective-permute-start | bytes 196616 | tf_op jit(solution)/shard_map/ppermute | solution.py:212
  35.6 1.3 %collective-permute-start.10 = (f32[32,512]{1,0:T(8,128)S(1)}, f32[32,512]{1,0:T(8,128)S(1)}, u32[]{:S(2)}, u32[]{:S(2)}) collective-permute-start(f32[32,512]{1,0:T(8,128)S(1)} %added.9.mine), channel_id=1, source_target_pairs={{0,1},{1,0},{2,3},{3,2},{4,5},{5,4},{6,7},{7,6},{8,9},{9,8},{10,11... | collective-permute-start | bytes 196616 | tf_op jit(solution)/shard_map/ppermute | solution.py:212
  39.3 5.8 %collective-permute-start.11 = (bf16[32,896]{1,0:T(8,128)(2,1)S(1)}, bf16[32,896]{1,0:T(8,128)(2,1)S(1)}, u32[]{:S(2)}, u32[]{:S(2)}) collective-permute-start(bf16[32,896]{1,0:T(8,128)(2,1)S(1)} %get-tuple-element.23), channel_id=1, source_target_pairs={{0,16},{8,24},{16,0},{24,8},{32,48},{40,56},{48,32},{56,40},{64,80... | collective-permute-start | bytes 172040 | tf_op jit(solution)/shard_map/ppermute | solution.py:212
  41.2 5.4 %collective-permute-start.12 = (bf16[32,896]{1,0:T(8,128)(2,1)S(1)}, bf16[32,896]{1,0:T(8,128)(2,1)S(1)}, u32[]{:S(2)}, u32[]{:S(2)}) collective-permute-start(bf16[32,896]{1,0:T(8,128)(2,1)S(1)} %get-tuple-element.24), channel_id=1, source_target_pairs={{0,24},{8,16},{16,8},{24,0},{32,56},{40,48},{48,40},{56,32},{64,88... | collective-permute-start | bytes 172040 | tf_op jit(solution)/shard_map/ppermute | solution.py:212
  41.8 4.8 %collective-permute-start.13 = (bf16[32,896]{1,0:T(8,128)(2,1)S(1)}, bf16[32,896]{1,0:T(8,128)(2,1)S(1)}, u32[]{:S(2)}, u32[]{:S(2)}) collective-permute-start(bf16[32,896]{1,0:T(8,128)(2,1)S(1)} %get-tuple-element.25), channel_id=1, source_target_pairs={{0,8},{8,0},{16,24},{24,16},{32,40},{40,32},{48,56},{56,48},{64,72... | collective-permute-start | bytes 172040 | tf_op jit(solution)/shard_map/ppermute | solution.py:212
  46.7 6.3 %collective-permute-start.14 = (bf16[32,896]{1,0:T(8,128)(2,1)S(1)}, bf16[32,896]{1,0:T(8,128)(2,1)S(1)}, u32[]{:S(2)}, u32[]{:S(2)}) collective-permute-start(bf16[32,896]{1,0:T(8,128)(2,1)S(1)} %added.10.refs_3_), channel_id=1, source_target_pairs={{0,64},{8,72},{16,80},{24,88},{32,96},{40,104},{48,112},{56,120},{... | collective-permute-start | bytes 172040 | tf_op jit(solution)/shard_map/ppermute | solution.py:212
  48.3 5.4 %collective-permute-start.15 = (bf16[32,896]{1,0:T(8,128)(2,1)S(1)}, bf16[32,896]{1,0:T(8,128)(2,1)S(1)}, u32[]{:S(2)}, u32[]{:S(2)}) collective-permute-start(bf16[32,896]{1,0:T(8,128)(2,1)S(1)} %added.10.refs_3_), channel_id=1, source_target_pairs={{0,96},{8,104},{16,112},{24,120},{32,64},{40,72},{48,80},{56,88},{... | collective-permute-start | bytes 172040 | tf_op jit(solution)/shard_map/ppermute | solution.py:212
  49.2 4.4 %collective-permute-start.16 = (bf16[32,896]{1,0:T(8,128)(2,1)S(1)}, bf16[32,896]{1,0:T(8,128)(2,1)S(1)}, u32[]{:S(2)}, u32[]{:S(2)}) collective-permute-start(bf16[32,896]{1,0:T(8,128)(2,1)S(1)} %added.10.refs_3_), channel_id=1, source_target_pairs={{0,32},{8,40},{16,48},{24,56},{32,0},{40,8},{48,16},{56,24},{64,96... | collective-permute-start | bytes 172040 | tf_op jit(solution)/shard_map/ppermute | solution.py:212
  53.7 5.8 %collective-permute-start.19 = (bf16[32,896]{1,0:T(8,128)(2,1)S(1)}, bf16[32,896]{1,0:T(8,128)(2,1)S(1)}, u32[]{:S(2)}, u32[]{:S(2)}) collective-permute-start(bf16[32,896]{1,0:T(8,128)(2,1)S(1)} %added.11.q_part), channel_id=1, source_target_pairs={{0,16},{8,24},{16,0},{24,8},{32,48},{40,56},{48,32},{56,40},{64,80... | collective-permute-start | bytes 172040 | tf_op jit(solution)/shard_map/ppermute | solution.py:212
  55.6 5.4 %collective-permute-start.18 = (bf16[32,896]{1,0:T(8,128)(2,1)S(1)}, bf16[32,896]{1,0:T(8,128)(2,1)S(1)}, u32[]{:S(2)}, u32[]{:S(2)}) collective-permute-start(bf16[32,896]{1,0:T(8,128)(2,1)S(1)} %added.11.q_part), channel_id=1, source_target_pairs={{0,8},{8,0},{16,24},{24,16},{32,40},{40,32},{48,56},{56,48},{64,72... | collective-permute-start | bytes 172040 | tf_op jit(solution)/shard_map/ppermute | solution.py:212
  56.7 6.1 %collective-permute-start.17 = (bf16[32,896]{1,0:T(8,128)(2,1)S(1)}, bf16[32,896]{1,0:T(8,128)(2,1)S(1)}, u32[]{:S(2)}, u32[]{:S(2)}) collective-permute-start(bf16[32,896]{1,0:T(8,128)(2,1)S(1)} %added.11.q_part), channel_id=1, source_target_pairs={{0,24},{8,16},{16,8},{24,0},{32,56},{40,48},{48,40},{56,32},{64,88... | collective-permute-start | bytes 172040 | tf_op jit(solution)/shard_map/ppermute | solution.py:212

commit v8 on v7

--- a/solution.py
+++ b/solution.py
@@ -13,7 +13,7 @@
 IN_VMEM = pl.BlockSpec(memory_space=pltpu.VMEM)
 IN_HBM = pl.BlockSpec(memory_space=pltpu.HBM)
 LANES = 128
-CHUNKS = 4
+CHUNKS = 8
 BLOCK = 16
 RING = 4
 FAR_FIRST = (2, 3, 1, 0)
@@ -142,52 +142,57 @@
     )(mine, other, matrix)
 
 
-def subtract_kernel(mean, distance, q_part, p_b, matrix, *refs):
-    new_errors, q_out, out_buf, q_buf, sems, q_sem = refs[-6:]
-    width = q_part.shape[1]
+def subtract_kernel(mean, distances, *refs):
+    q_parts, (p_b, matrix) = refs[: len(distances)], refs[len(distances) : len(distances) + 2]
+    new_errors, q_out, out_buf, q_buf, sems, q_sems = refs[-6:]
+    width = q_parts[0].shape[1]
     rows = matrix.shape[0]
     step = rows // CHUNKS
     position = lax.rem(lax.axis_index("dp"), RING)
-    cols = pl.ds(pl.multiple_of((position ^ distance) * width, LANES), width)
-    q_buf[...] = q_part[...].astype(F32) * mean
-    q_copy = pltpu.make_async_copy(q_buf, q_out.at[:, cols], q_sem)
-    q_copy.start()
-    q_b = q_buf[...].astype(BF16)
     left = p_b[...].T
     copies = []
-    for i in range(CHUNKS):
-        part = pl.ds(i * step, step)
-        approx = jnp.dot(left[i * step : (i + 1) * step], q_b, preferred_element_type=F32)
-        out_buf[part, :] = (matrix[part, cols].astype(F32) - approx).astype(BF16)
-        copies.append(pltpu.make_async_copy(out_buf.at[part], new_errors.at[0, part, cols], sems.at[i]))
+    for n, distance in enumerate(distances):
+        cols = pl.ds(pl.multiple_of((position ^ distance) * width, LANES), width)
+        q_buf[n] = q_parts[n][...].astype(F32) * mean
+        copies.append(pltpu.make_async_copy(q_buf.at[n], q_out.at[:, cols], q_sems.at[n]))
         copies[-1].start()
+        q_b = q_buf[n].astype(BF16)
+        for i in range(CHUNKS):
+            part = pl.ds(i * step, step)
+            approx = jnp.dot(left[i * step : (i + 1) * step], q_b, preferred_element_type=F32)
+            out_buf[n, part, :] = (matrix[part, cols].astype(F32) - approx).astype(BF16)
+            copies.append(
+                pltpu.make_async_copy(out_buf.at[n, part], new_errors.at[0, part, cols], sems.at[n, i])
+            )
+            copies[-1].start()
     for copy in copies:
         copy.wait()
-    q_copy.wait()
-
-
-def subtract(q_part, p_b, matrix, mean, distance, earlier):
+
+
+def subtract(q_parts, p_b, matrix, mean, distances, earlier):
     rows, cols = matrix.shape
-    rank, width = q_part.shape
-    return pl.pallas_call(
-        functools.partial(subtract_kernel, mean, distance),
+    rank, width = q_parts[0].shape
+    count = len(q_parts)
+    size = count * rows * width
+    return pl.pallas_call(
+        functools.partial(subtract_kernel, mean, distances),
         out_shape=(
             jax.ShapeDtypeStruct((1, rows, cols), BF16),
             jax.ShapeDtypeStruct((rank, cols), F32),
         ),
-        in_specs=[IN_VMEM] * 3 + [IN_HBM] * len(earlier),
+        in_specs=[IN_VMEM] * (count + 2) + [IN_HBM] * len(earlier),
         out_specs=(IN_HBM, IN_HBM),
         scratch_shapes=[
-            pltpu.VMEM((rows, width), BF16),
-            pltpu.VMEM((rank, width), F32),
-            pltpu.SemaphoreType.DMA((CHUNKS,)),
-            pltpu.SemaphoreType.DMA(()),
+            pltpu.VMEM((count, rows, width), BF16),
+            pltpu.VMEM((count, rank, width), F32),
+            pltpu.SemaphoreType.DMA((count, CHUNKS)),
+            pltpu.SemaphoreType.DMA((count,)),
         ],
-        input_output_aliases={3: 0, 4: 1} if earlier else {},
+        input_output_aliases={count + 2: 0, count + 3: 1} if earlier else {},
         compiler_params=pltpu.CompilerParams(vmem_limit_bytes=12 << 20),
-        cost_estimate=pl.CostEstimate(flops=2 * rows * width * rank, bytes_accessed=2 * rows * width, transcendentals=0),
+        cost_estimate=pl.CostEstimate(flops=2 * size * rank, bytes_accessed=2 * size, transcendentals=0),
         name="subtract",
-    )(q_part, p_b, matrix, *earlier)
+    )(*q_parts, p_b, matrix, *earlier)
 
 
 def added_kernel(*refs):
@@ -227,9 +232,9 @@
     one, three, two = (swapped(q_parts[distance], "dp", 1, distance) for distance in (1, 3, 2))
     q_sum = summed_over_four(added(two, three, one, q_parts[0]), "dp", 4)
     mean, earlier = 1.0 / lax.axis_size("dp"), ()
-    for distance in (0, 2, 1, 3):
-        q_part = swapped(q_sum, "dp", 1, distance) if distance else q_sum
-        earlier = subtract(q_part, p_b, matrix, mean, distance, earlier)
+    for distances in ((0,), (2,), (3, 1)):
+        q_now = [swapped(q_sum, "dp", 1, distance) if distance else q_sum for distance in distances]
+        earlier = subtract(q_now, p_b, matrix, mean, distances, earlier)
     new_errors, q_out = earlier
     return new_errors, p_own.T, q_out.T
 

time: 64.5 us -> 63.5 us (0.984)
  Pallas kernels: 14.5 us -> 13.5 us
    pallas_call x4 -> x3, Pallas kernels: 6.39 us -> 5.37 us  [subtract(): pl.pallas_call(functools.partial(subtract_kernel, mean, distances), out_s...]
    ppermute x20, waiting for transfers between devices: 22.9 us -> 23.5 us  [swapped(): lax.ppermute(value, axis, [(i, i ^ distance * stride) for i in range(lax....]
  transfers between devices with their start and end apart: 20 -> 20, of which waited for: 12 -> 13; matrix products, arithmetic and copies ran while one was open for 0% -> 0% of each run, Pallas kernels for 7% -> 5%
where the time goes in v8:
time: 63.5 us; the launch traced here: 63.3 us
  starting transfers between devices  24.5 us (39%)
  waiting for transfers between devices  23.5 us (37%)
  Pallas kernels  13.5 us (21%)
  local copies, waits for them, and re-layouts  1.01 us (2%)
  between operations  0.73 us (1%)
    ppermute x20, starting transfers between devices, swapped(): lax.ppermute(value, axis, [(i, i ^ distance * stride) for i in range(lax....  24.5 us
    ppermute x20, waiting for transfers between devices, swapped(): lax.ppermute(value, axis, [(i, i ^ distance * stride) for i in range(lax....  23.5 us
    pallas_call x1, Pallas kernels, merge(): pl.pallas_call(merge_kernel, out_shape=(jax.ShapeDtypeStruct((rows, cols)...  5.68 us
    pallas_call x3, Pallas kernels, subtract(): pl.pallas_call(functools.partial(subtract_kernel, mean, distances), out_s...  5.37 us
    pallas_call x1, Pallas kernels, project(): pl.pallas_call(project_kernel, out_shape=(jax.ShapeDtypeStruct((rank, LAN...  2.33 us
  transfers between devices with their start and end apart: 20, of which 13 were waited for; matrix products, arithmetic and copies ran while one was open for 0% of the time, Pallas kernels for 5%

profile of v8, /device:TPU:0, one launch (start us, length us, event | category | flops | bytes accessed | tf_op | source)
XLA Modules:
  0.0 63.3 jit_solution(9479939721813883403)
XLA Ops:
  1.6 5.7 %merge.1 = (bf16[1024,3584]{1,0:T(8,128)(2,1)S(1)}, f32[32,512]{1,0:T(8,128)S(1)}, f32[32,512]{1,0:T(8,128)S(1)}) custom-call(bf16[1,1024,3584]{2,1,0:T(8,128)(2,1)} %grads.1, bf16[1,1024,3584]{2,1,0:T(8,128)(2,1)} %errors.1, f32[32,3584]{1,0:T(8,128)S(1)} %bitcast.3), custom_call_target="tpu_custom_call" | custom-call | tf_op jit(solution)/shard_map/merge/pallas_call | solution.py:60
  7.4 1.2 %collective-permute-done.refs_1_ = f32[32,512]{1,0:T(8,128)S(1)} collective-permute-done((f32[32,512]{1,0:T(8,128)S(1)}, f32[32,512]{1,0:T(8,128)S(1)}, u32[]{:S(2)}, u32[]{:S(2)}) %collective-permute-start) | collective-permute-done | bytes 65568 | tf_op jit(solution)/shard_map/ppermute | solution.py:217
  8.7 3.2 %collective-permute-start.1 = (f32[32,512]{1,0:T(8,128)S(1)}, f32[32,512]{1,0:T(8,128)S(1)}, u32[]{:S(2)}, u32[]{:S(2)}) collective-permute-start(f32[32,512]{1,0:T(8,128)S(1)} %added.6.refs_3_), channel_id=1, source_target_pairs={{0,4},{1,5},{2,6},{3,7},{4,0},{5,1},{6,2},{7,3},{8,12},{9,13},{10,... | collective-permute-start | bytes 196616 | tf_op jit(solution)/shard_map/ppermute | solution.py:217
  11.9 1.1 %collective-permute-start.2 = (f32[32,512]{1,0:T(8,128)S(1)}, f32[32,512]{1,0:T(8,128)S(1)}, u32[]{:S(2)}, u32[]{:S(2)}) collective-permute-start(f32[32,512]{1,0:T(8,128)S(1)} %added.6.refs_3_), channel_id=1, source_target_pairs={{0,6},{1,7},{2,4},{3,5},{4,2},{5,3},{6,0},{7,1},{8,14},{9,15},{10,... | collective-permute-start | bytes 196616 | tf_op jit(solution)/shard_map/ppermute | solution.py:217
  13.0 1.5 %collective-permute-done.1.refs_0_ = f32[32,512]{1,0:T(8,128)S(1)} collective-permute-done((f32[32,512]{1,0:T(8,128)S(1)}, f32[32,512]{1,0:T(8,128)S(1)}, u32[]{:S(2)}, u32[]{:S(2)}) %collective-permute-start.1) | collective-permute-done | bytes 65568 | tf_op jit(solution)/shard_map/ppermute | solution.py:217
  14.5 2.8 %collective-permute-done.2.refs_1_ = f32[32,512]{1,0:T(8,128)S(1)} collective-permute-done((f32[32,512]{1,0:T(8,128)S(1)}, f32[32,512]{1,0:T(8,128)S(1)}, u32[]{:S(2)}, u32[]{:S(2)}) %collective-permute-start.2) | collective-permute-done | bytes 65568 | tf_op jit(solution)/shard_map/ppermute | solution.py:217
  17.4 3.3 %collective-permute-start.4 = (f32[32,512]{1,0:T(8,128)S(1)}, f32[32,512]{1,0:T(8,128)S(1)}, u32[]{:S(2)}, u32[]{:S(2)}) collective-permute-start(f32[32,512]{1,0:T(8,128)S(1)} %added.7.refs_3_), channel_id=1, source_target_pairs={{0,64},{8,72},{16,80},{24,88},{32,96},{40,104},{48,112},{56,120},{... | collective-permute-start | bytes 196616 | tf_op jit(solution)/shard_map/ppermute | solution.py:217
  21.7 1.5 %collective-permute-done.4.refs_0_ = f32[32,512]{1,0:T(8,128)S(1)} collective-permute-done((f32[32,512]{1,0:T(8,128)S(1)}, f32[32,512]{1,0:T(8,128)S(1)}, u32[]{:S(2)}, u32[]{:S(2)}) %collective-permute-start.4) | collective-permute-done | bytes 65568 | tf_op jit(solution)/shard_map/ppermute | solution.py:217
  23.3 2.9 %collective-permute-done.5.refs_1_ = f32[32,512]{1,0:T(8,128)S(1)} collective-permute-done((f32[32,512]{1,0:T(8,128)S(1)}, f32[32,512]{1,0:T(8,128)S(1)}, u32[]{:S(2)}, u32[]{:S(2)}) %collective-permute-start.5) | collective-permute-done | bytes 65568 | tf_op jit(solution)/shard_map/ppermute | solution.py:217
  26.1 4.0 %collective-permute-start.7 = (f32[32,512]{1,0:T(8,128)S(1)}, f32[32,512]{1,0:T(8,128)S(1)}, u32[]{:S(2)}, u32[]{:S(2)}) collective-permute-start(f32[32,512]{1,0:T(8,128)S(1)} %added.8.refs_3_), channel_id=1, source_target_pairs={{0,16},{8,24},{16,0},{24,8},{32,48},{40,56},{48,32},{56,40},{64,80... | collective-permute-start | bytes 196616 | tf_op jit(solution)/shard_map/ppermute | solution.py:217
  31.1 1.3 %collective-permute-done.7.refs_0_ = f32[32,512]{1,0:T(8,128)S(1)} collective-permute-done((f32[32,512]{1,0:T(8,128)S(1)}, f32[32,512]{1,0:T(8,128)S(1)}, u32[]{:S(2)}, u32[]{:S(2)}) %collective-permute-start.7) | collective-permute-done | bytes 65568 | tf_op jit(solution)/shard_map/ppermute | solution.py:217
  32.5 3.1 %collective-permute-done.8.refs_1_ = f32[32,512]{1,0:T(8,128)S(1)} collective-permute-done((f32[32,512]{1,0:T(8,128)S(1)}, f32[32,512]{1,0:T(8,128)S(1)}, u32[]{:S(2)}, u32[]{:S(2)}) %collective-permute-start.8) | collective-permute-done | bytes 65568 | tf_op jit(solution)/shard_map/ppermute | solution.py:217
  35.7 1.2 %collective-permute-done.10.other = f32[32,512]{1,0:T(8,128)S(1)} collective-permute-done((f32[32,512]{1,0:T(8,128)S(1)}, f32[32,512]{1,0:T(8,128)S(1)}, u32[]{:S(2)}, u32[]{:S(2)}) %collective-permute-start.10) | collective-permute-done | bytes 65568 | tf_op jit(solution)/shard_map/ppermute | solution.py:217
  36.9 2.3 %project.1 = (f32[32,128]{1,0:T(8,128)}, bf16[32,1024]{1,0:T(8,128)(2,1)S(1)}, bf16[32,896]{1,0:T(8,128)(2,1)S(1)}, bf16[32,896]{1,0:T(8,128)(2,1)S(1)}, bf16[32...) custom-call(f32[32,512]{1,0:T(8,128)S(1)} %added.9.mine, f32[32,512]{1,0:T(8,128)S(1)} %collective-permute-done.10.other, ...), custom_call_target="tpu_custom_call" | custom-call | tf_op jit(solution)/shard_map/project/pallas_call | solution.py:130
  39.3 1.9 %collective-permute-start.11 = (bf16[32,896]{1,0:T(8,128)(2,1)S(1)}, bf16[32,896]{1,0:T(8,128)(2,1)S(1)}, u32[]{:S(2)}, u32[]{:S(2)}) collective-permute-start(bf16[32,896]{1,0:T(8,128)(2,1)S(1)} %get-tuple-element.21), channel_id=1, source_target_pairs={{0,16},{8,24},{16,0},{24,8},{32,48},{40,56},{48,32},{56,40},{64,80... | collective-permute-start | bytes 172040 | tf_op jit(solution)/shard_map/ppermute | solution.py:217
  42.8 2.2 %collective-permute-done.11.refs_0_ = bf16[32,896]{1,0:T(8,128)(2,1)S(1)} collective-permute-done((bf16[32,896]{1,0:T(8,128)(2,1)S(1)}, bf16[32,896]{1,0:T(8,128)(2,1)S(1)}, u32[]{:S(2)}, u32[]{:S(2)}) %collective-permute-start.11) | collective-permute-done | bytes 57376 | tf_op jit(solution)/shard_map/ppermute | solution.py:217
  45.1 1.6 %collective-permute-done.12.refs_1_ = bf16[32,896]{1,0:T(8,128)(2,1)S(1)} collective-permute-done((bf16[32,896]{1,0:T(8,128)(2,1)S(1)}, bf16[32,896]{1,0:T(8,128)(2,1)S(1)}, u32[]{:S(2)}, u32[]{:S(2)}) %collective-permute-start.12) | collective-permute-done | bytes 57376 | tf_op jit(solution)/shard_map/ppermute | solution.py:217
  46.7 1.6 %collective-permute-start.14 = (bf16[32,896]{1,0:T(8,128)(2,1)S(1)}, bf16[32,896]{1,0:T(8,128)(2,1)S(1)}, u32[]{:S(2)}, u32[]{:S(2)}) collective-permute-start(bf16[32,896]{1,0:T(8,128)(2,1)S(1)} %added.10.refs_3_), channel_id=1, source_target_pairs={{0,64},{8,72},{16,80},{24,88},{32,96},{40,104},{48,112},{56,120},{... | collective-permute-start | bytes 172040 | tf_op jit(solution)/shard_map/ppermute | solution.py:217
  50.2 2.8 %collective-permute-done.14.refs_0_ = bf16[32,896]{1,0:T(8,128)(2,1)S(1)} collective-permute-done((bf16[32,896]{1,0:T(8,128)(2,1)S(1)}, bf16[32,896]{1,0:T(8,128)(2,1)S(1)}, u32[]{:S(2)}, u32[]{:S(2)}) %collective-permute-start.14) | collective-permute-done | bytes 57376 | tf_op jit(solution)/shard_map/ppermute | solution.py:217
  53.7 1.9 %collective-permute-start.19 = (bf16[32,896]{1,0:T(8,128)(2,1)S(1)}, bf16[32,896]{1,0:T(8,128)(2,1)S(1)}, u32[]{:S(2)}, u32[]{:S(2)}) collective-permute-start(bf16[32,896]{1,0:T(8,128)(2,1)S(1)} %added.11.refs_0_), channel_id=1, source_target_pairs={{0,16},{8,24},{16,0},{24,8},{32,48},{40,56},{48,32},{56,40},{64,80... | collective-permute-start | bytes 172040 | tf_op jit(solution)/shard_map/ppermute | solution.py:217
  55.6 1.2 %collective-permute-start.17 = (bf16[32,896]{1,0:T(8,128)(2,1)S(1)}, bf16[32,896]{1,0:T(8,128)(2,1)S(1)}, u32[]{:S(2)}, u32[]{:S(2)}) collective-permute-start(bf16[32,896]{1,0:T(8,128)(2,1)S(1)} %added.11.refs_0_), channel_id=1, source_target_pairs={{0,24},{8,16},{16,8},{24,0},{32,56},{40,48},{48,40},{56,32},{64,88... | collective-permute-start | bytes 172040 | tf_op jit(solution)/shard_map/ppermute | solution.py:217
  57.3 1.5 %subtract.3 = (bf16[1,1024,3584]{2,1,0:T(8,128)(2,1)}, f32[32,3584]{1,0:T(8,128)}) custom-call(bf16[32,896]{1,0:T(8,128)(2,1)S(1)} %added.11.refs_0_, bf16[32,1024]{1,0:T(8,128)(2,1)S(1)} %get-tuple-element.25.refs_1_.refs_2_, bf16[1024,3584]{1,0:T(8,128)(2,1)S(1)} %get-tuple-element.20.matrix.refs_2_.refs_3_), custom_call_target="tpu_custom_call" | custom-call | flops 58720256 | bytes 1835008 | tf_op jit(solution)/shard_map/subtract/pallas_call | solution.py:177
  59.5 1.6 %subtract.4 = (bf16[1,1024,3584]{2,1,0:T(8,128)(2,1)}, f32[32,3584]{1,0:T(8,128)}) custom-call(bf16[32,896]{1,0:T(8,128)(2,1)S(1)} %collective-permute-done.19.refs_0_, bf16[32,1024]{1,0:T(8,128)(2,1)S(1)} %get-tuple-element.25.refs_1_.refs_2_, ...), custom_call_target="tpu_custom_call", output_to_operand_aliasing={{0}: (3, {}), {1}: (4, {})} | custom-call | flops 58720256 | bytes 1835008 | tf_op jit(solution)/shard_map/subtract/pallas_call | solution.py:177
  61.0 2.3 %subtract.5 = (bf16[1,1024,3584]{2,1,0:T(8,128)(2,1)}, f32[32,3584]{1,0:T(8,128)}) custom-call(bf16[32,896]{1,0:T(8,128)(2,1)S(1)} %collective-permute-done.17.refs_0_, bf16[32,896]{1,0:T(8,128)(2,1)S(1)} %collective-permute-done.18.refs_1_, bf16[32,1024]{1,0:T(8,128)(2,1)S(1)} %get-tuple-element.25.refs_1_.refs_2_, ...), custom_call_target="tpu_custom_call", output_to_operand_aliasing={{0}: (4, {}), {1}: (5, {})} | custom-call | flops 117440512 | bytes 3670016 | tf_op jit(solution)/shard_map/subtract/pallas_call | solution.py:177
  (29 shorter events, 8.7 us)
Async XLA Ops:
  0.6 1.0 %copy-start = (f32[3584,32]{0,1:T(8,128)S(1)}, f32[3584,32]{0,1:T(8,128)}, u32[]{:S(2)}) copy-start(f32[3584,32]{0,1:T(8,128)} %param.5) | copy-start | bytes 1376260
  7.3 1.3 %collective-permute-start = (f32[32,512]{1,0:T(8,128)S(1)}, f32[32,512]{1,0:T(8,128)S(1)}, u32[]{:S(2)}, u32[]{:S(2)}) collective-permute-start(f32[32,512]{1,0:T(8,128)S(1)} %get-tuple-element.19), channel_id=1, source_target_pairs={{0,1},{1,0},{2,3},{3,2},{4,5},{5,4},{6,7},{7,6},{8,9},{9,8},{10,11... | collective-permute-start | bytes 196616 | tf_op jit(solution)/shard_map/ppermute | solution.py:217
  8.7 5.8 %collective-permute-start.1 = (f32[32,512]{1,0:T(8,128)S(1)}, f32[32,512]{1,0:T(8,128)S(1)}, u32[]{:S(2)}, u32[]{:S(2)}) collective-permute-start(f32[32,512]{1,0:T(8,128)S(1)} %added.6.refs_3_), channel_id=1, source_target_pairs={{0,4},{1,5},{2,6},{3,7},{4,0},{5,1},{6,2},{7,3},{8,12},{9,13},{10,... | collective-permute-start | bytes 196616 | tf_op jit(solution)/shard_map/ppermute | solution.py:217
  11.9 5.5 %collective-permute-start.2 = (f32[32,512]{1,0:T(8,128)S(1)}, f32[32,512]{1,0:T(8,128)S(1)}, u32[]{:S(2)}, u32[]{:S(2)}) collective-permute-start(f32[32,512]{1,0:T(8,128)S(1)} %added.6.refs_3_), channel_id=1, source_target_pairs={{0,6},{1,7},{2,4},{3,5},{4,2},{5,3},{6,0},{7,1},{8,14},{9,15},{10,... | collective-permute-start | bytes 196616 | tf_op jit(solution)/shard_map/ppermute | solution.py:217
  13.0 4.3 %collective-permute-start.3 = (f32[32,512]{1,0:T(8,128)S(1)}, f32[32,512]{1,0:T(8,128)S(1)}, u32[]{:S(2)}, u32[]{:S(2)}) collective-permute-start(f32[32,512]{1,0:T(8,128)S(1)} %added.6.refs_3_), channel_id=1, source_target_pairs={{0,2},{1,3},{2,0},{3,1},{4,6},{5,7},{6,4},{7,5},{8,10},{9,11},{10,... | collective-permute-start | bytes 196616 | tf_op jit(solution)/shard_map/ppermute | solution.py:217
  17.4 5.9 %collective-permute-start.4 = (f32[32,512]{1,0:T(8,128)S(1)}, f32[32,512]{1,0:T(8,128)S(1)}, u32[]{:S(2)}, u32[]{:S(2)}) collective-permute-start(f32[32,512]{1,0:T(8,128)S(1)} %added.7.refs_3_), channel_id=1, source_target_pairs={{0,64},{8,72},{16,80},{24,88},{32,96},{40,104},{48,112},{56,120},{... | collective-permute-start | bytes 196616 | tf_op jit(solution)/shard_map/ppermute | solution.py:217
  20.6 5.5 %collective-permute-start.5 = (f32[32,512]{1,0:T(8,128)S(1)}, f32[32,512]{1,0:T(8,128)S(1)}, u32[]{:S(2)}, u32[]{:S(2)}) collective-permute-start(f32[32,512]{1,0:T(8,128)S(1)} %added.7.refs_3_), channel_id=1, source_target_pairs={{0,96},{8,104},{16,112},{24,120},{32,64},{40,72},{48,80},{56,88},{... | collective-permute-start | bytes 196616 | tf_op jit(solution)/shard_map/ppermute | solution.py:217
  21.7 4.4 %collective-permute-start.6 = (f32[32,512]{1,0:T(8,128)S(1)}, f32[32,512]{1,0:T(8,128)S(1)}, u32[]{:S(2)}, u32[]{:S(2)}) collective-permute-start(f32[32,512]{1,0:T(8,128)S(1)} %added.7.refs_3_), channel_id=1, source_target_pairs={{0,32},{8,40},{16,48},{24,56},{32,0},{40,8},{48,16},{56,24},{64,96... | collective-permute-start | bytes 196616 | tf_op jit(solution)/shard_map/ppermute | solution.py:217
  26.1 6.3 %collective-permute-start.7 = (f32[32,512]{1,0:T(8,128)S(1)}, f32[32,512]{1,0:T(8,128)S(1)}, u32[]{:S(2)}, u32[]{:S(2)}) collective-permute-start(f32[32,512]{1,0:T(8,128)S(1)} %added.8.refs_3_), channel_id=1, source_target_pairs={{0,16},{8,24},{16,0},{24,8},{32,48},{40,56},{48,32},{56,40},{64,80... | collective-permute-start | bytes 196616 | tf_op jit(solution)/shard_map/ppermute | solution.py:217
  30.1 5.5 %collective-permute-start.8 = (f32[32,512]{1,0:T(8,128)S(1)}, f32[32,512]{1,0:T(8,128)S(1)}, u32[]{:S(2)}, u32[]{:S(2)}) collective-permute-start(f32[32,512]{1,0:T(8,128)S(1)} %added.8.refs_3_), channel_id=1, source_target_pairs={{0,24},{8,16},{16,8},{24,0},{32,56},{40,48},{48,40},{56,32},{64,88... | collective-permute-start | bytes 196616 | tf_op jit(solution)/shard_map/ppermute | solution.py:217
  30.8 4.8 %collective-permute-start.9 = (f32[32,512]{1,0:T(8,128)S(1)}, f32[32,512]{1,0:T(8,128)S(1)}, u32[]{:S(2)}, u32[]{:S(2)}) collective-permute-start(f32[32,512]{1,0:T(8,128)S(1)} %added.8.refs_3_), channel_id=1, source_target_pairs={{0,8},{8,0},{16,24},{24,16},{32,40},{40,32},{48,56},{56,48},{64,72... | collective-permute-start | bytes 196616 | tf_op jit(solution)/shard_map/ppermute | solution.py:217
  35.6 1.3 %collective-permute-start.10 = (f32[32,512]{1,0:T(8,128)S(1)}, f32[32,512]{1,0:T(8,128)S(1)}, u32[]{:S(2)}, u32[]{:S(2)}) collective-permute-start(f32[32,512]{1,0:T(8,128)S(1)} %added.9.mine), channel_id=1, source_target_pairs={{0,1},{1,0},{2,3},{3,2},{4,5},{5,4},{6,7},{7,6},{8,9},{9,8},{10,11... | collective-permute-start | bytes 196616 | tf_op jit(solution)/shard_map/ppermute | solution.py:217
  39.3 5.8 %collective-permute-start.11 = (bf16[32,896]{1,0:T(8,128)(2,1)S(1)}, bf16[32,896]{1,0:T(8,128)(2,1)S(1)}, u32[]{:S(2)}, u32[]{:S(2)}) collective-permute-start(bf16[32,896]{1,0:T(8,128)(2,1)S(1)} %get-tuple-element.21), channel_id=1, source_target_pairs={{0,16},{8,24},{16,0},{24,8},{32,48},{40,56},{48,32},{56,40},{64,80... | collective-permute-start | bytes 172040 | tf_op jit(solution)/shard_map/ppermute | solution.py:217
  41.2 5.4 %collective-permute-start.12 = (bf16[32,896]{1,0:T(8,128)(2,1)S(1)}, bf16[32,896]{1,0:T(8,128)(2,1)S(1)}, u32[]{:S(2)}, u32[]{:S(2)}) collective-permute-start(bf16[32,896]{1,0:T(8,128)(2,1)S(1)} %get-tuple-element.22), channel_id=1, source_target_pairs={{0,24},{8,16},{16,8},{24,0},{32,56},{40,48},{48,40},{56,32},{64,88... | collective-permute-start | bytes 172040 | tf_op jit(solution)/shard_map/ppermute | solution.py:217
  41.8 4.8 %collective-permute-start.13 = (bf16[32,896]{1,0:T(8,128)(2,1)S(1)}, bf16[32,896]{1,0:T(8,128)(2,1)S(1)}, u32[]{:S(2)}, u32[]{:S(2)}) collective-permute-start(bf16[32,896]{1,0:T(8,128)(2,1)S(1)} %get-tuple-element.23), channel_id=1, source_target_pairs={{0,8},{8,0},{16,24},{24,16},{32,40},{40,32},{48,56},{56,48},{64,72... | collective-permute-start | bytes 172040 | tf_op jit(solution)/shard_map/ppermute | solution.py:217
  46.7 6.3 %collective-permute-start.14 = (bf16[32,896]{1,0:T(8,128)(2,1)S(1)}, bf16[32,896]{1,0:T(8,128)(2,1)S(1)}, u32[]{:S(2)}, u32[]{:S(2)}) collective-permute-start(bf16[32,896]{1,0:T(8,128)(2,1)S(1)} %added.10.refs_3_), channel_id=1, source_target_pairs={{0,64},{8,72},{16,80},{24,88},{32,96},{40,104},{48,112},{56,120},{... | collective-permute-start | bytes 172040 | tf_op jit(solution)/shard_map/ppermute | solution.py:217
  48.3 5.4 %collective-permute-start.15 = (bf16[32,896]{1,0:T(8,128)(2,1)S(1)}, bf16[32,896]{1,0:T(8,128)(2,1)S(1)}, u32[]{:S(2)}, u32[]{:S(2)}) collective-permute-start(bf16[32,896]{1,0:T(8,128)(2,1)S(1)} %added.10.refs_3_), channel_id=1, source_target_pairs={{0,96},{8,104},{16,112},{24,120},{32,64},{40,72},{48,80},{56,88},{... | collective-permute-start | bytes 172040 | tf_op jit(solution)/shard_map/ppermute | solution.py:217
  49.2 4.4 %collective-permute-start.16 = (bf16[32,896]{1,0:T(8,128)(2,1)S(1)}, bf16[32,896]{1,0:T(8,128)(2,1)S(1)}, u32[]{:S(2)}, u32[]{:S(2)}) collective-permute-start(bf16[32,896]{1,0:T(8,128)(2,1)S(1)} %added.10.refs_3_), channel_id=1, source_target_pairs={{0,32},{8,40},{16,48},{24,56},{32,0},{40,8},{48,16},{56,24},{64,96... | collective-permute-start | bytes 172040 | tf_op jit(solution)/shard_map/ppermute | solution.py:217
  53.7 5.8 %collective-permute-start.19 = (bf16[32,896]{1,0:T(8,128)(2,1)S(1)}, bf16[32,896]{1,0:T(8,128)(2,1)S(1)}, u32[]{:S(2)}, u32[]{:S(2)}) collective-permute-start(bf16[32,896]{1,0:T(8,128)(2,1)S(1)} %added.11.refs_0_), channel_id=1, source_target_pairs={{0,16},{8,24},{16,0},{24,8},{32,48},{40,56},{48,32},{56,40},{64,80... | collective-permute-start | bytes 172040 | tf_op jit(solution)/shard_map/ppermute | solution.py:217
  55.6 5.4 %collective-permute-start.17 = (bf16[32,896]{1,0:T(8,128)(2,1)S(1)}, bf16[32,896]{1,0:T(8,128)(2,1)S(1)}, u32[]{:S(2)}, u32[]{:S(2)}) collective-permute-start(bf16[32,896]{1,0:T(8,128)(2,1)S(1)} %added.11.refs_0_), channel_id=1, source_target_pairs={{0,24},{8,16},{16,8},{24,0},{32,56},{40,48},{48,40},{56,32},{64,88... | collective-permute-start | bytes 172040 | tf_op jit(solution)/shard_map/ppermute | solution.py:217
  56.9 4.2 %collective-permute-start.18 = (bf16[32,896]{1,0:T(8,128)(2,1)S(1)}, bf16[32,896]{1,0:T(8,128)(2,1)S(1)}, u32[]{:S(2)}, u32[]{:S(2)}) collective-permute-start(bf16[32,896]{1,0:T(8,128)(2,1)S(1)} %added.11.refs_0_), channel_id=1, source_target_pairs={{0,8},{8,0},{16,24},{24,16},{32,40},{40,32},{48,56},{56,48},{64,72... | collective-permute-start | bytes 172040 | tf_op jit(solution)/shard_map/ppermute | solution.py:217

commit v9 on v8

--- a/solution.py
+++ b/solution.py
@@ -117,7 +117,7 @@
     rounded = jnp.dot(inverse, p_sum, precision=HIGHEST, preferred_element_type=F32).astype(BF16)
     p_b[...] = rounded
     width = q_parts[0].shape[1]
-    position = lax.rem(lax.axis_index("dp"), RING)
+    position = lax.div(lax.axis_index("dp"), RING)
     for distance in FAR_FIRST:
         cols = pl.ds(pl.multiple_of((position ^ distance) * width, LANES), width)
         product = jnp.dot(rounded, matrix[:, cols], preferred_element_type=F32)
@@ -148,7 +148,7 @@
     width = q_parts[0].shape[1]
     rows = matrix.shape[0]
     step = rows // CHUNKS
-    position = lax.rem(lax.axis_index("dp"), RING)
+    position = lax.div(lax.axis_index("dp"), RING)
     left = p_b[...].T
     copies = []
     for n, distance in enumerate(distances):
@@ -229,11 +229,11 @@
     mine = summed_over_four(mine, "dp", 4)
     mine = summed_over_four(mine, "dp", 1)
     p_own, p_b, *q_parts = project(mine, swapped(mine, "tensor", 1, 1), matrix)
-    one, three, two = (swapped(q_parts[distance], "dp", 1, distance) for distance in (1, 3, 2))
-    q_sum = summed_over_four(added(two, three, one, q_parts[0]), "dp", 4)
+    one, three, two = (swapped(q_parts[distance], "dp", RING, distance) for distance in (1, 3, 2))
+    q_sum = summed_over_four(added(two, three, one, q_parts[0]), "dp", 1)
     mean, earlier = 1.0 / lax.axis_size("dp"), ()
     for distances in ((0,), (2,), (3, 1)):
-        q_now = [swapped(q_sum, "dp", 1, distance) if distance else q_sum for distance in distances]
+        q_now = [swapped(q_sum, "dp", RING, distance) if distance else q_sum for distance in distances]
         earlier = subtract(q_now, p_b, matrix, mean, distances, earlier)
     new_errors, q_out = earlier
     return new_errors, p_own.T, q_out.T

time: 63.5 us -> 63.8 us (level)
  transfers between devices with their start and end apart: 20 -> 20, of which waited for: 13 -> 14; matrix products, arithmetic and copies ran while one was open for 0% -> 0% of each run, Pallas kernels for 5% -> 5%
where the time goes in v9:
time: 63.8 us; the launch traced here: 63.6 us
  starting transfers between devices  24.5 us (38%)
  waiting for transfers between devices  23.9 us (37%)
  Pallas kernels  13.5 us (21%)
  local copies, waits for them, and re-layouts  1.01 us (2%)
  between operations  0.73 us (1%)
    ppermute x20, starting transfers between devices, swapped(): lax.ppermute(value, axis, [(i, i ^ distance * stride) for i in range(lax....  24.5 us
    ppermute x20, waiting for transfers between devices, swapped(): lax.ppermute(value, axis, [(i, i ^ distance * stride) for i in range(lax....  23.9 us
    pallas_call x1, Pallas kernels, merge(): pl.pallas_call(merge_kernel, out_shape=(jax.ShapeDtypeStruct((rows, cols)...  5.68 us
    pallas_call x3, Pallas kernels, subtract(): pl.pallas_call(functools.partial(subtract_kernel, mean, distances), out_s...  5.37 us
    pallas_call x1, Pallas kernels, project(): pl.pallas_call(project_kernel, out_shape=(jax.ShapeDtypeStruct((rank, LAN...  2.33 us
  transfers between devices with their start and end apart: 20, of which 14 were waited for; matrix products, arithmetic and copies ran while one was open for 0% of the time, Pallas kernels for 5%

profile of v9, /device:TPU:0, one launch (start us, length us, event | category | flops | bytes accessed | tf_op | source)
XLA Modules:
  0.0 63.6 jit_solution(14168113974676187035)
XLA Ops:
  1.6 5.7 %merge.1 = (bf16[1024,3584]{1,0:T(8,128)(2,1)S(1)}, f32[32,512]{1,0:T(8,128)S(1)}, f32[32,512]{1,0:T(8,128)S(1)}) custom-call(bf16[1,1024,3584]{2,1,0:T(8,128)(2,1)} %grads.1, bf16[1,1024,3584]{2,1,0:T(8,128)(2,1)} %errors.1, f32[32,3584]{1,0:T(8,128)S(1)} %bitcast.3), custom_call_target="tpu_custom_call" | custom-call | tf_op jit(solution)/shard_map/merge/pallas_call | solution.py:60
  7.4 1.2 %collective-permute-done.refs_1_ = f32[32,512]{1,0:T(8,128)S(1)} collective-permute-done((f32[32,512]{1,0:T(8,128)S(1)}, f32[32,512]{1,0:T(8,128)S(1)}, u32[]{:S(2)}, u32[]{:S(2)}) %collective-permute-start) | collective-permute-done | bytes 65568 | tf_op jit(solution)/shard_map/ppermute | solution.py:217
  8.7 3.2 %collective-permute-start.1 = (f32[32,512]{1,0:T(8,128)S(1)}, f32[32,512]{1,0:T(8,128)S(1)}, u32[]{:S(2)}, u32[]{:S(2)}) collective-permute-start(f32[32,512]{1,0:T(8,128)S(1)} %added.6.refs_3_), channel_id=1, source_target_pairs={{0,4},{1,5},{2,6},{3,7},{4,0},{5,1},{6,2},{7,3},{8,12},{9,13},{10,... | collective-permute-start | bytes 196616 | tf_op jit(solution)/shard_map/ppermute | solution.py:217
  13.0 1.5 %collective-permute-done.1.refs_0_ = f32[32,512]{1,0:T(8,128)S(1)} collective-permute-done((f32[32,512]{1,0:T(8,128)S(1)}, f32[32,512]{1,0:T(8,128)S(1)}, u32[]{:S(2)}, u32[]{:S(2)}) %collective-permute-start.1) | collective-permute-done | bytes 65568 | tf_op jit(solution)/shard_map/ppermute | solution.py:217
  14.5 2.8 %collective-permute-done.2.refs_1_ = f32[32,512]{1,0:T(8,128)S(1)} collective-permute-done((f32[32,512]{1,0:T(8,128)S(1)}, f32[32,512]{1,0:T(8,128)S(1)}, u32[]{:S(2)}, u32[]{:S(2)}) %collective-permute-start.2) | collective-permute-done | bytes 65568 | tf_op jit(solution)/shard_map/ppermute | solution.py:217
  17.4 3.3 %collective-permute-start.4 = (f32[32,512]{1,0:T(8,128)S(1)}, f32[32,512]{1,0:T(8,128)S(1)}, u32[]{:S(2)}, u32[]{:S(2)}) collective-permute-start(f32[32,512]{1,0:T(8,128)S(1)} %added.7.refs_3_), channel_id=1, source_target_pairs={{0,64},{8,72},{16,80},{24,88},{32,96},{40,104},{48,112},{56,120},{... | collective-permute-start | bytes 196616 | tf_op jit(solution)/shard_map/ppermute | solution.py:217
  21.7 1.5 %collective-permute-done.4.refs_0_ = f32[32,512]{1,0:T(8,128)S(1)} collective-permute-done((f32[32,512]{1,0:T(8,128)S(1)}, f32[32,512]{1,0:T(8,128)S(1)}, u32[]{:S(2)}, u32[]{:S(2)}) %collective-permute-start.4) | collective-permute-done | bytes 65568 | tf_op jit(solution)/shard_map/ppermute | solution.py:217
  23.3 2.9 %collective-permute-done.5.refs_1_ = f32[32,512]{1,0:T(8,128)S(1)} collective-permute-done((f32[32,512]{1,0:T(8,128)S(1)}, f32[32,512]{1,0:T(8,128)S(1)}, u32[]{:S(2)}, u32[]{:S(2)}) %collective-permute-start.5) | collective-permute-done | bytes 65568 | tf_op jit(solution)/shard_map/ppermute | solution.py:217
  26.1 4.0 %collective-permute-start.7 = (f32[32,512]{1,0:T(8,128)S(1)}, f32[32,512]{1,0:T(8,128)S(1)}, u32[]{:S(2)}, u32[]{:S(2)}) collective-permute-start(f32[32,512]{1,0:T(8,128)S(1)} %added.8.refs_3_), channel_id=1, source_target_pairs={{0,16},{8,24},{16,0},{24,8},{32,48},{40,56},{48,32},{56,40},{64,80... | collective-permute-start | bytes 196616 | tf_op jit(solution)/shard_map/ppermute | solution.py:217
  31.1 1.3 %collective-permute-done.7.refs_0_ = f32[32,512]{1,0:T(8,128)S(1)} collective-permute-done((f32[32,512]{1,0:T(8,128)S(1)}, f32[32,512]{1,0:T(8,128)S(1)}, u32[]{:S(2)}, u32[]{:S(2)}) %collective-permute-start.7) | collective-permute-done | bytes 65568 | tf_op jit(solution)/shard_map/ppermute | solution.py:217
  32.5 3.1 %collective-permute-done.8.refs_1_ = f32[32,512]{1,0:T(8,128)S(1)} collective-permute-done((f32[32,512]{1,0:T(8,128)S(1)}, f32[32,512]{1,0:T(8,128)S(1)}, u32[]{:S(2)}, u32[]{:S(2)}) %collective-permute-start.8) | collective-permute-done | bytes 65568 | tf_op jit(solution)/shard_map/ppermute | solution.py:217
  35.7 1.2 %collective-permute-done.10.other = f32[32,512]{1,0:T(8,128)S(1)} collective-permute-done((f32[32,512]{1,0:T(8,128)S(1)}, f32[32,512]{1,0:T(8,128)S(1)}, u32[]{:S(2)}, u32[]{:S(2)}) %collective-permute-start.10) | collective-permute-done | bytes 65568 | tf_op jit(solution)/shard_map/ppermute | solution.py:217
  36.9 2.3 %project.1 = (f32[32,128]{1,0:T(8,128)}, bf16[32,1024]{1,0:T(8,128)(2,1)S(1)}, bf16[32,896]{1,0:T(8,128)(2,1)S(1)}, bf16[32,896]{1,0:T(8,128)(2,1)S(1)}, bf16[32...) custom-call(f32[32,512]{1,0:T(8,128)S(1)} %added.9.mine, f32[32,512]{1,0:T(8,128)S(1)} %collective-permute-done.10.other, ...), custom_call_target="tpu_custom_call" | custom-call | tf_op jit(solution)/shard_map/project/pallas_call | solution.py:130
  39.3 1.6 %collective-permute-start.11 = (bf16[32,896]{1,0:T(8,128)(2,1)S(1)}, bf16[32,896]{1,0:T(8,128)(2,1)S(1)}, u32[]{:S(2)}, u32[]{:S(2)}) collective-permute-start(bf16[32,896]{1,0:T(8,128)(2,1)S(1)} %get-tuple-element.21), channel_id=1, source_target_pairs={{0,64},{8,72},{16,80},{24,88},{32,96},{40,104},{48,112},{56,120},{... | collective-permute-start | bytes 172040 | tf_op jit(solution)/shard_map/ppermute | solution.py:217
  42.8 2.2 %collective-permute-done.11.refs_0_ = bf16[32,896]{1,0:T(8,128)(2,1)S(1)} collective-permute-done((bf16[32,896]{1,0:T(8,128)(2,1)S(1)}, bf16[32,896]{1,0:T(8,128)(2,1)S(1)}, u32[]{:S(2)}, u32[]{:S(2)}) %collective-permute-start.11) | collective-permute-done | bytes 57376 | tf_op jit(solution)/shard_map/ppermute | solution.py:217
  45.1 1.2 %collective-permute-done.12.refs_1_ = bf16[32,896]{1,0:T(8,128)(2,1)S(1)} collective-permute-done((bf16[32,896]{1,0:T(8,128)(2,1)S(1)}, bf16[32,896]{1,0:T(8,128)(2,1)S(1)}, u32[]{:S(2)}, u32[]{:S(2)}) %collective-permute-start.12) | collective-permute-done | bytes 57376 | tf_op jit(solution)/shard_map/ppermute | solution.py:217
  46.3 1.9 %collective-permute-start.14 = (bf16[32,896]{1,0:T(8,128)(2,1)S(1)}, bf16[32,896]{1,0:T(8,128)(2,1)S(1)}, u32[]{:S(2)}, u32[]{:S(2)}) collective-permute-start(bf16[32,896]{1,0:T(8,128)(2,1)S(1)} %added.10.refs_3_), channel_id=1, source_target_pairs={{0,16},{8,24},{16,0},{24,8},{32,48},{40,56},{48,32},{56,40},{64,80... | collective-permute-start | bytes 172040 | tf_op jit(solution)/shard_map/ppermute | solution.py:217
  49.9 2.3 %collective-permute-done.14.refs_0_ = bf16[32,896]{1,0:T(8,128)(2,1)S(1)} collective-permute-done((bf16[32,896]{1,0:T(8,128)(2,1)S(1)}, bf16[32,896]{1,0:T(8,128)(2,1)S(1)}, u32[]{:S(2)}, u32[]{:S(2)}) %collective-permute-start.14) | collective-permute-done | bytes 57376 | tf_op jit(solution)/shard_map/ppermute | solution.py:217
  52.2 1.5 %collective-permute-done.15.refs_1_ = bf16[32,896]{1,0:T(8,128)(2,1)S(1)} collective-permute-done((bf16[32,896]{1,0:T(8,128)(2,1)S(1)}, bf16[32,896]{1,0:T(8,128)(2,1)S(1)}, u32[]{:S(2)}, u32[]{:S(2)}) %collective-permute-start.15) | collective-permute-done | bytes 57376 | tf_op jit(solution)/shard_map/ppermute | solution.py:217
  53.7 2.3 %collective-permute-start.19 = (bf16[32,896]{1,0:T(8,128)(2,1)S(1)}, bf16[32,896]{1,0:T(8,128)(2,1)S(1)}, u32[]{:S(2)}, u32[]{:S(2)}) collective-permute-start(bf16[32,896]{1,0:T(8,128)(2,1)S(1)} %added.11.refs_0_), channel_id=1, source_target_pairs={{0,64},{8,72},{16,80},{24,88},{32,96},{40,104},{48,112},{56,120},{... | collective-permute-start | bytes 172040 | tf_op jit(solution)/shard_map/ppermute | solution.py:217
  56.0 1.2 %collective-permute-start.17 = (bf16[32,896]{1,0:T(8,128)(2,1)S(1)}, bf16[32,896]{1,0:T(8,128)(2,1)S(1)}, u32[]{:S(2)}, u32[]{:S(2)}) collective-permute-start(bf16[32,896]{1,0:T(8,128)(2,1)S(1)} %added.11.refs_0_), channel_id=1, source_target_pairs={{0,96},{8,104},{16,112},{24,120},{32,64},{40,72},{48,80},{56,88},{... | collective-permute-start | bytes 172040 | tf_op jit(solution)/shard_map/ppermute | solution.py:217
  57.3 1.5 %subtract.3 = (bf16[1,1024,3584]{2,1,0:T(8,128)(2,1)}, f32[32,3584]{1,0:T(8,128)}) custom-call(bf16[32,896]{1,0:T(8,128)(2,1)S(1)} %added.11.refs_0_, bf16[32,1024]{1,0:T(8,128)(2,1)S(1)} %get-tuple-element.25.refs_1_.refs_2_, bf16[1024,3584]{1,0:T(8,128)(2,1)S(1)} %get-tuple-element.20.matrix.refs_2_.refs_3_), custom_call_target="tpu_custom_call" | custom-call | flops 58720256 | bytes 1835008 | tf_op jit(solution)/shard_map/subtract/pallas_call | solution.py:177
  59.5 1.5 %subtract.4 = (bf16[1,1024,3584]{2,1,0:T(8,128)(2,1)}, f32[32,3584]{1,0:T(8,128)}) custom-call(bf16[32,896]{1,0:T(8,128)(2,1)S(1)} %collective-permute-done.19.refs_0_, bf16[32,1024]{1,0:T(8,128)(2,1)S(1)} %get-tuple-element.25.refs_1_.refs_2_, ...), custom_call_target="tpu_custom_call", output_to_operand_aliasing={{0}: (3, {}), {1}: (4, {})} | custom-call | flops 58720256 | bytes 1835008 | tf_op jit(solution)/shard_map/subtract/pallas_call | solution.py:177
  61.4 2.3 %subtract.5 = (bf16[1,1024,3584]{2,1,0:T(8,128)(2,1)}, f32[32,3584]{1,0:T(8,128)}) custom-call(bf16[32,896]{1,0:T(8,128)(2,1)S(1)} %collective-permute-done.17.refs_0_, bf16[32,896]{1,0:T(8,128)(2,1)S(1)} %collective-permute-done.18.refs_1_, bf16[32,1024]{1,0:T(8,128)(2,1)S(1)} %get-tuple-element.25.refs_1_.refs_2_, ...), custom_call_target="tpu_custom_call", output_to_operand_aliasing={{0}: (4, {}), {1}: (5, {})} | custom-call | flops 117440512 | bytes 3670016 | tf_op jit(solution)/shard_map/subtract/pallas_call | solution.py:177
  (29 shorter events, 9.2 us)
Async XLA Ops:
  0.6 1.0 %copy-start = (f32[3584,32]{0,1:T(8,128)S(1)}, f32[3584,32]{0,1:T(8,128)}, u32[]{:S(2)}) copy-start(f32[3584,32]{0,1:T(8,128)} %param.5) | copy-start | bytes 1376260
  7.3 1.3 %collective-permute-start = (f32[32,512]{1,0:T(8,128)S(1)}, f32[32,512]{1,0:T(8,128)S(1)}, u32[]{:S(2)}, u32[]{:S(2)}) collective-permute-start(f32[32,512]{1,0:T(8,128)S(1)} %get-tuple-element.19), channel_id=1, source_target_pairs={{0,1},{1,0},{2,3},{3,2},{4,5},{5,4},{6,7},{7,6},{8,9},{9,8},{10,11... | collective-permute-start | bytes 196616 | tf_op jit(solution)/shard_map/ppermute | solution.py:217
  8.7 5.8 %collective-permute-start.1 = (f32[32,512]{1,0:T(8,128)S(1)}, f32[32,512]{1,0:T(8,128)S(1)}, u32[]{:S(2)}, u32[]{:S(2)}) collective-permute-start(f32[32,512]{1,0:T(8,128)S(1)} %added.6.refs_3_), channel_id=1, source_target_pairs={{0,4},{1,5},{2,6},{3,7},{4,0},{5,1},{6,2},{7,3},{8,12},{9,13},{10,... | collective-permute-start | bytes 196616 | tf_op jit(solution)/shard_map/ppermute | solution.py:217
  11.9 5.5 %collective-permute-start.2 = (f32[32,512]{1,0:T(8,128)S(1)}, f32[32,512]{1,0:T(8,128)S(1)}, u32[]{:S(2)}, u32[]{:S(2)}) collective-permute-start(f32[32,512]{1,0:T(8,128)S(1)} %added.6.refs_3_), channel_id=1, source_target_pairs={{0,6},{1,7},{2,4},{3,5},{4,2},{5,3},{6,0},{7,1},{8,14},{9,15},{10,... | collective-permute-start | bytes 196616 | tf_op jit(solution)/shard_map/ppermute | solution.py:217
  13.0 4.3 %collective-permute-start.3 = (f32[32,512]{1,0:T(8,128)S(1)}, f32[32,512]{1,0:T(8,128)S(1)}, u32[]{:S(2)}, u32[]{:S(2)}) collective-permute-start(f32[32,512]{1,0:T(8,128)S(1)} %added.6.refs_3_), channel_id=1, source_target_pairs={{0,2},{1,3},{2,0},{3,1},{4,6},{5,7},{6,4},{7,5},{8,10},{9,11},{10,... | collective-permute-start | bytes 196616 | tf_op jit(solution)/shard_map/ppermute | solution.py:217
  17.4 5.9 %collective-permute-start.4 = (f32[32,512]{1,0:T(8,128)S(1)}, f32[32,512]{1,0:T(8,128)S(1)}, u32[]{:S(2)}, u32[]{:S(2)}) collective-permute-start(f32[32,512]{1,0:T(8,128)S(1)} %added.7.refs_3_), channel_id=1, source_target_pairs={{0,64},{8,72},{16,80},{24,88},{32,96},{40,104},{48,112},{56,120},{... | collective-permute-start | bytes 196616 | tf_op jit(solution)/shard_map/ppermute | solution.py:217
  20.6 5.5 %collective-permute-start.5 = (f32[32,512]{1,0:T(8,128)S(1)}, f32[32,512]{1,0:T(8,128)S(1)}, u32[]{:S(2)}, u32[]{:S(2)}) collective-permute-start(f32[32,512]{1,0:T(8,128)S(1)} %added.7.refs_3_), channel_id=1, source_target_pairs={{0,96},{8,104},{16,112},{24,120},{32,64},{40,72},{48,80},{56,88},{... | collective-permute-start | bytes 196616 | tf_op jit(solution)/shard_map/ppermute | solution.py:217
  21.7 4.4 %collective-permute-start.6 = (f32[32,512]{1,0:T(8,128)S(1)}, f32[32,512]{1,0:T(8,128)S(1)}, u32[]{:S(2)}, u32[]{:S(2)}) collective-permute-start(f32[32,512]{1,0:T(8,128)S(1)} %added.7.refs_3_), channel_id=1, source_target_pairs={{0,32},{8,40},{16,48},{24,56},{32,0},{40,8},{48,16},{56,24},{64,96... | collective-permute-start | bytes 196616 | tf_op jit(solution)/shard_map/ppermute | solution.py:217
  26.1 6.3 %collective-permute-start.7 = (f32[32,512]{1,0:T(8,128)S(1)}, f32[32,512]{1,0:T(8,128)S(1)}, u32[]{:S(2)}, u32[]{:S(2)}) collective-permute-start(f32[32,512]{1,0:T(8,128)S(1)} %added.8.refs_3_), channel_id=1, source_target_pairs={{0,16},{8,24},{16,0},{24,8},{32,48},{40,56},{48,32},{56,40},{64,80... | collective-permute-start | bytes 196616 | tf_op jit(solution)/shard_map/ppermute | solution.py:217
  30.1 5.5 %collective-permute-start.8 = (f32[32,512]{1,0:T(8,128)S(1)}, f32[32,512]{1,0:T(8,128)S(1)}, u32[]{:S(2)}, u32[]{:S(2)}) collective-permute-start(f32[32,512]{1,0:T(8,128)S(1)} %added.8.refs_3_), channel_id=1, source_target_pairs={{0,24},{8,16},{16,8},{24,0},{32,56},{40,48},{48,40},{56,32},{64,88... | collective-permute-start | bytes 196616 | tf_op jit(solution)/shard_map/ppermute | solution.py:217
  30.8 4.8 %collective-permute-start.9 = (f32[32,512]{1,0:T(8,128)S(1)}, f32[32,512]{1,0:T(8,128)S(1)}, u32[]{:S(2)}, u32[]{:S(2)}) collective-permute-start(f32[32,512]{1,0:T(8,128)S(1)} %added.8.refs_3_), channel_id=1, source_target_pairs={{0,8},{8,0},{16,24},{24,16},{32,40},{40,32},{48,56},{56,48},{64,72... | collective-permute-start | bytes 196616 | tf_op jit(solution)/shard_map/ppermute | solution.py:217
  35.6 1.3 %collective-permute-start.10 = (f32[32,512]{1,0:T(8,128)S(1)}, f32[32,512]{1,0:T(8,128)S(1)}, u32[]{:S(2)}, u32[]{:S(2)}) collective-permute-start(f32[32,512]{1,0:T(8,128)S(1)} %added.9.mine), channel_id=1, source_target_pairs={{0,1},{1,0},{2,3},{3,2},{4,5},{5,4},{6,7},{7,6},{8,9},{9,8},{10,11... | collective-permute-start | bytes 196616 | tf_op jit(solution)/shard_map/ppermute | solution.py:217
  39.3 5.8 %collective-permute-start.11 = (bf16[32,896]{1,0:T(8,128)(2,1)S(1)}, bf16[32,896]{1,0:T(8,128)(2,1)S(1)}, u32[]{:S(2)}, u32[]{:S(2)}) collective-permute-start(bf16[32,896]{1,0:T(8,128)(2,1)S(1)} %get-tuple-element.21), channel_id=1, source_target_pairs={{0,64},{8,72},{16,80},{24,88},{32,96},{40,104},{48,112},{56,120},{... | collective-permute-start | bytes 172040 | tf_op jit(solution)/shard_map/ppermute | solution.py:217
  40.9 5.4 %collective-permute-start.12 = (bf16[32,896]{1,0:T(8,128)(2,1)S(1)}, bf16[32,896]{1,0:T(8,128)(2,1)S(1)}, u32[]{:S(2)}, u32[]{:S(2)}) collective-permute-start(bf16[32,896]{1,0:T(8,128)(2,1)S(1)} %get-tuple-element.22), channel_id=1, source_target_pairs={{0,96},{8,104},{16,112},{24,120},{32,64},{40,72},{48,80},{56,88},{... | collective-permute-start | bytes 172040 | tf_op jit(solution)/shard_map/ppermute | solution.py:217
  41.9 4.4 %collective-permute-start.13 = (bf16[32,896]{1,0:T(8,128)(2,1)S(1)}, bf16[32,896]{1,0:T(8,128)(2,1)S(1)}, u32[]{:S(2)}, u32[]{:S(2)}) collective-permute-start(bf16[32,896]{1,0:T(8,128)(2,1)S(1)} %get-tuple-element.23), channel_id=1, source_target_pairs={{0,32},{8,40},{16,48},{24,56},{32,0},{40,8},{48,16},{56,24},{64,96... | collective-permute-start | bytes 172040 | tf_op jit(solution)/shard_map/ppermute | solution.py:217
  46.3 5.9 %collective-permute-start.14 = (bf16[32,896]{1,0:T(8,128)(2,1)S(1)}, bf16[32,896]{1,0:T(8,128)(2,1)S(1)}, u32[]{:S(2)}, u32[]{:S(2)}) collective-permute-start(bf16[32,896]{1,0:T(8,128)(2,1)S(1)} %added.10.refs_3_), channel_id=1, source_target_pairs={{0,16},{8,24},{16,0},{24,8},{32,48},{40,56},{48,32},{56,40},{64,80... | collective-permute-start | bytes 172040 | tf_op jit(solution)/shard_map/ppermute | solution.py:217
  48.3 5.4 %collective-permute-start.15 = (bf16[32,896]{1,0:T(8,128)(2,1)S(1)}, bf16[32,896]{1,0:T(8,128)(2,1)S(1)}, u32[]{:S(2)}, u32[]{:S(2)}) collective-permute-start(bf16[32,896]{1,0:T(8,128)(2,1)S(1)} %added.10.refs_3_), channel_id=1, source_target_pairs={{0,24},{8,16},{16,8},{24,0},{32,56},{40,48},{48,40},{56,32},{64,88... | collective-permute-start | bytes 172040 | tf_op jit(solution)/shard_map/ppermute | solution.py:217
  48.9 4.8 %collective-permute-start.16 = (bf16[32,896]{1,0:T(8,128)(2,1)S(1)}, bf16[32,896]{1,0:T(8,128)(2,1)S(1)}, u32[]{:S(2)}, u32[]{:S(2)}) collective-permute-start(bf16[32,896]{1,0:T(8,128)(2,1)S(1)} %added.10.refs_3_), channel_id=1, source_target_pairs={{0,8},{8,0},{16,24},{24,16},{32,40},{40,32},{48,56},{56,48},{64,72... | collective-permute-start | bytes 172040 | tf_op jit(solution)/shard_map/ppermute | solution.py:217
  53.7 5.8 %collective-permute-start.19 = (bf16[32,896]{1,0:T(8,128)(2,1)S(1)}, bf16[32,896]{1,0:T(8,128)(2,1)S(1)}, u32[]{:S(2)}, u32[]{:S(2)}) collective-permute-start(bf16[32,896]{1,0:T(8,128)(2,1)S(1)} %added.11.refs_0_), channel_id=1, source_target_pairs={{0,64},{8,72},{16,80},{24,88},{32,96},{40,104},{48,112},{56,120},{... | collective-permute-start | bytes 172040 | tf_op jit(solution)/shard_map/ppermute | solution.py:217
  56.0 5.4 %collective-permute-start.17 = (bf16[32,896]{1,0:T(8,128)(2,1)S(1)}, bf16[32,896]{1,0:T(8,128)(2,1)S(1)}, u32[]{:S(2)}, u32[]{:S(2)}) collective-permute-start(bf16[32,896]{1,0:T(8,128)(2,1)S(1)} %added.11.refs_0_), channel_id=1, source_target_pairs={{0,96},{8,104},{16,112},{24,120},{32,64},{40,72},{48,80},{56,88},{... | collective-permute-start | bytes 172040 | tf_op jit(solution)/shard_map/ppermute | solution.py:217
  57.2 4.2 %collective-permute-start.18 = (bf16[32,896]{1,0:T(8,128)(2,1)S(1)}, bf16[32,896]{1,0:T(8,128)(2,1)S(1)}, u32[]{:S(2)}, u32[]{:S(2)}) collective-permute-start(bf16[32,896]{1,0:T(8,128)(2,1)S(1)} %added.11.refs_0_), channel_id=1, source_target_pairs={{0,32},{8,40},{16,48},{24,56},{32,0},{40,8},{48,16},{56,24},{64,96... | collective-permute-start | bytes 172040 | tf_op jit(solution)/shard_map/ppermute | solution.py:217

commit v10 on v9

--- a/solution.py
+++ b/solution.py
@@ -16,6 +16,8 @@
 CHUNKS = 8
 BLOCK = 16
 RING = 4
+X, Z, Y = 2, 8, 32
+CORES = (1, 1)
 FAR_FIRST = (2, 3, 1, 0)
 WIDTHS = (768, 768, 768, 512, 512, 256)
 STARTS = tuple(sum(WIDTHS[:i]) for i in range(len(WIDTHS)))
@@ -23,6 +25,11 @@
 
 def on_first_core():
     return lax.rem(lax.axis_index("tensor"), 2) == 0
+
+
+def place_in_ring():
+    index = lax.axis_index("dp")
+    return jnp.where(on_first_core(), lax.rem(index, RING), lax.div(index, RING))
 
 
 def merge_kernel(grads, errors, basis_t, matrix, kept, sent, held, partial, grad_sems, error_sems):
@@ -117,7 +124,7 @@
     rounded = jnp.dot(inverse, p_sum, precision=HIGHEST, preferred_element_type=F32).astype(BF16)
     p_b[...] = rounded
     width = q_parts[0].shape[1]
-    position = lax.div(lax.axis_index("dp"), RING)
+    position = place_in_ring()
     for distance in FAR_FIRST:
         cols = pl.ds(pl.multiple_of((position ^ distance) * width, LANES), width)
         product = jnp.dot(rounded, matrix[:, cols], preferred_element_type=F32)
@@ -148,7 +155,7 @@
     width = q_parts[0].shape[1]
     rows = matrix.shape[0]
     step = rows // CHUNKS
-    position = lax.div(lax.axis_index("dp"), RING)
+    position = place_in_ring()
     left = p_b[...].T
     copies = []
     for n, distance in enumerate(distances):
@@ -213,27 +220,28 @@
     )(*terms)
 
 
-def swapped(value, axis, stride, distance):
-    return lax.ppermute(value, axis, [(i, i ^ (distance * stride)) for i in range(lax.axis_size(axis))])
-
-
-def summed_over_four(value, axis, stride):
-    one, three, two = (swapped(value, axis, stride, distance) for distance in (1, 3, 2))
-    return added(two, three, one, value)
+def swapped(value, strides, distance):
+    axes = ("dp", "tensor")
+    pairs = [(i, i ^ (distance * strides[i % 2])) for i in range(lax.axis_size(axes))]
+    return lax.ppermute(value, axes, pairs)
+
+
+def summed_over_four(values, strides):
+    two, three, one = (swapped(values[distance], strides, distance) for distance in (2, 3, 1))
+    return added(two, three, one, values[0])
 
 
 def on_device(grads, errors, basis):
     matrix, kept, sent = merge(grads, errors, basis.T)
-    mine = added(kept, swapped(sent, "tensor", 1, 1))
-    mine = summed_over_four(mine, "tensor", 2)
-    mine = summed_over_four(mine, "dp", 4)
-    mine = summed_over_four(mine, "dp", 1)
-    p_own, p_b, *q_parts = project(mine, swapped(mine, "tensor", 1, 1), matrix)
-    one, three, two = (swapped(q_parts[distance], "dp", RING, distance) for distance in (1, 3, 2))
-    q_sum = summed_over_four(added(two, three, one, q_parts[0]), "dp", 1)
+    mine = added(kept, swapped(sent, CORES, 1))
+    for strides in ((X, Y), (Y, Z), (Z, X)):
+        mine = summed_over_four([mine] * RING, strides)
+    p_own, p_b, *q_parts = project(mine, swapped(mine, CORES, 1), matrix)
+    q_sum = summed_over_four(q_parts, (Z, Y))
+    q_sum = summed_over_four([q_sum] * RING, (Y, Z))
     mean, earlier = 1.0 / lax.axis_size("dp"), ()
     for distances in ((0,), (2,), (3, 1)):
-        q_now = [swapped(q_sum, "dp", RING, distance) if distance else q_sum for distance in distances]
+        q_now = [swapped(q_sum, (Z, Y), distance) if distance else q_sum for distance in distances]
         earlier = subtract(q_now, p_b, matrix, mean, distances, earlier)
     new_errors, q_out = earlier
     return new_errors, p_own.T, q_out.T

time: 63.8 us -> 63.5 us (level)
  transfers between devices with their start and end apart: 20 -> 20, of which waited for: 14 -> 13; matrix products, arithmetic and copies ran while one was open for 0% -> 0% of each run, Pallas kernels for 5% -> 5%
where the time goes in v10:
time: 63.5 us; the launch traced here: 63.3 us
  starting transfers between devices  24.5 us (39%)
  waiting for transfers between devices  23.5 us (37%)
  Pallas kernels  13.5 us (21%)
  local copies, waits for them, and re-layouts  1.01 us (2%)
  between operations  0.73 us (1%)
    ppermute x20, starting transfers between devices, swapped(): return lax.ppermute(value, axes, pairs)  24.5 us
    ppermute x20, waiting for transfers between devices, swapped(): return lax.ppermute(value, axes, pairs)  23.5 us
    pallas_call x1, Pallas kernels, merge(): pl.pallas_call(merge_kernel, out_shape=(jax.ShapeDtypeStruct((rows, cols)...  5.68 us
    pallas_call x3, Pallas kernels, subtract(): pl.pallas_call(functools.partial(subtract_kernel, mean, distances), out_s...  5.37 us
    pallas_call x1, Pallas kernels, project(): pl.pallas_call(project_kernel, out_shape=(jax.ShapeDtypeStruct((rank, LAN...  2.33 us
  transfers between devices with their start and end apart: 20, of which 13 were waited for; matrix products, arithmetic and copies ran while one was open for 0% of the time, Pallas kernels for 5%

profile of v10, /device:TPU:0, one launch (start us, length us, event | category | flops | bytes accessed | tf_op | source)
XLA Modules:
  0.0 63.3 jit_solution(127889634715994160)
XLA Ops:
  1.6 5.7 %merge.1 = (bf16[1024,3584]{1,0:T(8,128)(2,1)S(1)}, f32[32,512]{1,0:T(8,128)S(1)}, f32[32,512]{1,0:T(8,128)S(1)}) custom-call(bf16[1,1024,3584]{2,1,0:T(8,128)(2,1)} %grads.1, bf16[1,1024,3584]{2,1,0:T(8,128)(2,1)} %errors.1, f32[32,3584]{1,0:T(8,128)S(1)} %bitcast.3), custom_call_target="tpu_custom_call" | custom-call | tf_op jit(solution)/shard_map/merge/pallas_call | solution.py:67
  7.4 1.2 %collective-permute-done.refs_1_ = f32[32,512]{1,0:T(8,128)S(1)} collective-permute-done((f32[32,512]{1,0:T(8,128)S(1)}, f32[32,512]{1,0:T(8,128)S(1)}, u32[]{:S(2)}, u32[]{:S(2)}) %collective-permute-start) | collective-permute-done | bytes 65568 | tf_op jit(solution)/shard_map/ppermute | solution.py:226
  8.7 3.2 %collective-permute-start.1 = (f32[32,512]{1,0:T(8,128)S(1)}, f32[32,512]{1,0:T(8,128)S(1)}, u32[]{:S(2)}, u32[]{:S(2)}) collective-permute-start(f32[32,512]{1,0:T(8,128)S(1)} %added.6.refs_3_), channel_id=1, source_target_pairs={{0,4},{1,65},{2,6},{3,67},{4,0},{5,69},{6,2},{7,71},{8,12},{9,73},... | collective-permute-start | bytes 196616 | tf_op jit(solution)/shard_map/ppermute | solution.py:226
  13.0 1.5 %collective-permute-done.1.refs_0_ = f32[32,512]{1,0:T(8,128)S(1)} collective-permute-done((f32[32,512]{1,0:T(8,128)S(1)}, f32[32,512]{1,0:T(8,128)S(1)}, u32[]{:S(2)}, u32[]{:S(2)}) %collective-permute-start.1) | collective-permute-done | bytes 65568 | tf_op jit(solution)/shard_map/ppermute | solution.py:226
  14.5 2.8 %collective-permute-done.2.refs_1_ = f32[32,512]{1,0:T(8,128)S(1)} collective-permute-done((f32[32,512]{1,0:T(8,128)S(1)}, f32[32,512]{1,0:T(8,128)S(1)}, u32[]{:S(2)}, u32[]{:S(2)}) %collective-permute-start.2) | collective-permute-done | bytes 65568 | tf_op jit(solution)/shard_map/ppermute | solution.py:226
  17.4 3.3 %collective-permute-start.4 = (f32[32,512]{1,0:T(8,128)S(1)}, f32[32,512]{1,0:T(8,128)S(1)}, u32[]{:S(2)}, u32[]{:S(2)}) collective-permute-start(f32[32,512]{1,0:T(8,128)S(1)} %added.7.refs_3_), channel_id=1, source_target_pairs={{0,64},{1,17},{2,66},{3,19},{4,68},{5,21},{6,70},{7,23},{8,72},{9,... | collective-permute-start | bytes 196616 | tf_op jit(solution)/shard_map/ppermute | solution.py:226
  21.7 1.5 %collective-permute-done.4.refs_0_ = f32[32,512]{1,0:T(8,128)S(1)} collective-permute-done((f32[32,512]{1,0:T(8,128)S(1)}, f32[32,512]{1,0:T(8,128)S(1)}, u32[]{:S(2)}, u32[]{:S(2)}) %collective-permute-start.4) | collective-permute-done | bytes 65568 | tf_op jit(solution)/shard_map/ppermute | solution.py:226
  23.2 2.9 %collective-permute-done.5.refs_1_ = f32[32,512]{1,0:T(8,128)S(1)} collective-permute-done((f32[32,512]{1,0:T(8,128)S(1)}, f32[32,512]{1,0:T(8,128)S(1)}, u32[]{:S(2)}, u32[]{:S(2)}) %collective-permute-start.5) | collective-permute-done | bytes 65568 | tf_op jit(solution)/shard_map/ppermute | solution.py:226
  26.1 4.0 %collective-permute-start.7 = (f32[32,512]{1,0:T(8,128)S(1)}, f32[32,512]{1,0:T(8,128)S(1)}, u32[]{:S(2)}, u32[]{:S(2)}) collective-permute-start(f32[32,512]{1,0:T(8,128)S(1)} %added.8.refs_3_), channel_id=1, source_target_pairs={{0,16},{1,5},{2,18},{3,7},{4,20},{5,1},{6,22},{7,3},{8,24},{9,13},... | collective-permute-start | bytes 196616 | tf_op jit(solution)/shard_map/ppermute | solution.py:226
  31.1 1.2 %collective-permute-done.7.refs_0_ = f32[32,512]{1,0:T(8,128)S(1)} collective-permute-done((f32[32,512]{1,0:T(8,128)S(1)}, f32[32,512]{1,0:T(8,128)S(1)}, u32[]{:S(2)}, u32[]{:S(2)}) %collective-permute-start.7) | collective-permute-done | bytes 65568 | tf_op jit(solution)/shard_map/ppermute | solution.py:226
  32.4 3.2 %collective-permute-done.8.refs_1_ = f32[32,512]{1,0:T(8,128)S(1)} collective-permute-done((f32[32,512]{1,0:T(8,128)S(1)}, f32[32,512]{1,0:T(8,128)S(1)}, u32[]{:S(2)}, u32[]{:S(2)}) %collective-permute-start.8) | collective-permute-done | bytes 65568 | tf_op jit(solution)/shard_map/ppermute | solution.py:226
  35.7 1.2 %collective-permute-done.10.other = f32[32,512]{1,0:T(8,128)S(1)} collective-permute-done((f32[32,512]{1,0:T(8,128)S(1)}, f32[32,512]{1,0:T(8,128)S(1)}, u32[]{:S(2)}, u32[]{:S(2)}) %collective-permute-start.10) | collective-permute-done | bytes 65568 | tf_op jit(solution)/shard_map/ppermute | solution.py:226
  36.9 2.3 %project.1 = (f32[32,128]{1,0:T(8,128)}, bf16[32,1024]{1,0:T(8,128)(2,1)S(1)}, bf16[32,896]{1,0:T(8,128)(2,1)S(1)}, bf16[32,896]{1,0:T(8,128)(2,1)S(1)}, bf16[32...) custom-call(f32[32,512]{1,0:T(8,128)S(1)} %added.9.mine, f32[32,512]{1,0:T(8,128)S(1)} %collective-permute-done.10.other, ...), custom_call_target="tpu_custom_call" | custom-call | tf_op jit(solution)/shard_map/project/pallas_call | solution.py:137
  39.3 1.9 %collective-permute-start.11 = (bf16[32,896]{1,0:T(8,128)(2,1)S(1)}, bf16[32,896]{1,0:T(8,128)(2,1)S(1)}, u32[]{:S(2)}, u32[]{:S(2)}) collective-permute-start(bf16[32,896]{1,0:T(8,128)(2,1)S(1)} %get-tuple-element.21), channel_id=1, source_target_pairs={{0,16},{1,65},{2,18},{3,67},{4,20},{5,69},{6,22},{7,71},{8,24},{9,... | collective-permute-start | bytes 172040 | tf_op jit(solution)/shard_map/ppermute | solution.py:226
  42.8 2.2 %collective-permute-done.11.refs_0_ = bf16[32,896]{1,0:T(8,128)(2,1)S(1)} collective-permute-done((bf16[32,896]{1,0:T(8,128)(2,1)S(1)}, bf16[32,896]{1,0:T(8,128)(2,1)S(1)}, u32[]{:S(2)}, u32[]{:S(2)}) %collective-permute-start.11) | collective-permute-done | bytes 57376 | tf_op jit(solution)/shard_map/ppermute | solution.py:226
  45.0 1.6 %collective-permute-done.12.refs_1_ = bf16[32,896]{1,0:T(8,128)(2,1)S(1)} collective-permute-done((bf16[32,896]{1,0:T(8,128)(2,1)S(1)}, bf16[32,896]{1,0:T(8,128)(2,1)S(1)}, u32[]{:S(2)}, u32[]{:S(2)}) %collective-permute-start.12) | collective-permute-done | bytes 57376 | tf_op jit(solution)/shard_map/ppermute | solution.py:226
  46.7 1.6 %collective-permute-start.14 = (bf16[32,896]{1,0:T(8,128)(2,1)S(1)}, bf16[32,896]{1,0:T(8,128)(2,1)S(1)}, u32[]{:S(2)}, u32[]{:S(2)}) collective-permute-start(bf16[32,896]{1,0:T(8,128)(2,1)S(1)} %added.10.refs_3_), channel_id=1, source_target_pairs={{0,64},{1,17},{2,66},{3,19},{4,68},{5,21},{6,70},{7,23},{8,72},{9,... | collective-permute-start | bytes 172040 | tf_op jit(solution)/shard_map/ppermute | solution.py:226
  50.2 2.2 %collective-permute-done.14.refs_0_ = bf16[32,896]{1,0:T(8,128)(2,1)S(1)} collective-permute-done((bf16[32,896]{1,0:T(8,128)(2,1)S(1)}, bf16[32,896]{1,0:T(8,128)(2,1)S(1)}, u32[]{:S(2)}, u32[]{:S(2)}) %collective-permute-start.14) | collective-permute-done | bytes 57376 | tf_op jit(solution)/shard_map/ppermute | solution.py:226
  52.4 1.2 %collective-permute-done.15.refs_1_ = bf16[32,896]{1,0:T(8,128)(2,1)S(1)} collective-permute-done((bf16[32,896]{1,0:T(8,128)(2,1)S(1)}, bf16[32,896]{1,0:T(8,128)(2,1)S(1)}, u32[]{:S(2)}, u32[]{:S(2)}) %collective-permute-start.15) | collective-permute-done | bytes 57376 | tf_op jit(solution)/shard_map/ppermute | solution.py:226
  53.7 1.9 %collective-permute-start.19 = (bf16[32,896]{1,0:T(8,128)(2,1)S(1)}, bf16[32,896]{1,0:T(8,128)(2,1)S(1)}, u32[]{:S(2)}, u32[]{:S(2)}) collective-permute-start(bf16[32,896]{1,0:T(8,128)(2,1)S(1)} %added.11.refs_0_), channel_id=1, source_target_pairs={{0,16},{1,65},{2,18},{3,67},{4,20},{5,69},{6,22},{7,71},{8,24},{9,... | collective-permute-start | bytes 172040 | tf_op jit(solution)/shard_map/ppermute | solution.py:226
  55.6 1.2 %collective-permute-start.17 = (bf16[32,896]{1,0:T(8,128)(2,1)S(1)}, bf16[32,896]{1,0:T(8,128)(2,1)S(1)}, u32[]{:S(2)}, u32[]{:S(2)}) collective-permute-start(bf16[32,896]{1,0:T(8,128)(2,1)S(1)} %added.11.refs_0_), channel_id=1, source_target_pairs={{0,24},{1,97},{2,26},{3,99},{4,28},{5,101},{6,30},{7,103},{8,16},{... | collective-permute-start | bytes 172040 | tf_op jit(solution)/shard_map/ppermute | solution.py:226
  57.3 1.5 %subtract.3 = (bf16[1,1024,3584]{2,1,0:T(8,128)(2,1)}, f32[32,3584]{1,0:T(8,128)}) custom-call(bf16[32,896]{1,0:T(8,128)(2,1)S(1)} %added.11.refs_0_, bf16[32,1024]{1,0:T(8,128)(2,1)S(1)} %get-tuple-element.25.refs_1_.refs_2_, bf16[1024,3584]{1,0:T(8,128)(2,1)S(1)} %get-tuple-element.20.matrix.refs_2_.refs_3_), custom_call_target="tpu_custom_call" | custom-call | flops 58720256 | bytes 1835008 | tf_op jit(solution)/shard_map/subtract/pallas_call | solution.py:184
  59.5 1.6 %subtract.4 = (bf16[1,1024,3584]{2,1,0:T(8,128)(2,1)}, f32[32,3584]{1,0:T(8,128)}) custom-call(bf16[32,896]{1,0:T(8,128)(2,1)S(1)} %collective-permute-done.19.refs_0_, bf16[32,1024]{1,0:T(8,128)(2,1)S(1)} %get-tuple-element.25.refs_1_.refs_2_, ...), custom_call_target="tpu_custom_call", output_to_operand_aliasing={{0}: (3, {}), {1}: (4, {})} | custom-call | flops 58720256 | bytes 1835008 | tf_op jit(solution)/shard_map/subtract/pallas_call | solution.py:184
  61.0 2.3 %subtract.5 = (bf16[1,1024,3584]{2,1,0:T(8,128)(2,1)}, f32[32,3584]{1,0:T(8,128)}) custom-call(bf16[32,896]{1,0:T(8,128)(2,1)S(1)} %collective-permute-done.17.refs_0_, bf16[32,896]{1,0:T(8,128)(2,1)S(1)} %collective-permute-done.18.refs_1_, bf16[32,1024]{1,0:T(8,128)(2,1)S(1)} %get-tuple-element.25.refs_1_.refs_2_, ...), custom_call_target="tpu_custom_call", output_to_operand_aliasing={{0}: (4, {}), {1}: (5, {})} | custom-call | flops 117440512 | bytes 3670016 | tf_op jit(solution)/shard_map/subtract/pallas_call | solution.py:184
  (29 shorter events, 9.2 us)
Async XLA Ops:
  0.6 1.0 %copy-start = (f32[3584,32]{0,1:T(8,128)S(1)}, f32[3584,32]{0,1:T(8,128)}, u32[]{:S(2)}) copy-start(f32[3584,32]{0,1:T(8,128)} %param.5) | copy-start | bytes 1376260
  7.3 1.3 %collective-permute-start = (f32[32,512]{1,0:T(8,128)S(1)}, f32[32,512]{1,0:T(8,128)S(1)}, u32[]{:S(2)}, u32[]{:S(2)}) collective-permute-start(f32[32,512]{1,0:T(8,128)S(1)} %get-tuple-element.19), channel_id=1, source_target_pairs={{0,1},{1,0},{2,3},{3,2},{4,5},{5,4},{6,7},{7,6},{8,9},{9,8},{10,11... | collective-permute-start | bytes 196616 | tf_op jit(solution)/shard_map/ppermute | solution.py:226
  8.7 5.8 %collective-permute-start.1 = (f32[32,512]{1,0:T(8,128)S(1)}, f32[32,512]{1,0:T(8,128)S(1)}, u32[]{:S(2)}, u32[]{:S(2)}) collective-permute-start(f32[32,512]{1,0:T(8,128)S(1)} %added.6.refs_3_), channel_id=1, source_target_pairs={{0,4},{1,65},{2,6},{3,67},{4,0},{5,69},{6,2},{7,71},{8,12},{9,73},... | collective-permute-start | bytes 196616 | tf_op jit(solution)/shard_map/ppermute | solution.py:226
  11.9 5.5 %collective-permute-start.2 = (f32[32,512]{1,0:T(8,128)S(1)}, f32[32,512]{1,0:T(8,128)S(1)}, u32[]{:S(2)}, u32[]{:S(2)}) collective-permute-start(f32[32,512]{1,0:T(8,128)S(1)} %added.6.refs_3_), channel_id=1, source_target_pairs={{0,6},{1,97},{2,4},{3,99},{4,2},{5,101},{6,0},{7,103},{8,14},{9,10... | collective-permute-start | bytes 196616 | tf_op jit(solution)/shard_map/ppermute | solution.py:226
  13.0 4.3 %collective-permute-start.3 = (f32[32,512]{1,0:T(8,128)S(1)}, f32[32,512]{1,0:T(8,128)S(1)}, u32[]{:S(2)}, u32[]{:S(2)}) collective-permute-start(f32[32,512]{1,0:T(8,128)S(1)} %added.6.refs_3_), channel_id=1, source_target_pairs={{0,2},{1,33},{2,0},{3,35},{4,6},{5,37},{6,4},{7,39},{8,10},{9,41},... | collective-permute-start | bytes 196616 | tf_op jit(solution)/shard_map/ppermute | solution.py:226
  17.4 5.8 %collective-permute-start.4 = (f32[32,512]{1,0:T(8,128)S(1)}, f32[32,512]{1,0:T(8,128)S(1)}, u32[]{:S(2)}, u32[]{:S(2)}) collective-permute-start(f32[32,512]{1,0:T(8,128)S(1)} %added.7.refs_3_), channel_id=1, source_target_pairs={{0,64},{1,17},{2,66},{3,19},{4,68},{5,21},{6,70},{7,23},{8,72},{9,... | collective-permute-start | bytes 196616 | tf_op jit(solution)/shard_map/ppermute | solution.py:226
  20.6 5.5 %collective-permute-start.5 = (f32[32,512]{1,0:T(8,128)S(1)}, f32[32,512]{1,0:T(8,128)S(1)}, u32[]{:S(2)}, u32[]{:S(2)}) collective-permute-start(f32[32,512]{1,0:T(8,128)S(1)} %added.7.refs_3_), channel_id=1, source_target_pairs={{0,96},{1,25},{2,98},{3,27},{4,100},{5,29},{6,102},{7,31},{8,104},... | collective-permute-start | bytes 196616 | tf_op jit(solution)/shard_map/ppermute | solution.py:226
  21.7 4.4 %collective-permute-start.6 = (f32[32,512]{1,0:T(8,128)S(1)}, f32[32,512]{1,0:T(8,128)S(1)}, u32[]{:S(2)}, u32[]{:S(2)}) collective-permute-start(f32[32,512]{1,0:T(8,128)S(1)} %added.7.refs_3_), channel_id=1, source_target_pairs={{0,32},{1,9},{2,34},{3,11},{4,36},{5,13},{6,38},{7,15},{8,40},{9,1... | collective-permute-start | bytes 196616 | tf_op jit(solution)/shard_map/ppermute | solution.py:226
  26.1 6.2 %collective-permute-start.7 = (f32[32,512]{1,0:T(8,128)S(1)}, f32[32,512]{1,0:T(8,128)S(1)}, u32[]{:S(2)}, u32[]{:S(2)}) collective-permute-start(f32[32,512]{1,0:T(8,128)S(1)} %added.8.refs_3_), channel_id=1, source_target_pairs={{0,16},{1,5},{2,18},{3,7},{4,20},{5,1},{6,22},{7,3},{8,24},{9,13},... | collective-permute-start | bytes 196616 | tf_op jit(solution)/shard_map/ppermute | solution.py:226
  30.1 5.5 %collective-permute-start.8 = (f32[32,512]{1,0:T(8,128)S(1)}, f32[32,512]{1,0:T(8,128)S(1)}, u32[]{:S(2)}, u32[]{:S(2)}) collective-permute-start(f32[32,512]{1,0:T(8,128)S(1)} %added.8.refs_3_), channel_id=1, source_target_pairs={{0,24},{1,7},{2,26},{3,5},{4,28},{5,3},{6,30},{7,1},{8,16},{9,15},... | collective-permute-start | bytes 196616 | tf_op jit(solution)/shard_map/ppermute | solution.py:226
  30.8 4.8 %collective-permute-start.9 = (f32[32,512]{1,0:T(8,128)S(1)}, f32[32,512]{1,0:T(8,128)S(1)}, u32[]{:S(2)}, u32[]{:S(2)}) collective-permute-start(f32[32,512]{1,0:T(8,128)S(1)} %added.8.refs_3_), channel_id=1, source_target_pairs={{0,8},{1,3},{2,10},{3,1},{4,12},{5,7},{6,14},{7,5},{8,0},{9,11},{1... | collective-permute-start | bytes 196616 | tf_op jit(solution)/shard_map/ppermute | solution.py:226
  35.6 1.3 %collective-permute-start.10 = (f32[32,512]{1,0:T(8,128)S(1)}, f32[32,512]{1,0:T(8,128)S(1)}, u32[]{:S(2)}, u32[]{:S(2)}) collective-permute-start(f32[32,512]{1,0:T(8,128)S(1)} %added.9.mine), channel_id=1, source_target_pairs={{0,1},{1,0},{2,3},{3,2},{4,5},{5,4},{6,7},{7,6},{8,9},{9,8},{10,11... | collective-permute-start | bytes 196616 | tf_op jit(solution)/shard_map/ppermute | solution.py:226
  39.3 5.8 %collective-permute-start.11 = (bf16[32,896]{1,0:T(8,128)(2,1)S(1)}, bf16[32,896]{1,0:T(8,128)(2,1)S(1)}, u32[]{:S(2)}, u32[]{:S(2)}) collective-permute-start(bf16[32,896]{1,0:T(8,128)(2,1)S(1)} %get-tuple-element.21), channel_id=1, source_target_pairs={{0,16},{1,65},{2,18},{3,67},{4,20},{5,69},{6,22},{7,71},{8,24},{9,... | collective-permute-start | bytes 172040 | tf_op jit(solution)/shard_map/ppermute | solution.py:226
  41.2 5.4 %collective-permute-start.12 = (bf16[32,896]{1,0:T(8,128)(2,1)S(1)}, bf16[32,896]{1,0:T(8,128)(2,1)S(1)}, u32[]{:S(2)}, u32[]{:S(2)}) collective-permute-start(bf16[32,896]{1,0:T(8,128)(2,1)S(1)} %get-tuple-element.22), channel_id=1, source_target_pairs={{0,24},{1,97},{2,26},{3,99},{4,28},{5,101},{6,30},{7,103},{8,16},{... | collective-permute-start | bytes 172040 | tf_op jit(solution)/shard_map/ppermute | solution.py:226
  41.8 4.8 %collective-permute-start.13 = (bf16[32,896]{1,0:T(8,128)(2,1)S(1)}, bf16[32,896]{1,0:T(8,128)(2,1)S(1)}, u32[]{:S(2)}, u32[]{:S(2)}) collective-permute-start(bf16[32,896]{1,0:T(8,128)(2,1)S(1)} %get-tuple-element.23), channel_id=1, source_target_pairs={{0,8},{1,33},{2,10},{3,35},{4,12},{5,37},{6,14},{7,39},{8,0},{9,41... | collective-permute-start | bytes 172040 | tf_op jit(solution)/shard_map/ppermute | solution.py:226
  46.7 5.8 %collective-permute-start.14 = (bf16[32,896]{1,0:T(8,128)(2,1)S(1)}, bf16[32,896]{1,0:T(8,128)(2,1)S(1)}, u32[]{:S(2)}, u32[]{:S(2)}) collective-permute-start(bf16[32,896]{1,0:T(8,128)(2,1)S(1)} %added.10.refs_3_), channel_id=1, source_target_pairs={{0,64},{1,17},{2,66},{3,19},{4,68},{5,21},{6,70},{7,23},{8,72},{9,... | collective-permute-start | bytes 172040 | tf_op jit(solution)/shard_map/ppermute | solution.py:226
  48.3 5.4 %collective-permute-start.15 = (bf16[32,896]{1,0:T(8,128)(2,1)S(1)}, bf16[32,896]{1,0:T(8,128)(2,1)S(1)}, u32[]{:S(2)}, u32[]{:S(2)}) collective-permute-start(bf16[32,896]{1,0:T(8,128)(2,1)S(1)} %added.10.refs_3_), channel_id=1, source_target_pairs={{0,96},{1,25},{2,98},{3,27},{4,100},{5,29},{6,102},{7,31},{8,104},... | collective-permute-start | bytes 172040 | tf_op jit(solution)/shard_map/ppermute | solution.py:226
  49.2 4.4 %collective-permute-start.16 = (bf16[32,896]{1,0:T(8,128)(2,1)S(1)}, bf16[32,896]{1,0:T(8,128)(2,1)S(1)}, u32[]{:S(2)}, u32[]{:S(2)}) collective-permute-start(bf16[32,896]{1,0:T(8,128)(2,1)S(1)} %added.10.refs_3_), channel_id=1, source_target_pairs={{0,32},{1,9},{2,34},{3,11},{4,36},{5,13},{6,38},{7,15},{8,40},{9,1... | collective-permute-start | bytes 172040 | tf_op jit(solution)/shard_map/ppermute | solution.py:226
  53.7 5.8 %collective-permute-start.19 = (bf16[32,896]{1,0:T(8,128)(2,1)S(1)}, bf16[32,896]{1,0:T(8,128)(2,1)S(1)}, u32[]{:S(2)}, u32[]{:S(2)}) collective-permute-start(bf16[32,896]{1,0:T(8,128)(2,1)S(1)} %added.11.refs_0_), channel_id=1, source_target_pairs={{0,16},{1,65},{2,18},{3,67},{4,20},{5,69},{6,22},{7,71},{8,24},{9,... | collective-permute-start | bytes 172040 | tf_op jit(solution)/shard_map/ppermute | solution.py:226
  55.6 5.4 %collective-permute-start.17 = (bf16[32,896]{1,0:T(8,128)(2,1)S(1)}, bf16[32,896]{1,0:T(8,128)(2,1)S(1)}, u32[]{:S(2)}, u32[]{:S(2)}) collective-permute-start(bf16[32,896]{1,0:T(8,128)(2,1)S(1)} %added.11.refs_0_), channel_id=1, source_target_pairs={{0,24},{1,97},{2,26},{3,99},{4,28},{5,101},{6,30},{7,103},{8,16},{... | collective-permute-start | bytes 172040 | tf_op jit(solution)/shard_map/ppermute | solution.py:226
  56.9 4.2 %collective-permute-start.18 = (bf16[32,896]{1,0:T(8,128)(2,1)S(1)}, bf16[32,896]{1,0:T(8,128)(2,1)S(1)}, u32[]{:S(2)}, u32[]{:S(2)}) collective-permute-start(bf16[32,896]{1,0:T(8,128)(2,1)S(1)} %added.11.refs_0_), channel_id=1, source_target_pairs={{0,8},{1,33},{2,10},{3,35},{4,12},{5,37},{6,14},{7,39},{8,0},{9,41... | collective-permute-start | bytes 172040 | tf_op jit(solution)/shard_map/ppermute | solution.py:226

commit v11 on v8

--- a/solution.py
+++ b/solution.py
@@ -36,7 +36,7 @@
     for i in range(len(WIDTHS)):
         for copy in copies(i):
             copy.start()
-    basis_b = basis_t[...].astype(BF16)
+    basis_b = basis_t[...]
     half = kept.shape[1]
     first = on_first_core()
     for i in range(len(WIDTHS)):
@@ -223,7 +223,7 @@
 
 
 def on_device(grads, errors, basis):
-    matrix, kept, sent = merge(grads, errors, basis.T)
+    matrix, kept, sent = merge(grads, errors, basis.T.astype(BF16))
     mine = added(kept, swapped(sent, "tensor", 1, 1))
     mine = summed_over_four(mine, "tensor", 2)
     mine = summed_over_four(mine, "dp", 4)

time: 63.5 us -> 63.5 us (level)
  other arithmetic: 0 us -> 1.04 us
  local copies, waits for them, and re-layouts: 1.01 us -> 0 us
    convert_element_type x0 -> x1, other arithmetic: none -> 1.04 us  [on_device(): matrix, kept, sent = merge(grads, errors, basis.T.astype(BF16))]
    unnamed x2 -> x0, local copies, waits for them, and re-layouts: 1.01 us -> none
where the time goes in v11:
time: 63.5 us; the launch traced here: 63.3 us
  starting transfers between devices  24.5 us (39%)
  waiting for transfers between devices  23.5 us (37%)
  Pallas kernels  13.5 us (21%)
  other arithmetic  1.04 us (2%)
  between operations  0.73 us (1%)
    ppermute x20, starting transfers between devices, swapped(): lax.ppermute(value, axis, [(i, i ^ distance * stride) for i in range(lax....  24.5 us
    ppermute x20, waiting for transfers between devices, swapped(): lax.ppermute(value, axis, [(i, i ^ distance * stride) for i in range(lax....  23.5 us
    pallas_call x1, Pallas kernels, merge(): pl.pallas_call(merge_kernel, out_shape=(jax.ShapeDtypeStruct((rows, cols)...  5.69 us
    pallas_call x3, Pallas kernels, subtract(): pl.pallas_call(functools.partial(subtract_kernel, mean, distances), out_s...  5.37 us
    pallas_call x1, Pallas kernels, project(): pl.pallas_call(project_kernel, out_shape=(jax.ShapeDtypeStruct((rank, LAN...  2.33 us
  transfers between devices with their start and end apart: 20, of which 13 were waited for; matrix products, arithmetic and copies ran while one was open for 0% of the time, Pallas kernels for 5%

profile of v11, /device:TPU:0, one launch (start us, length us, event | category | flops | bytes accessed | tf_op | source)
XLA Modules:
  0.0 63.3 jit_solution(16416021370404858511)
XLA Ops:
  1.7 5.7 %merge.1 = (bf16[1024,3584]{1,0:T(8,128)(2,1)S(1)}, f32[32,512]{1,0:T(8,128)S(1)}, f32[32,512]{1,0:T(8,128)S(1)}) custom-call(bf16[1,1024,3584]{2,1,0:T(8,128)(2,1)} %grads.1, bf16[1,1024,3584]{2,1,0:T(8,128)(2,1)} %errors.1, bf16[32,3584]{1,0:T(8,128)(2,1)S(1)} %convert_bitcast_fusion.basis_t), custom_call_target="tpu_custom_call" | custom-call | tf_op jit(solution)/shard_map/merge/pallas_call | solution.py:60
  7.5 1.2 %collective-permute-done.refs_1_ = f32[32,512]{1,0:T(8,128)S(1)} collective-permute-done((f32[32,512]{1,0:T(8,128)S(1)}, f32[32,512]{1,0:T(8,128)S(1)}, u32[]{:S(2)}, u32[]{:S(2)}) %collective-permute-start) | collective-permute-done | bytes 65568 | tf_op jit(solution)/shard_map/ppermute | solution.py:217
  8.7 3.2 %collective-permute-start.1 = (f32[32,512]{1,0:T(8,128)S(1)}, f32[32,512]{1,0:T(8,128)S(1)}, u32[]{:S(2)}, u32[]{:S(2)}) collective-permute-start(f32[32,512]{1,0:T(8,128)S(1)} %added.6.refs_3_), channel_id=1, source_target_pairs={{0,4},{1,5},{2,6},{3,7},{4,0},{5,1},{6,2},{7,3},{8,12},{9,13},{10,... | collective-permute-start | bytes 196616 | tf_op jit(solution)/shard_map/ppermute | solution.py:217
  11.9 1.1 %collective-permute-start.2 = (f32[32,512]{1,0:T(8,128)S(1)}, f32[32,512]{1,0:T(8,128)S(1)}, u32[]{:S(2)}, u32[]{:S(2)}) collective-permute-start(f32[32,512]{1,0:T(8,128)S(1)} %added.6.refs_3_), channel_id=1, source_target_pairs={{0,6},{1,7},{2,4},{3,5},{4,2},{5,3},{6,0},{7,1},{8,14},{9,15},{10,... | collective-permute-start | bytes 196616 | tf_op jit(solution)/shard_map/ppermute | solution.py:217
  13.1 1.5 %collective-permute-done.1.refs_0_ = f32[32,512]{1,0:T(8,128)S(1)} collective-permute-done((f32[32,512]{1,0:T(8,128)S(1)}, f32[32,512]{1,0:T(8,128)S(1)}, u32[]{:S(2)}, u32[]{:S(2)}) %collective-permute-start.1) | collective-permute-done | bytes 65568 | tf_op jit(solution)/shard_map/ppermute | solution.py:217
  14.6 2.8 %collective-permute-done.2.refs_1_ = f32[32,512]{1,0:T(8,128)S(1)} collective-permute-done((f32[32,512]{1,0:T(8,128)S(1)}, f32[32,512]{1,0:T(8,128)S(1)}, u32[]{:S(2)}, u32[]{:S(2)}) %collective-permute-start.2) | collective-permute-done | bytes 65568 | tf_op jit(solution)/shard_map/ppermute | solution.py:217
  17.4 3.3 %collective-permute-start.4 = (f32[32,512]{1,0:T(8,128)S(1)}, f32[32,512]{1,0:T(8,128)S(1)}, u32[]{:S(2)}, u32[]{:S(2)}) collective-permute-start(f32[32,512]{1,0:T(8,128)S(1)} %added.7.refs_3_), channel_id=1, source_target_pairs={{0,64},{8,72},{16,80},{24,88},{32,96},{40,104},{48,112},{56,120},{... | collective-permute-start | bytes 196616 | tf_op jit(solution)/shard_map/ppermute | solution.py:217
  21.7 1.5 %collective-permute-done.4.refs_0_ = f32[32,512]{1,0:T(8,128)S(1)} collective-permute-done((f32[32,512]{1,0:T(8,128)S(1)}, f32[32,512]{1,0:T(8,128)S(1)}, u32[]{:S(2)}, u32[]{:S(2)}) %collective-permute-start.4) | collective-permute-done | bytes 65568 | tf_op jit(solution)/shard_map/ppermute | solution.py:217
  23.3 2.9 %collective-permute-done.5.refs_1_ = f32[32,512]{1,0:T(8,128)S(1)} collective-permute-done((f32[32,512]{1,0:T(8,128)S(1)}, f32[32,512]{1,0:T(8,128)S(1)}, u32[]{:S(2)}, u32[]{:S(2)}) %collective-permute-start.5) | collective-permute-done | bytes 65568 | tf_op jit(solution)/shard_map/ppermute | solution.py:217
  26.2 4.0 %collective-permute-start.7 = (f32[32,512]{1,0:T(8,128)S(1)}, f32[32,512]{1,0:T(8,128)S(1)}, u32[]{:S(2)}, u32[]{:S(2)}) collective-permute-start(f32[32,512]{1,0:T(8,128)S(1)} %added.8.refs_3_), channel_id=1, source_target_pairs={{0,16},{8,24},{16,0},{24,8},{32,48},{40,56},{48,32},{56,40},{64,80... | collective-permute-start | bytes 196616 | tf_op jit(solution)/shard_map/ppermute | solution.py:217
  31.2 1.3 %collective-permute-done.7.refs_0_ = f32[32,512]{1,0:T(8,128)S(1)} collective-permute-done((f32[32,512]{1,0:T(8,128)S(1)}, f32[32,512]{1,0:T(8,128)S(1)}, u32[]{:S(2)}, u32[]{:S(2)}) %collective-permute-start.7) | collective-permute-done | bytes 65568 | tf_op jit(solution)/shard_map/ppermute | solution.py:217
  32.5 3.1 %collective-permute-done.8.refs_1_ = f32[32,512]{1,0:T(8,128)S(1)} collective-permute-done((f32[32,512]{1,0:T(8,128)S(1)}, f32[32,512]{1,0:T(8,128)S(1)}, u32[]{:S(2)}, u32[]{:S(2)}) %collective-permute-start.8) | collective-permute-done | bytes 65568 | tf_op jit(solution)/shard_map/ppermute | solution.py:217
  35.7 1.2 %collective-permute-done.10.other = f32[32,512]{1,0:T(8,128)S(1)} collective-permute-done((f32[32,512]{1,0:T(8,128)S(1)}, f32[32,512]{1,0:T(8,128)S(1)}, u32[]{:S(2)}, u32[]{:S(2)}) %collective-permute-start.10) | collective-permute-done | bytes 65568 | tf_op jit(solution)/shard_map/ppermute | solution.py:217
  37.0 2.3 %project.1 = (f32[32,128]{1,0:T(8,128)}, bf16[32,1024]{1,0:T(8,128)(2,1)S(1)}, bf16[32,896]{1,0:T(8,128)(2,1)S(1)}, bf16[32,896]{1,0:T(8,128)(2,1)S(1)}, bf16[32...) custom-call(f32[32,512]{1,0:T(8,128)S(1)} %added.9.mine, f32[32,512]{1,0:T(8,128)S(1)} %collective-permute-done.10.other, ...), custom_call_target="tpu_custom_call" | custom-call | tf_op jit(solution)/shard_map/project/pallas_call | solution.py:130
  39.3 1.9 %collective-permute-start.11 = (bf16[32,896]{1,0:T(8,128)(2,1)S(1)}, bf16[32,896]{1,0:T(8,128)(2,1)S(1)}, u32[]{:S(2)}, u32[]{:S(2)}) collective-permute-start(bf16[32,896]{1,0:T(8,128)(2,1)S(1)} %get-tuple-element.21), channel_id=1, source_target_pairs={{0,16},{8,24},{16,0},{24,8},{32,48},{40,56},{48,32},{56,40},{64,80... | collective-permute-start | bytes 172040 | tf_op jit(solution)/shard_map/ppermute | solution.py:217
  42.9 2.2 %collective-permute-done.11.refs_0_ = bf16[32,896]{1,0:T(8,128)(2,1)S(1)} collective-permute-done((bf16[32,896]{1,0:T(8,128)(2,1)S(1)}, bf16[32,896]{1,0:T(8,128)(2,1)S(1)}, u32[]{:S(2)}, u32[]{:S(2)}) %collective-permute-start.11) | collective-permute-done | bytes 57376 | tf_op jit(solution)/shard_map/ppermute | solution.py:217
  45.1 1.6 %collective-permute-done.12.refs_1_ = bf16[32,896]{1,0:T(8,128)(2,1)S(1)} collective-permute-done((bf16[32,896]{1,0:T(8,128)(2,1)S(1)}, bf16[32,896]{1,0:T(8,128)(2,1)S(1)}, u32[]{:S(2)}, u32[]{:S(2)}) %collective-permute-start.12) | collective-permute-done | bytes 57376 | tf_op jit(solution)/shard_map/ppermute | solution.py:217
  46.7 1.6 %collective-permute-start.14 = (bf16[32,896]{1,0:T(8,128)(2,1)S(1)}, bf16[32,896]{1,0:T(8,128)(2,1)S(1)}, u32[]{:S(2)}, u32[]{:S(2)}) collective-permute-start(bf16[32,896]{1,0:T(8,128)(2,1)S(1)} %added.10.refs_3_), channel_id=1, source_target_pairs={{0,64},{8,72},{16,80},{24,88},{32,96},{40,104},{48,112},{56,120},{... | collective-permute-start | bytes 172040 | tf_op jit(solution)/shard_map/ppermute | solution.py:217
  50.3 2.8 %collective-permute-done.14.refs_0_ = bf16[32,896]{1,0:T(8,128)(2,1)S(1)} collective-permute-done((bf16[32,896]{1,0:T(8,128)(2,1)S(1)}, bf16[32,896]{1,0:T(8,128)(2,1)S(1)}, u32[]{:S(2)}, u32[]{:S(2)}) %collective-permute-start.14) | collective-permute-done | bytes 57376 | tf_op jit(solution)/shard_map/ppermute | solution.py:217
  53.7 1.9 %collective-permute-start.19 = (bf16[32,896]{1,0:T(8,128)(2,1)S(1)}, bf16[32,896]{1,0:T(8,128)(2,1)S(1)}, u32[]{:S(2)}, u32[]{:S(2)}) collective-permute-start(bf16[32,896]{1,0:T(8,128)(2,1)S(1)} %added.11.refs_0_), channel_id=1, source_target_pairs={{0,16},{8,24},{16,0},{24,8},{32,48},{40,56},{48,32},{56,40},{64,80... | collective-permute-start | bytes 172040 | tf_op jit(solution)/shard_map/ppermute | solution.py:217
  55.7 1.2 %collective-permute-start.17 = (bf16[32,896]{1,0:T(8,128)(2,1)S(1)}, bf16[32,896]{1,0:T(8,128)(2,1)S(1)}, u32[]{:S(2)}, u32[]{:S(2)}) collective-permute-start(bf16[32,896]{1,0:T(8,128)(2,1)S(1)} %added.11.refs_0_), channel_id=1, source_target_pairs={{0,24},{8,16},{16,8},{24,0},{32,56},{40,48},{48,40},{56,32},{64,88... | collective-permute-start | bytes 172040 | tf_op jit(solution)/shard_map/ppermute | solution.py:217
  57.3 1.5 %subtract.3 = (bf16[1,1024,3584]{2,1,0:T(8,128)(2,1)}, f32[32,3584]{1,0:T(8,128)}) custom-call(bf16[32,896]{1,0:T(8,128)(2,1)S(1)} %added.11.refs_0_, bf16[32,1024]{1,0:T(8,128)(2,1)S(1)} %get-tuple-element.25.refs_1_.refs_2_, bf16[1024,3584]{1,0:T(8,128)(2,1)S(1)} %get-tuple-element.20.matrix.refs_2_.refs_3_), custom_call_target="tpu_custom_call" | custom-call | flops 58720256 | bytes 1835008 | tf_op jit(solution)/shard_map/subtract/pallas_call | solution.py:177
  59.5 1.6 %subtract.4 = (bf16[1,1024,3584]{2,1,0:T(8,128)(2,1)}, f32[32,3584]{1,0:T(8,128)}) custom-call(bf16[32,896]{1,0:T(8,128)(2,1)S(1)} %collective-permute-done.19.refs_0_, bf16[32,1024]{1,0:T(8,128)(2,1)S(1)} %get-tuple-element.25.refs_1_.refs_2_, ...), custom_call_target="tpu_custom_call", output_to_operand_aliasing={{0}: (3, {}), {1}: (4, {})} | custom-call | flops 58720256 | bytes 1835008 | tf_op jit(solution)/shard_map/subtract/pallas_call | solution.py:177
  61.1 2.3 %subtract.5 = (bf16[1,1024,3584]{2,1,0:T(8,128)(2,1)}, f32[32,3584]{1,0:T(8,128)}) custom-call(bf16[32,896]{1,0:T(8,128)(2,1)S(1)} %collective-permute-done.17.refs_0_, bf16[32,896]{1,0:T(8,128)(2,1)S(1)} %collective-permute-done.18.refs_1_, bf16[32,1024]{1,0:T(8,128)(2,1)S(1)} %get-tuple-element.25.refs_1_.refs_2_, ...), custom_call_target="tpu_custom_call", output_to_operand_aliasing={{0}: (4, {}), {1}: (5, {})} | custom-call | flops 117440512 | bytes 3670016 | tf_op jit(solution)/shard_map/subtract/pallas_call | solution.py:177
  (28 shorter events, 8.7 us)
Async XLA Ops:
  7.4 1.3 %collective-permute-start = (f32[32,512]{1,0:T(8,128)S(1)}, f32[32,512]{1,0:T(8,128)S(1)}, u32[]{:S(2)}, u32[]{:S(2)}) collective-permute-start(f32[32,512]{1,0:T(8,128)S(1)} %get-tuple-element.19), channel_id=1, source_target_pairs={{0,1},{1,0},{2,3},{3,2},{4,5},{5,4},{6,7},{7,6},{8,9},{9,8},{10,11... | collective-permute-start | bytes 196616 | tf_op jit(solution)/shard_map/ppermute | solution.py:217
  8.7 5.8 %collective-permute-start.1 = (f32[32,512]{1,0:T(8,128)S(1)}, f32[32,512]{1,0:T(8,128)S(1)}, u32[]{:S(2)}, u32[]{:S(2)}) collective-permute-start(f32[32,512]{1,0:T(8,128)S(1)} %added.6.refs_3_), channel_id=1, source_target_pairs={{0,4},{1,5},{2,6},{3,7},{4,0},{5,1},{6,2},{7,3},{8,12},{9,13},{10,... | collective-permute-start | bytes 196616 | tf_op jit(solution)/shard_map/ppermute | solution.py:217
  11.9 5.5 %collective-permute-start.2 = (f32[32,512]{1,0:T(8,128)S(1)}, f32[32,512]{1,0:T(8,128)S(1)}, u32[]{:S(2)}, u32[]{:S(2)}) collective-permute-start(f32[32,512]{1,0:T(8,128)S(1)} %added.6.refs_3_), channel_id=1, source_target_pairs={{0,6},{1,7},{2,4},{3,5},{4,2},{5,3},{6,0},{7,1},{8,14},{9,15},{10,... | collective-permute-start | bytes 196616 | tf_op jit(solution)/shard_map/ppermute | solution.py:217
  13.0 4.3 %collective-permute-start.3 = (f32[32,512]{1,0:T(8,128)S(1)}, f32[32,512]{1,0:T(8,128)S(1)}, u32[]{:S(2)}, u32[]{:S(2)}) collective-permute-start(f32[32,512]{1,0:T(8,128)S(1)} %added.6.refs_3_), channel_id=1, source_target_pairs={{0,2},{1,3},{2,0},{3,1},{4,6},{5,7},{6,4},{7,5},{8,10},{9,11},{10,... | collective-permute-start | bytes 196616 | tf_op jit(solution)/shard_map/ppermute | solution.py:217
  17.4 5.9 %collective-permute-start.4 = (f32[32,512]{1,0:T(8,128)S(1)}, f32[32,512]{1,0:T(8,128)S(1)}, u32[]{:S(2)}, u32[]{:S(2)}) collective-permute-start(f32[32,512]{1,0:T(8,128)S(1)} %added.7.refs_3_), channel_id=1, source_target_pairs={{0,64},{8,72},{16,80},{24,88},{32,96},{40,104},{48,112},{56,120},{... | collective-permute-start | bytes 196616 | tf_op jit(solution)/shard_map/ppermute | solution.py:217
  20.7 5.5 %collective-permute-start.5 = (f32[32,512]{1,0:T(8,128)S(1)}, f32[32,512]{1,0:T(8,128)S(1)}, u32[]{:S(2)}, u32[]{:S(2)}) collective-permute-start(f32[32,512]{1,0:T(8,128)S(1)} %added.7.refs_3_), channel_id=1, source_target_pairs={{0,96},{8,104},{16,112},{24,120},{32,64},{40,72},{48,80},{56,88},{... | collective-permute-start | bytes 196616 | tf_op jit(solution)/shard_map/ppermute | solution.py:217
  21.7 4.4 %collective-permute-start.6 = (f32[32,512]{1,0:T(8,128)S(1)}, f32[32,512]{1,0:T(8,128)S(1)}, u32[]{:S(2)}, u32[]{:S(2)}) collective-permute-start(f32[32,512]{1,0:T(8,128)S(1)} %added.7.refs_3_), channel_id=1, source_target_pairs={{0,32},{8,40},{16,48},{24,56},{32,0},{40,8},{48,16},{56,24},{64,96... | collective-permute-start | bytes 196616 | tf_op jit(solution)/shard_map/ppermute | solution.py:217
  26.2 6.3 %collective-permute-start.7 = (f32[32,512]{1,0:T(8,128)S(1)}, f32[32,512]{1,0:T(8,128)S(1)}, u32[]{:S(2)}, u32[]{:S(2)}) collective-permute-start(f32[32,512]{1,0:T(8,128)S(1)} %added.8.refs_3_), channel_id=1, source_target_pairs={{0,16},{8,24},{16,0},{24,8},{32,48},{40,56},{48,32},{56,40},{64,80... | collective-permute-start | bytes 196616 | tf_op jit(solution)/shard_map/ppermute | solution.py:217
  30.1 5.5 %collective-permute-start.8 = (f32[32,512]{1,0:T(8,128)S(1)}, f32[32,512]{1,0:T(8,128)S(1)}, u32[]{:S(2)}, u32[]{:S(2)}) collective-permute-start(f32[32,512]{1,0:T(8,128)S(1)} %added.8.refs_3_), channel_id=1, source_target_pairs={{0,24},{8,16},{16,8},{24,0},{32,56},{40,48},{48,40},{56,32},{64,88... | collective-permute-start | bytes 196616 | tf_op jit(solution)/shard_map/ppermute | solution.py:217
  30.9 4.8 %collective-permute-start.9 = (f32[32,512]{1,0:T(8,128)S(1)}, f32[32,512]{1,0:T(8,128)S(1)}, u32[]{:S(2)}, u32[]{:S(2)}) collective-permute-start(f32[32,512]{1,0:T(8,128)S(1)} %added.8.refs_3_), channel_id=1, source_target_pairs={{0,8},{8,0},{16,24},{24,16},{32,40},{40,32},{48,56},{56,48},{64,72... | collective-permute-start | bytes 196616 | tf_op jit(solution)/shard_map/ppermute | solution.py:217
  35.6 1.3 %collective-permute-start.10 = (f32[32,512]{1,0:T(8,128)S(1)}, f32[32,512]{1,0:T(8,128)S(1)}, u32[]{:S(2)}, u32[]{:S(2)}) collective-permute-start(f32[32,512]{1,0:T(8,128)S(1)} %added.9.mine), channel_id=1, source_target_pairs={{0,1},{1,0},{2,3},{3,2},{4,5},{5,4},{6,7},{7,6},{8,9},{9,8},{10,11... | collective-permute-start | bytes 196616 | tf_op jit(solution)/shard_map/ppermute | solution.py:217
  39.3 5.8 %collective-permute-start.11 = (bf16[32,896]{1,0:T(8,128)(2,1)S(1)}, bf16[32,896]{1,0:T(8,128)(2,1)S(1)}, u32[]{:S(2)}, u32[]{:S(2)}) collective-permute-start(bf16[32,896]{1,0:T(8,128)(2,1)S(1)} %get-tuple-element.21), channel_id=1, source_target_pairs={{0,16},{8,24},{16,0},{24,8},{32,48},{40,56},{48,32},{56,40},{64,80... | collective-permute-start | bytes 172040 | tf_op jit(solution)/shard_map/ppermute | solution.py:217
  41.3 5.4 %collective-permute-start.12 = (bf16[32,896]{1,0:T(8,128)(2,1)S(1)}, bf16[32,896]{1,0:T(8,128)(2,1)S(1)}, u32[]{:S(2)}, u32[]{:S(2)}) collective-permute-start(bf16[32,896]{1,0:T(8,128)(2,1)S(1)} %get-tuple-element.22), channel_id=1, source_target_pairs={{0,24},{8,16},{16,8},{24,0},{32,56},{40,48},{48,40},{56,32},{64,88... | collective-permute-start | bytes 172040 | tf_op jit(solution)/shard_map/ppermute | solution.py:217
  41.9 4.8 %collective-permute-start.13 = (bf16[32,896]{1,0:T(8,128)(2,1)S(1)}, bf16[32,896]{1,0:T(8,128)(2,1)S(1)}, u32[]{:S(2)}, u32[]{:S(2)}) collective-permute-start(bf16[32,896]{1,0:T(8,128)(2,1)S(1)} %get-tuple-element.23), channel_id=1, source_target_pairs={{0,8},{8,0},{16,24},{24,16},{32,40},{40,32},{48,56},{56,48},{64,72... | collective-permute-start | bytes 172040 | tf_op jit(solution)/shard_map/ppermute | solution.py:217
  46.7 6.3 %collective-permute-start.14 = (bf16[32,896]{1,0:T(8,128)(2,1)S(1)}, bf16[32,896]{1,0:T(8,128)(2,1)S(1)}, u32[]{:S(2)}, u32[]{:S(2)}) collective-permute-start(bf16[32,896]{1,0:T(8,128)(2,1)S(1)} %added.10.refs_3_), channel_id=1, source_target_pairs={{0,64},{8,72},{16,80},{24,88},{32,96},{40,104},{48,112},{56,120},{... | collective-permute-start | bytes 172040 | tf_op jit(solution)/shard_map/ppermute | solution.py:217
  48.3 5.4 %collective-permute-start.15 = (bf16[32,896]{1,0:T(8,128)(2,1)S(1)}, bf16[32,896]{1,0:T(8,128)(2,1)S(1)}, u32[]{:S(2)}, u32[]{:S(2)}) collective-permute-start(bf16[32,896]{1,0:T(8,128)(2,1)S(1)} %added.10.refs_3_), channel_id=1, source_target_pairs={{0,96},{8,104},{16,112},{24,120},{32,64},{40,72},{48,80},{56,88},{... | collective-permute-start | bytes 172040 | tf_op jit(solution)/shard_map/ppermute | solution.py:217
  49.3 4.4 %collective-permute-start.16 = (bf16[32,896]{1,0:T(8,128)(2,1)S(1)}, bf16[32,896]{1,0:T(8,128)(2,1)S(1)}, u32[]{:S(2)}, u32[]{:S(2)}) collective-permute-start(bf16[32,896]{1,0:T(8,128)(2,1)S(1)} %added.10.refs_3_), channel_id=1, source_target_pairs={{0,32},{8,40},{16,48},{24,56},{32,0},{40,8},{48,16},{56,24},{64,96... | collective-permute-start | bytes 172040 | tf_op jit(solution)/shard_map/ppermute | solution.py:217
  53.7 5.8 %collective-permute-start.19 = (bf16[32,896]{1,0:T(8,128)(2,1)S(1)}, bf16[32,896]{1,0:T(8,128)(2,1)S(1)}, u32[]{:S(2)}, u32[]{:S(2)}) collective-permute-start(bf16[32,896]{1,0:T(8,128)(2,1)S(1)} %added.11.refs_0_), channel_id=1, source_target_pairs={{0,16},{8,24},{16,0},{24,8},{32,48},{40,56},{48,32},{56,40},{64,80... | collective-permute-start | bytes 172040 | tf_op jit(solution)/shard_map/ppermute | solution.py:217
  55.7 5.4 %collective-permute-start.17 = (bf16[32,896]{1,0:T(8,128)(2,1)S(1)}, bf16[32,896]{1,0:T(8,128)(2,1)S(1)}, u32[]{:S(2)}, u32[]{:S(2)}) collective-permute-start(bf16[32,896]{1,0:T(8,128)(2,1)S(1)} %added.11.refs_0_), channel_id=1, source_target_pairs={{0,24},{8,16},{16,8},{24,0},{32,56},{40,48},{48,40},{56,32},{64,88... | collective-permute-start | bytes 172040 | tf_op jit(solution)/shard_map/ppermute | solution.py:217
  56.9 4.2 %collective-permute-start.18 = (bf16[32,896]{1,0:T(8,128)(2,1)S(1)}, bf16[32,896]{1,0:T(8,128)(2,1)S(1)}, u32[]{:S(2)}, u32[]{:S(2)}) collective-permute-start(bf16[32,896]{1,0:T(8,128)(2,1)S(1)} %added.11.refs_0_), channel_id=1, source_target_pairs={{0,8},{8,0},{16,24},{24,16},{32,40},{40,32},{48,56},{56,48},{64,72... | collective-permute-start | bytes 172040 | tf_op jit(solution)/shard_map/ppermute | solution.py:217

commit v12 on v8

--- a/solution.py
+++ b/solution.py
@@ -17,7 +17,7 @@
 BLOCK = 16
 RING = 4
 FAR_FIRST = (2, 3, 1, 0)
-WIDTHS = (768, 768, 768, 512, 512, 256)
+WIDTHS = (256, 768, 768, 768, 512, 512)
 STARTS = tuple(sum(WIDTHS[:i]) for i in range(len(WIDTHS)))
 
 
@@ -25,29 +25,41 @@
     return lax.rem(lax.axis_index("tensor"), 2) == 0
 
 
-def merge_kernel(grads, errors, basis_t, matrix, kept, sent, held, partial, grad_sems, error_sems):
-    def copies(i):
-        part = (slice(None), pl.ds(STARTS[i], WIDTHS[i]))
-        return (
-            pltpu.make_async_copy(grads.at[(0, *part)], matrix.at[part], grad_sems.at[i]),
-            pltpu.make_async_copy(errors.at[(0, *part)], held.at[part], error_sems.at[i]),
-        )
-
-    for i in range(len(WIDTHS)):
-        for copy in copies(i):
+def chunk_copies(grads, errors, matrix, held, grad_sems, error_sems, i):
+    part = (slice(None), pl.ds(STARTS[i], WIDTHS[i]))
+    return (
+        pltpu.make_async_copy(grads.at[(0, *part)], matrix.at[part], grad_sems.at[i]),
+        pltpu.make_async_copy(errors.at[(0, *part)], held.at[part], error_sems.at[i]),
+    )
+
+
+def begin_kernel(grads, errors, matrix, held, grad_sems, error_sems):
+    copies = chunk_copies(grads, errors, matrix, held, grad_sems, error_sems, 0)
+    for copy in copies:
+        copy.start()
+    for copy in copies:
+        copy.wait()
+    matrix[:, : WIDTHS[0]] = matrix[:, : WIDTHS[0]] + held[:, : WIDTHS[0]]
+
+
+def merge_kernel(grads, errors, basis_t, begun, matrix, kept, sent, held, partial, grad_sems, error_sems):
+    later = range(1, len(WIDTHS))
+    for i in later:
+        for copy in chunk_copies(grads, errors, matrix, held, grad_sems, error_sems, i):
             copy.start()
     basis_b = basis_t[...].astype(BF16)
     half = kept.shape[1]
     first = on_first_core()
-    for i in range(len(WIDTHS)):
-        for copy in copies(i):
+    begun_part = begun[:, : WIDTHS[0]]
+    partial[...] = lax.dot_general(basis_b[:, : WIDTHS[0]], begun_part, LAST_BY_LAST, preferred_element_type=F32)
+    for i in later:
+        for copy in chunk_copies(grads, errors, matrix, held, grad_sems, error_sems, i):
             copy.wait()
         part = slice(STARTS[i], STARTS[i] + WIDTHS[i])
         total = matrix[:, part] + held[:, part]
         matrix[:, part] = total
         product = lax.dot_general(basis_b[:, part], total, LAST_BY_LAST, preferred_element_type=F32)
-        if i:
-            product = partial[...] + product
+        product = partial[...] + product
         if i < len(WIDTHS) - 1:
             partial[...] = product
     kept[...] = jnp.where(first, product[:, :half], product[:, half:])
@@ -57,24 +69,30 @@
 def merge(grads, errors, basis_t):
     rows, cols = grads.shape[1:]
     rank = basis_t.shape[0]
+    whole = jax.ShapeDtypeStruct((rows, cols), BF16)
+    half = jax.ShapeDtypeStruct((rank, rows // 2), F32)
+    sems = [pltpu.SemaphoreType.DMA((len(WIDTHS),))] * 2
+    params = pltpu.CompilerParams(vmem_limit_bytes=44 << 20)
+    begun = pl.pallas_call(
+        begin_kernel,
+        out_shape=whole,
+        in_specs=[IN_HBM] * 2,
+        out_specs=IN_VMEM,
+        scratch_shapes=[pltpu.VMEM((rows, WIDTHS[0]), BF16), *sems],
+        compiler_params=params,
+        cost_estimate=pl.CostEstimate(flops=rows * WIDTHS[0], bytes_accessed=4 * rows * WIDTHS[0], transcendentals=0),
+        name="begin",
+    )(grads, errors)
     return pl.pallas_call(
         merge_kernel,
-        out_shape=(
-            jax.ShapeDtypeStruct((rows, cols), BF16),
-            jax.ShapeDtypeStruct((rank, rows // 2), F32),
-            jax.ShapeDtypeStruct((rank, rows // 2), F32),
-        ),
-        in_specs=[IN_HBM, IN_HBM, IN_VMEM],
+        out_shape=(whole, half, half),
+        in_specs=[IN_HBM, IN_HBM, IN_VMEM, IN_VMEM],
         out_specs=(IN_VMEM,) * 3,
-        scratch_shapes=[
-            pltpu.VMEM((rows, cols), BF16),
-            pltpu.VMEM((rank, rows), F32),
-            pltpu.SemaphoreType.DMA((len(WIDTHS),)),
-            pltpu.SemaphoreType.DMA((len(WIDTHS),)),
-        ],
-        compiler_params=pltpu.CompilerParams(vmem_limit_bytes=44 << 20),
+        scratch_shapes=[pltpu.VMEM((rows, cols), BF16), pltpu.VMEM((rank, rows), F32), *sems],
+        input_output_aliases={3: 0},
+        compiler_params=params,
         name="merge",
-    )(grads, errors, basis_t)
+    )(grads, errors, basis_t, begun)
 
 
 def inverse_factor(gram):

time: 63.5 us -> 64 us (level)
  Pallas kernels: 13.5 us -> 15.1 us
  local copies, waits for them, and re-layouts: 1.01 us -> 0.01 us
    pallas_call x1 -> x2, Pallas kernels: 5.68 us -> 7.26 us  [the longest x1 5.84 us: merge(): pl.pallas_call(merge_kernel, out_shape=(whole, half, half), in_specs=[IN_...]
    unnamed x2, local copies, waits for them, and re-layouts: 1.01 us -> 0.01 us
where the time goes in v12:
time: 64 us; the launch traced here: 63.9 us
  starting transfers between devices  24.5 us (38%)
  waiting for transfers between devices  23.6 us (37%)
  Pallas kernels  15.1 us (24%)
  between operations  0.74 us (1%)
    ppermute x20, starting transfers between devices, swapped(): lax.ppermute(value, axis, [(i, i ^ distance * stride) for i in range(lax....  24.5 us
    ppermute x20, waiting for transfers between devices, swapped(): lax.ppermute(value, axis, [(i, i ^ distance * stride) for i in range(lax....  23.6 us
    pallas_call x1, Pallas kernels, merge(): pl.pallas_call(merge_kernel, out_shape=(whole, half, half), in_specs=[IN_...  5.84 us
    pallas_call x3, Pallas kernels, subtract(): pl.pallas_call(functools.partial(subtract_kernel, mean, distances), out_s...  5.37 us
    pallas_call x1, Pallas kernels, project(): pl.pallas_call(project_kernel, out_shape=(jax.ShapeDtypeStruct((rank, LAN...  2.33 us
    pallas_call x1, Pallas kernels, merge(): pl.pallas_call(begin_kernel, out_shape=whole, in_specs=[IN_HBM] * 2, out_...  1.42 us
  transfers between devices with their start and end apart: 20, of which 13 were waited for; matrix products, arithmetic and copies ran while one was open for 0% of the time, Pallas kernels for 5%

profile of v12, /device:TPU:0, one launch (start us, length us, event | category | flops | bytes accessed | tf_op | source)
XLA Modules:
  0.0 63.9 jit_solution(5069655706138747896)
XLA Ops:
  0.6 1.4 %begin.1.begun = bf16[1024,3584]{1,0:T(8,128)(2,1)S(1)} custom-call(bf16[1,1024,3584]{2,1,0:T(8,128)(2,1)} %grads.3, bf16[1,1024,3584]{2,1,0:T(8,128)(2,1)} %errors.3), custom_call_target="tpu_custom_call" | custom-call | flops 262144 | bytes 1048576 | tf_op jit(solution)/shard_map/begin/pallas_call | solution.py:76
  2.1 5.8 %merge.1 = (bf16[1024,3584]{1,0:T(8,128)(2,1)S(1)}, f32[32,512]{1,0:T(8,128)S(1)}, f32[32,512]{1,0:T(8,128)S(1)}) custom-call(bf16[1,1024,3584]{2,1,0:T(8,128)(2,1)} %grads.3, bf16[1,1024,3584]{2,1,0:T(8,128)(2,1)} %errors.3, f32[32,3584]{1,0:T(8,128)S(1)} %bitcast.3, bf16[1024,3584]{1,0:T(8,128)(2,1)S(1)} %begin.1.begun), custom_call_target="tpu_custom_call", output_to_operand_aliasing={{0}: (3, {})} | custom-call | tf_op jit(solution)/shard_map/merge/pallas_call | solution.py:86
  8.0 1.2 %collective-permute-done.refs_1_ = f32[32,512]{1,0:T(8,128)S(1)} collective-permute-done((f32[32,512]{1,0:T(8,128)S(1)}, f32[32,512]{1,0:T(8,128)S(1)}, u32[]{:S(2)}, u32[]{:S(2)}) %collective-permute-start) | collective-permute-done | bytes 65568 | tf_op jit(solution)/shard_map/ppermute | solution.py:235
  9.3 3.2 %collective-permute-start.1 = (f32[32,512]{1,0:T(8,128)S(1)}, f32[32,512]{1,0:T(8,128)S(1)}, u32[]{:S(2)}, u32[]{:S(2)}) collective-permute-start(f32[32,512]{1,0:T(8,128)S(1)} %added.6.refs_3_), channel_id=1, source_target_pairs={{0,4},{1,5},{2,6},{3,7},{4,0},{5,1},{6,2},{7,3},{8,12},{9,13},{10,... | collective-permute-start | bytes 196616 | tf_op jit(solution)/shard_map/ppermute | solution.py:235
  13.6 1.5 %collective-permute-done.1.refs_0_ = f32[32,512]{1,0:T(8,128)S(1)} collective-permute-done((f32[32,512]{1,0:T(8,128)S(1)}, f32[32,512]{1,0:T(8,128)S(1)}, u32[]{:S(2)}, u32[]{:S(2)}) %collective-permute-start.1) | collective-permute-done | bytes 65568 | tf_op jit(solution)/shard_map/ppermute | solution.py:235
  15.1 2.8 %collective-permute-done.2.refs_1_ = f32[32,512]{1,0:T(8,128)S(1)} collective-permute-done((f32[32,512]{1,0:T(8,128)S(1)}, f32[32,512]{1,0:T(8,128)S(1)}, u32[]{:S(2)}, u32[]{:S(2)}) %collective-permute-start.2) | collective-permute-done | bytes 65568 | tf_op jit(solution)/shard_map/ppermute | solution.py:235
  18.0 3.3 %collective-permute-start.4 = (f32[32,512]{1,0:T(8,128)S(1)}, f32[32,512]{1,0:T(8,128)S(1)}, u32[]{:S(2)}, u32[]{:S(2)}) collective-permute-start(f32[32,512]{1,0:T(8,128)S(1)} %added.7.refs_3_), channel_id=1, source_target_pairs={{0,64},{8,72},{16,80},{24,88},{32,96},{40,104},{48,112},{56,120},{... | collective-permute-start | bytes 196616 | tf_op jit(solution)/shard_map/ppermute | solution.py:235
  22.3 1.6 %collective-permute-done.4.refs_0_ = f32[32,512]{1,0:T(8,128)S(1)} collective-permute-done((f32[32,512]{1,0:T(8,128)S(1)}, f32[32,512]{1,0:T(8,128)S(1)}, u32[]{:S(2)}, u32[]{:S(2)}) %collective-permute-start.4) | collective-permute-done | bytes 65568 | tf_op jit(solution)/shard_map/ppermute | solution.py:235
  23.8 2.9 %collective-permute-done.5.refs_1_ = f32[32,512]{1,0:T(8,128)S(1)} collective-permute-done((f32[32,512]{1,0:T(8,128)S(1)}, f32[32,512]{1,0:T(8,128)S(1)}, u32[]{:S(2)}, u32[]{:S(2)}) %collective-permute-start.5) | collective-permute-done | bytes 65568 | tf_op jit(solution)/shard_map/ppermute | solution.py:235
  26.7 4.0 %collective-permute-start.7 = (f32[32,512]{1,0:T(8,128)S(1)}, f32[32,512]{1,0:T(8,128)S(1)}, u32[]{:S(2)}, u32[]{:S(2)}) collective-permute-start(f32[32,512]{1,0:T(8,128)S(1)} %added.8.refs_3_), channel_id=1, source_target_pairs={{0,16},{8,24},{16,0},{24,8},{32,48},{40,56},{48,32},{56,40},{64,80... | collective-permute-start | bytes 196616 | tf_op jit(solution)/shard_map/ppermute | solution.py:235
  31.7 1.3 %collective-permute-done.7.refs_0_ = f32[32,512]{1,0:T(8,128)S(1)} collective-permute-done((f32[32,512]{1,0:T(8,128)S(1)}, f32[32,512]{1,0:T(8,128)S(1)}, u32[]{:S(2)}, u32[]{:S(2)}) %collective-permute-start.7) | collective-permute-done | bytes 65568 | tf_op jit(solution)/shard_map/ppermute | solution.py:235
  33.0 3.1 %collective-permute-done.8.refs_1_ = f32[32,512]{1,0:T(8,128)S(1)} collective-permute-done((f32[32,512]{1,0:T(8,128)S(1)}, f32[32,512]{1,0:T(8,128)S(1)}, u32[]{:S(2)}, u32[]{:S(2)}) %collective-permute-start.8) | collective-permute-done | bytes 65568 | tf_op jit(solution)/shard_map/ppermute | solution.py:235
  36.3 1.2 %collective-permute-done.10.other = f32[32,512]{1,0:T(8,128)S(1)} collective-permute-done((f32[32,512]{1,0:T(8,128)S(1)}, f32[32,512]{1,0:T(8,128)S(1)}, u32[]{:S(2)}, u32[]{:S(2)}) %collective-permute-start.10) | collective-permute-done | bytes 65568 | tf_op jit(solution)/shard_map/ppermute | solution.py:235
  37.5 2.3 %project.1 = (f32[32,128]{1,0:T(8,128)}, bf16[32,1024]{1,0:T(8,128)(2,1)S(1)}, bf16[32,896]{1,0:T(8,128)(2,1)S(1)}, bf16[32,896]{1,0:T(8,128)(2,1)S(1)}, bf16[32...) custom-call(f32[32,512]{1,0:T(8,128)S(1)} %added.9.mine, f32[32,512]{1,0:T(8,128)S(1)} %collective-permute-done.10.other, ...), custom_call_target="tpu_custom_call" | custom-call | tf_op jit(solution)/shard_map/project/pallas_call | solution.py:148
  39.9 1.9 %collective-permute-start.11 = (bf16[32,896]{1,0:T(8,128)(2,1)S(1)}, bf16[32,896]{1,0:T(8,128)(2,1)S(1)}, u32[]{:S(2)}, u32[]{:S(2)}) collective-permute-start(bf16[32,896]{1,0:T(8,128)(2,1)S(1)} %get-tuple-element.21), channel_id=1, source_target_pairs={{0,16},{8,24},{16,0},{24,8},{32,48},{40,56},{48,32},{56,40},{64,80... | collective-permute-start | bytes 172040 | tf_op jit(solution)/shard_map/ppermute | solution.py:235
  43.4 2.2 %collective-permute-done.11.refs_0_ = bf16[32,896]{1,0:T(8,128)(2,1)S(1)} collective-permute-done((bf16[32,896]{1,0:T(8,128)(2,1)S(1)}, bf16[32,896]{1,0:T(8,128)(2,1)S(1)}, u32[]{:S(2)}, u32[]{:S(2)}) %collective-permute-start.11) | collective-permute-done | bytes 57376 | tf_op jit(solution)/shard_map/ppermute | solution.py:235
  45.6 1.6 %collective-permute-done.12.refs_1_ = bf16[32,896]{1,0:T(8,128)(2,1)S(1)} collective-permute-done((bf16[32,896]{1,0:T(8,128)(2,1)S(1)}, bf16[32,896]{1,0:T(8,128)(2,1)S(1)}, u32[]{:S(2)}, u32[]{:S(2)}) %collective-permute-start.12) | collective-permute-done | bytes 57376 | tf_op jit(solution)/shard_map/ppermute | solution.py:235
  47.2 1.6 %collective-permute-start.14 = (bf16[32,896]{1,0:T(8,128)(2,1)S(1)}, bf16[32,896]{1,0:T(8,128)(2,1)S(1)}, u32[]{:S(2)}, u32[]{:S(2)}) collective-permute-start(bf16[32,896]{1,0:T(8,128)(2,1)S(1)} %added.10.refs_3_), channel_id=1, source_target_pairs={{0,64},{8,72},{16,80},{24,88},{32,96},{40,104},{48,112},{56,120},{... | collective-permute-start | bytes 172040 | tf_op jit(solution)/shard_map/ppermute | solution.py:235
  50.8 2.8 %collective-permute-done.14.refs_0_ = bf16[32,896]{1,0:T(8,128)(2,1)S(1)} collective-permute-done((bf16[32,896]{1,0:T(8,128)(2,1)S(1)}, bf16[32,896]{1,0:T(8,128)(2,1)S(1)}, u32[]{:S(2)}, u32[]{:S(2)}) %collective-permute-start.14) | collective-permute-done | bytes 57376 | tf_op jit(solution)/shard_map/ppermute | solution.py:235
  54.3 1.9 %collective-permute-start.19 = (bf16[32,896]{1,0:T(8,128)(2,1)S(1)}, bf16[32,896]{1,0:T(8,128)(2,1)S(1)}, u32[]{:S(2)}, u32[]{:S(2)}) collective-permute-start(bf16[32,896]{1,0:T(8,128)(2,1)S(1)} %added.11.refs_0_), channel_id=1, source_target_pairs={{0,16},{8,24},{16,0},{24,8},{32,48},{40,56},{48,32},{56,40},{64,80... | collective-permute-start | bytes 172040 | tf_op jit(solution)/shard_map/ppermute | solution.py:235
  56.2 1.2 %collective-permute-start.17 = (bf16[32,896]{1,0:T(8,128)(2,1)S(1)}, bf16[32,896]{1,0:T(8,128)(2,1)S(1)}, u32[]{:S(2)}, u32[]{:S(2)}) collective-permute-start(bf16[32,896]{1,0:T(8,128)(2,1)S(1)} %added.11.refs_0_), channel_id=1, source_target_pairs={{0,24},{8,16},{16,8},{24,0},{32,56},{40,48},{48,40},{56,32},{64,88... | collective-permute-start | bytes 172040 | tf_op jit(solution)/shard_map/ppermute | solution.py:235
  57.9 1.6 %subtract.3 = (bf16[1,1024,3584]{2,1,0:T(8,128)(2,1)}, f32[32,3584]{1,0:T(8,128)}) custom-call(bf16[32,896]{1,0:T(8,128)(2,1)S(1)} %added.11.refs_0_, bf16[32,1024]{1,0:T(8,128)(2,1)S(1)} %get-tuple-element.25.refs_1_.refs_2_, bf16[1024,3584]{1,0:T(8,128)(2,1)S(1)} %get-tuple-element.20.matrix.refs_2_.refs_3_), custom_call_target="tpu_custom_call" | custom-call | flops 58720256 | bytes 1835008 | tf_op jit(solution)/shard_map/subtract/pallas_call | solution.py:195
  60.0 1.5 %subtract.4 = (bf16[1,1024,3584]{2,1,0:T(8,128)(2,1)}, f32[32,3584]{1,0:T(8,128)}) custom-call(bf16[32,896]{1,0:T(8,128)(2,1)S(1)} %collective-permute-done.19.refs_0_, bf16[32,1024]{1,0:T(8,128)(2,1)S(1)} %get-tuple-element.25.refs_1_.refs_2_, ...), custom_call_target="tpu_custom_call", output_to_operand_aliasing={{0}: (3, {}), {1}: (4, {})} | custom-call | flops 58720256 | bytes 1835008 | tf_op jit(solution)/shard_map/subtract/pallas_call | solution.py:195
  61.6 2.3 %subtract.5 = (bf16[1,1024,3584]{2,1,0:T(8,128)(2,1)}, f32[32,3584]{1,0:T(8,128)}) custom-call(bf16[32,896]{1,0:T(8,128)(2,1)S(1)} %collective-permute-done.17.refs_0_, bf16[32,896]{1,0:T(8,128)(2,1)S(1)} %collective-permute-done.18.refs_1_, bf16[32,1024]{1,0:T(8,128)(2,1)S(1)} %get-tuple-element.25.refs_1_.refs_2_, ...), custom_call_target="tpu_custom_call", output_to_operand_aliasing={{0}: (4, {}), {1}: (5, {})} | custom-call | flops 117440512 | bytes 3670016 | tf_op jit(solution)/shard_map/subtract/pallas_call | solution.py:195
  (30 shorter events, 8.8 us)
Async XLA Ops:
  0.6 1.4 %copy-start = (f32[3584,32]{0,1:T(8,128)S(1)}, f32[3584,32]{0,1:T(8,128)}, u32[]{:S(2)}) copy-start(f32[3584,32]{0,1:T(8,128)} %param.5) | copy-start | bytes 1376260
  7.9 1.3 %collective-permute-start = (f32[32,512]{1,0:T(8,128)S(1)}, f32[32,512]{1,0:T(8,128)S(1)}, u32[]{:S(2)}, u32[]{:S(2)}) collective-permute-start(f32[32,512]{1,0:T(8,128)S(1)} %get-tuple-element.19), channel_id=1, source_target_pairs={{0,1},{1,0},{2,3},{3,2},{4,5},{5,4},{6,7},{7,6},{8,9},{9,8},{10,11... | collective-permute-start | bytes 196616 | tf_op jit(solution)/shard_map/ppermute | solution.py:235
  9.3 5.8 %collective-permute-start.1 = (f32[32,512]{1,0:T(8,128)S(1)}, f32[32,512]{1,0:T(8,128)S(1)}, u32[]{:S(2)}, u32[]{:S(2)}) collective-permute-start(f32[32,512]{1,0:T(8,128)S(1)} %added.6.refs_3_), channel_id=1, source_target_pairs={{0,4},{1,5},{2,6},{3,7},{4,0},{5,1},{6,2},{7,3},{8,12},{9,13},{10,... | collective-permute-start | bytes 196616 | tf_op jit(solution)/shard_map/ppermute | solution.py:235
  12.5 5.5 %collective-permute-start.2 = (f32[32,512]{1,0:T(8,128)S(1)}, f32[32,512]{1,0:T(8,128)S(1)}, u32[]{:S(2)}, u32[]{:S(2)}) collective-permute-start(f32[32,512]{1,0:T(8,128)S(1)} %added.6.refs_3_), channel_id=1, source_target_pairs={{0,6},{1,7},{2,4},{3,5},{4,2},{5,3},{6,0},{7,1},{8,14},{9,15},{10,... | collective-permute-start | bytes 196616 | tf_op jit(solution)/shard_map/ppermute | solution.py:235
  13.6 4.3 %collective-permute-start.3 = (f32[32,512]{1,0:T(8,128)S(1)}, f32[32,512]{1,0:T(8,128)S(1)}, u32[]{:S(2)}, u32[]{:S(2)}) collective-permute-start(f32[32,512]{1,0:T(8,128)S(1)} %added.6.refs_3_), channel_id=1, source_target_pairs={{0,2},{1,3},{2,0},{3,1},{4,6},{5,7},{6,4},{7,5},{8,10},{9,11},{10,... | collective-permute-start | bytes 196616 | tf_op jit(solution)/shard_map/ppermute | solution.py:235
  18.0 5.9 %collective-permute-start.4 = (f32[32,512]{1,0:T(8,128)S(1)}, f32[32,512]{1,0:T(8,128)S(1)}, u32[]{:S(2)}, u32[]{:S(2)}) collective-permute-start(f32[32,512]{1,0:T(8,128)S(1)} %added.7.refs_3_), channel_id=1, source_target_pairs={{0,64},{8,72},{16,80},{24,88},{32,96},{40,104},{48,112},{56,120},{... | collective-permute-start | bytes 196616 | tf_op jit(solution)/shard_map/ppermute | solution.py:235
  21.2 5.5 %collective-permute-start.5 = (f32[32,512]{1,0:T(8,128)S(1)}, f32[32,512]{1,0:T(8,128)S(1)}, u32[]{:S(2)}, u32[]{:S(2)}) collective-permute-start(f32[32,512]{1,0:T(8,128)S(1)} %added.7.refs_3_), channel_id=1, source_target_pairs={{0,96},{8,104},{16,112},{24,120},{32,64},{40,72},{48,80},{56,88},{... | collective-permute-start | bytes 196616 | tf_op jit(solution)/shard_map/ppermute | solution.py:235
  22.3 4.4 %collective-permute-start.6 = (f32[32,512]{1,0:T(8,128)S(1)}, f32[32,512]{1,0:T(8,128)S(1)}, u32[]{:S(2)}, u32[]{:S(2)}) collective-permute-start(f32[32,512]{1,0:T(8,128)S(1)} %added.7.refs_3_), channel_id=1, source_target_pairs={{0,32},{8,40},{16,48},{24,56},{32,0},{40,8},{48,16},{56,24},{64,96... | collective-permute-start | bytes 196616 | tf_op jit(solution)/shard_map/ppermute | solution.py:235
  26.7 6.3 %collective-permute-start.7 = (f32[32,512]{1,0:T(8,128)S(1)}, f32[32,512]{1,0:T(8,128)S(1)}, u32[]{:S(2)}, u32[]{:S(2)}) collective-permute-start(f32[32,512]{1,0:T(8,128)S(1)} %added.8.refs_3_), channel_id=1, source_target_pairs={{0,16},{8,24},{16,0},{24,8},{32,48},{40,56},{48,32},{56,40},{64,80... | collective-permute-start | bytes 196616 | tf_op jit(solution)/shard_map/ppermute | solution.py:235
  30.7 5.5 %collective-permute-start.8 = (f32[32,512]{1,0:T(8,128)S(1)}, f32[32,512]{1,0:T(8,128)S(1)}, u32[]{:S(2)}, u32[]{:S(2)}) collective-permute-start(f32[32,512]{1,0:T(8,128)S(1)} %added.8.refs_3_), channel_id=1, source_target_pairs={{0,24},{8,16},{16,8},{24,0},{32,56},{40,48},{48,40},{56,32},{64,88... | collective-permute-start | bytes 196616 | tf_op jit(solution)/shard_map/ppermute | solution.py:235
  31.4 4.8 %collective-permute-start.9 = (f32[32,512]{1,0:T(8,128)S(1)}, f32[32,512]{1,0:T(8,128)S(1)}, u32[]{:S(2)}, u32[]{:S(2)}) collective-permute-start(f32[32,512]{1,0:T(8,128)S(1)} %added.8.refs_3_), channel_id=1, source_target_pairs={{0,8},{8,0},{16,24},{24,16},{32,40},{40,32},{48,56},{56,48},{64,72... | collective-permute-start | bytes 196616 | tf_op jit(solution)/shard_map/ppermute | solution.py:235
  36.2 1.3 %collective-permute-start.10 = (f32[32,512]{1,0:T(8,128)S(1)}, f32[32,512]{1,0:T(8,128)S(1)}, u32[]{:S(2)}, u32[]{:S(2)}) collective-permute-start(f32[32,512]{1,0:T(8,128)S(1)} %added.9.mine), channel_id=1, source_target_pairs={{0,1},{1,0},{2,3},{3,2},{4,5},{5,4},{6,7},{7,6},{8,9},{9,8},{10,11... | collective-permute-start | bytes 196616 | tf_op jit(solution)/shard_map/ppermute | solution.py:235
  39.9 5.8 %collective-permute-start.11 = (bf16[32,896]{1,0:T(8,128)(2,1)S(1)}, bf16[32,896]{1,0:T(8,128)(2,1)S(1)}, u32[]{:S(2)}, u32[]{:S(2)}) collective-permute-start(bf16[32,896]{1,0:T(8,128)(2,1)S(1)} %get-tuple-element.21), channel_id=1, source_target_pairs={{0,16},{8,24},{16,0},{24,8},{32,48},{40,56},{48,32},{56,40},{64,80... | collective-permute-start | bytes 172040 | tf_op jit(solution)/shard_map/ppermute | solution.py:235
  41.8 5.4 %collective-permute-start.12 = (bf16[32,896]{1,0:T(8,128)(2,1)S(1)}, bf16[32,896]{1,0:T(8,128)(2,1)S(1)}, u32[]{:S(2)}, u32[]{:S(2)}) collective-permute-start(bf16[32,896]{1,0:T(8,128)(2,1)S(1)} %get-tuple-element.22), channel_id=1, source_target_pairs={{0,24},{8,16},{16,8},{24,0},{32,56},{40,48},{48,40},{56,32},{64,88... | collective-permute-start | bytes 172040 | tf_op jit(solution)/shard_map/ppermute | solution.py:235
  42.4 4.8 %collective-permute-start.13 = (bf16[32,896]{1,0:T(8,128)(2,1)S(1)}, bf16[32,896]{1,0:T(8,128)(2,1)S(1)}, u32[]{:S(2)}, u32[]{:S(2)}) collective-permute-start(bf16[32,896]{1,0:T(8,128)(2,1)S(1)} %get-tuple-element.23), channel_id=1, source_target_pairs={{0,8},{8,0},{16,24},{24,16},{32,40},{40,32},{48,56},{56,48},{64,72... | collective-permute-start | bytes 172040 | tf_op jit(solution)/shard_map/ppermute | solution.py:235
  47.2 6.3 %collective-permute-start.14 = (bf16[32,896]{1,0:T(8,128)(2,1)S(1)}, bf16[32,896]{1,0:T(8,128)(2,1)S(1)}, u32[]{:S(2)}, u32[]{:S(2)}) collective-permute-start(bf16[32,896]{1,0:T(8,128)(2,1)S(1)} %added.10.refs_3_), channel_id=1, source_target_pairs={{0,64},{8,72},{16,80},{24,88},{32,96},{40,104},{48,112},{56,120},{... | collective-permute-start | bytes 172040 | tf_op jit(solution)/shard_map/ppermute | solution.py:235
  48.9 5.4 %collective-permute-start.15 = (bf16[32,896]{1,0:T(8,128)(2,1)S(1)}, bf16[32,896]{1,0:T(8,128)(2,1)S(1)}, u32[]{:S(2)}, u32[]{:S(2)}) collective-permute-start(bf16[32,896]{1,0:T(8,128)(2,1)S(1)} %added.10.refs_3_), channel_id=1, source_target_pairs={{0,96},{8,104},{16,112},{24,120},{32,64},{40,72},{48,80},{56,88},{... | collective-permute-start | bytes 172040 | tf_op jit(solution)/shard_map/ppermute | solution.py:235
  49.8 4.4 %collective-permute-start.16 = (bf16[32,896]{1,0:T(8,128)(2,1)S(1)}, bf16[32,896]{1,0:T(8,128)(2,1)S(1)}, u32[]{:S(2)}, u32[]{:S(2)}) collective-permute-start(bf16[32,896]{1,0:T(8,128)(2,1)S(1)} %added.10.refs_3_), channel_id=1, source_target_pairs={{0,32},{8,40},{16,48},{24,56},{32,0},{40,8},{48,16},{56,24},{64,96... | collective-permute-start | bytes 172040 | tf_op jit(solution)/shard_map/ppermute | solution.py:235
  54.3 5.8 %collective-permute-start.19 = (bf16[32,896]{1,0:T(8,128)(2,1)S(1)}, bf16[32,896]{1,0:T(8,128)(2,1)S(1)}, u32[]{:S(2)}, u32[]{:S(2)}) collective-permute-start(bf16[32,896]{1,0:T(8,128)(2,1)S(1)} %added.11.refs_0_), channel_id=1, source_target_pairs={{0,16},{8,24},{16,0},{24,8},{32,48},{40,56},{48,32},{56,40},{64,80... | collective-permute-start | bytes 172040 | tf_op jit(solution)/shard_map/ppermute | solution.py:235
  56.2 5.4 %collective-permute-start.17 = (bf16[32,896]{1,0:T(8,128)(2,1)S(1)}, bf16[32,896]{1,0:T(8,128)(2,1)S(1)}, u32[]{:S(2)}, u32[]{:S(2)}) collective-permute-start(bf16[32,896]{1,0:T(8,128)(2,1)S(1)} %added.11.refs_0_), channel_id=1, source_target_pairs={{0,24},{8,16},{16,8},{24,0},{32,56},{40,48},{48,40},{56,32},{64,88... | collective-permute-start | bytes 172040 | tf_op jit(solution)/shard_map/ppermute | solution.py:235
  57.4 4.2 %collective-permute-start.18 = (bf16[32,896]{1,0:T(8,128)(2,1)S(1)}, bf16[32,896]{1,0:T(8,128)(2,1)S(1)}, u32[]{:S(2)}, u32[]{:S(2)}) collective-permute-start(bf16[32,896]{1,0:T(8,128)(2,1)S(1)} %added.11.refs_0_), channel_id=1, source_target_pairs={{0,8},{8,0},{16,24},{24,16},{32,40},{40,32},{48,56},{56,48},{64,72... | collective-permute-start | bytes 172040 | tf_op jit(solution)/shard_map/ppermute | solution.py:235

commit v13 on v8

--- a/solution.py
+++ b/solution.py
@@ -16,7 +16,7 @@
 CHUNKS = 8
 BLOCK = 16
 RING = 4
-FAR_FIRST = (2, 3, 1, 0)
+EARLY, LATE = (2, 3, 1), (0,)
 WIDTHS = (768, 768, 768, 512, 512, 256)
 STARTS = tuple(sum(WIDTHS[:i]) for i in range(len(WIDTHS)))
 
@@ -116,12 +116,33 @@
     p_own[...] = jnp.dot(inverse, own, precision=HIGHEST, preferred_element_type=F32)
     rounded = jnp.dot(inverse, p_sum, precision=HIGHEST, preferred_element_type=F32).astype(BF16)
     p_b[...] = rounded
+    quarters(rounded, matrix, EARLY, q_parts)
+
+
+def quarters(left, matrix, distances, q_parts):
     width = q_parts[0].shape[1]
     position = lax.rem(lax.axis_index("dp"), RING)
-    for distance in FAR_FIRST:
+    for distance, q_part in zip(distances, q_parts):
         cols = pl.ds(pl.multiple_of((position ^ distance) * width, LANES), width)
-        product = jnp.dot(rounded, matrix[:, cols], preferred_element_type=F32)
-        q_parts[distance][...] = product.astype(BF16)
+        q_part[...] = jnp.dot(left, matrix[:, cols], preferred_element_type=F32).astype(BF16)
+
+
+def rest_kernel(p_b, matrix, _, *q_parts):
+    quarters(p_b[...], matrix, LATE, q_parts)
+
+
+def rest(p_b, matrix, arrived):
+    rank, (rows, cols) = p_b.shape[0], matrix.shape
+    size = rows * cols // RING * len(LATE)
+    return pl.pallas_call(
+        rest_kernel,
+        out_shape=(jax.ShapeDtypeStruct((rank, cols // RING), BF16),) * len(LATE),
+        in_specs=[IN_VMEM] * 3,
+        out_specs=(IN_VMEM,) * len(LATE),
+        compiler_params=pltpu.CompilerParams(vmem_limit_bytes=8 << 20),
+        cost_estimate=pl.CostEstimate(flops=2 * size * rank, bytes_accessed=2 * size, transcendentals=0),
+        name="rest",
+    )(p_b, matrix, arrived)
 
 
 def project(mine, other, matrix):
@@ -132,10 +153,10 @@
         out_shape=(
             jax.ShapeDtypeStruct((rank, LANES), F32),
             jax.ShapeDtypeStruct((rank, rows), BF16),
-            *[jax.ShapeDtypeStruct((rank, cols // RING), BF16)] * RING,
+            *[jax.ShapeDtypeStruct((rank, cols // RING), BF16)] * len(EARLY),
         ),
         in_specs=[IN_VMEM] * 3,
-        out_specs=(IN_VMEM,) * (2 + RING),
+        out_specs=(IN_VMEM,) * (2 + len(EARLY)),
         scratch_shapes=[pltpu.VMEM((rank, rows), F32)],
         compiler_params=pltpu.CompilerParams(vmem_limit_bytes=24 << 20),
         name="project",
@@ -229,8 +250,9 @@
     mine = summed_over_four(mine, "dp", 4)
     mine = summed_over_four(mine, "dp", 1)
     p_own, p_b, *q_parts = project(mine, swapped(mine, "tensor", 1, 1), matrix)
-    one, three, two = (swapped(q_parts[distance], "dp", 1, distance) for distance in (1, 3, 2))
-    q_sum = summed_over_four(added(two, three, one, q_parts[0]), "dp", 4)
+    two, three, one = (swapped(q_part, "dp", 1, distance) for q_part, distance in zip(q_parts, EARLY))
+    (q_own,) = rest(p_b, matrix, two)
+    q_sum = summed_over_four(added(two, three, one, q_own), "dp", 4)
     mean, earlier = 1.0 / lax.axis_size("dp"), ()
     for distances in ((0,), (2,), (3, 1)):
         q_now = [swapped(q_sum, "dp", 1, distance) if distance else q_sum for distance in distances]

time: 63.5 us -> 63.2 us (level)
  transfers between devices with their start and end apart: 20 -> 20, of which waited for: 13 -> 13; matrix products, arithmetic and copies ran while one was open for 0% -> 0% of each run, Pallas kernels for 5% -> 6%
where the time goes in v13:
time: 63.2 us; the launch traced here: 63.1 us
  starting transfers between devices  24.5 us (39%)
  waiting for transfers between devices  23.1 us (37%)
  Pallas kernels  13.7 us (22%)
  local copies, waits for them, and re-layouts  1.01 us (2%)
  between operations  0.74 us (1%)
    ppermute x20, starting transfers between devices, swapped(): lax.ppermute(value, axis, [(i, i ^ distance * stride) for i in range(lax....  24.5 us
    ppermute x20, waiting for transfers between devices, swapped(): lax.ppermute(value, axis, [(i, i ^ distance * stride) for i in range(lax....  23.1 us
    pallas_call x1, Pallas kernels, merge(): pl.pallas_call(merge_kernel, out_shape=(jax.ShapeDtypeStruct((rows, cols)...  5.68 us
    pallas_call x3, Pallas kernels, subtract(): pl.pallas_call(functools.partial(subtract_kernel, mean, distances), out_s...  5.37 us
    pallas_call x1, Pallas kernels, project(): pl.pallas_call(project_kernel, out_shape=(jax.ShapeDtypeStruct((rank, LAN...  2.1 us
  transfers between devices with their start and end apart: 20, of which 13 were waited for; matrix products, arithmetic and copies ran while one was open for 0% of the time, Pallas kernels for 6%

profile of v13, /device:TPU:0, one launch (start us, length us, event | category | flops | bytes accessed | tf_op | source)
XLA Modules:
  0.0 63.1 jit_solution(17992450568253424214)
XLA Ops:
  1.6 5.7 %merge.1 = (bf16[1024,3584]{1,0:T(8,128)(2,1)S(1)}, f32[32,512]{1,0:T(8,128)S(1)}, f32[32,512]{1,0:T(8,128)S(1)}) custom-call(bf16[1,1024,3584]{2,1,0:T(8,128)(2,1)} %grads.1, bf16[1,1024,3584]{2,1,0:T(8,128)(2,1)} %errors.1, f32[32,3584]{1,0:T(8,128)S(1)} %bitcast.3), custom_call_target="tpu_custom_call" | custom-call | tf_op jit(solution)/shard_map/merge/pallas_call | solution.py:60
  7.4 1.2 %collective-permute-done.refs_1_ = f32[32,512]{1,0:T(8,128)S(1)} collective-permute-done((f32[32,512]{1,0:T(8,128)S(1)}, f32[32,512]{1,0:T(8,128)S(1)}, u32[]{:S(2)}, u32[]{:S(2)}) %collective-permute-start) | collective-permute-done | bytes 65568 | tf_op jit(solution)/shard_map/ppermute | solution.py:238
  8.7 3.2 %collective-permute-start.1 = (f32[32,512]{1,0:T(8,128)S(1)}, f32[32,512]{1,0:T(8,128)S(1)}, u32[]{:S(2)}, u32[]{:S(2)}) collective-permute-start(f32[32,512]{1,0:T(8,128)S(1)} %added.6.refs_3_), channel_id=1, source_target_pairs={{0,4},{1,5},{2,6},{3,7},{4,0},{5,1},{6,2},{7,3},{8,12},{9,13},{10,... | collective-permute-start | bytes 196616 | tf_op jit(solution)/shard_map/ppermute | solution.py:238
  11.9 1.1 %collective-permute-start.2 = (f32[32,512]{1,0:T(8,128)S(1)}, f32[32,512]{1,0:T(8,128)S(1)}, u32[]{:S(2)}, u32[]{:S(2)}) collective-permute-start(f32[32,512]{1,0:T(8,128)S(1)} %added.6.refs_3_), channel_id=1, source_target_pairs={{0,6},{1,7},{2,4},{3,5},{4,2},{5,3},{6,0},{7,1},{8,14},{9,15},{10,... | collective-permute-start | bytes 196616 | tf_op jit(solution)/shard_map/ppermute | solution.py:238
  13.0 1.5 %collective-permute-done.1.refs_0_ = f32[32,512]{1,0:T(8,128)S(1)} collective-permute-done((f32[32,512]{1,0:T(8,128)S(1)}, f32[32,512]{1,0:T(8,128)S(1)}, u32[]{:S(2)}, u32[]{:S(2)}) %collective-permute-start.1) | collective-permute-done | bytes 65568 | tf_op jit(solution)/shard_map/ppermute | solution.py:238
  14.5 2.8 %collective-permute-done.2.refs_1_ = f32[32,512]{1,0:T(8,128)S(1)} collective-permute-done((f32[32,512]{1,0:T(8,128)S(1)}, f32[32,512]{1,0:T(8,128)S(1)}, u32[]{:S(2)}, u32[]{:S(2)}) %collective-permute-start.2) | collective-permute-done | bytes 65568 | tf_op jit(solution)/shard_map/ppermute | solution.py:238
  17.4 3.3 %collective-permute-start.4 = (f32[32,512]{1,0:T(8,128)S(1)}, f32[32,512]{1,0:T(8,128)S(1)}, u32[]{:S(2)}, u32[]{:S(2)}) collective-permute-start(f32[32,512]{1,0:T(8,128)S(1)} %added.7.refs_3_), channel_id=1, source_target_pairs={{0,64},{8,72},{16,80},{24,88},{32,96},{40,104},{48,112},{56,120},{... | collective-permute-start | bytes 196616 | tf_op jit(solution)/shard_map/ppermute | solution.py:238
  21.7 1.5 %collective-permute-done.4.refs_0_ = f32[32,512]{1,0:T(8,128)S(1)} collective-permute-done((f32[32,512]{1,0:T(8,128)S(1)}, f32[32,512]{1,0:T(8,128)S(1)}, u32[]{:S(2)}, u32[]{:S(2)}) %collective-permute-start.4) | collective-permute-done | bytes 65568 | tf_op jit(solution)/shard_map/ppermute | solution.py:238
  23.3 2.9 %collective-permute-done.5.refs_1_ = f32[32,512]{1,0:T(8,128)S(1)} collective-permute-done((f32[32,512]{1,0:T(8,128)S(1)}, f32[32,512]{1,0:T(8,128)S(1)}, u32[]{:S(2)}, u32[]{:S(2)}) %collective-permute-start.5) | collective-permute-done | bytes 65568 | tf_op jit(solution)/shard_map/ppermute | solution.py:238
  26.1 4.0 %collective-permute-start.7 = (f32[32,512]{1,0:T(8,128)S(1)}, f32[32,512]{1,0:T(8,128)S(1)}, u32[]{:S(2)}, u32[]{:S(2)}) collective-permute-start(f32[32,512]{1,0:T(8,128)S(1)} %added.8.refs_3_), channel_id=1, source_target_pairs={{0,16},{8,24},{16,0},{24,8},{32,48},{40,56},{48,32},{56,40},{64,80... | collective-permute-start | bytes 196616 | tf_op jit(solution)/shard_map/ppermute | solution.py:238
  31.1 1.3 %collective-permute-done.7.refs_0_ = f32[32,512]{1,0:T(8,128)S(1)} collective-permute-done((f32[32,512]{1,0:T(8,128)S(1)}, f32[32,512]{1,0:T(8,128)S(1)}, u32[]{:S(2)}, u32[]{:S(2)}) %collective-permute-start.7) | collective-permute-done | bytes 65568 | tf_op jit(solution)/shard_map/ppermute | solution.py:238
  32.5 3.1 %collective-permute-done.8.refs_1_ = f32[32,512]{1,0:T(8,128)S(1)} collective-permute-done((f32[32,512]{1,0:T(8,128)S(1)}, f32[32,512]{1,0:T(8,128)S(1)}, u32[]{:S(2)}, u32[]{:S(2)}) %collective-permute-start.8) | collective-permute-done | bytes 65568 | tf_op jit(solution)/shard_map/ppermute | solution.py:238
  35.7 1.2 %collective-permute-done.10.other = f32[32,512]{1,0:T(8,128)S(1)} collective-permute-done((f32[32,512]{1,0:T(8,128)S(1)}, f32[32,512]{1,0:T(8,128)S(1)}, u32[]{:S(2)}, u32[]{:S(2)}) %collective-permute-start.10) | collective-permute-done | bytes 65568 | tf_op jit(solution)/shard_map/ppermute | solution.py:238
  36.9 2.1 %project.1 = (f32[32,128]{1,0:T(8,128)}, bf16[32,1024]{1,0:T(8,128)(2,1)S(1)}, bf16[32,896]{1,0:T(8,128)(2,1)S(1)}, bf16[32,896]{1,0:T(8,128)(2,1)S(1)}, bf16[32,896]{1,0:T(8,128)(2,1)S(1)}) custom-call(f32[32,512]{1,0:T(8,128)S(1)} %added.9.mine, f32[32,512]{1,0:T(8,128)S(1)} %collective-permute-done.10.other, ...), custom_call_target="tpu_custom_call" | custom-call | tf_op jit(solution)/shard_map/project/pallas_call | solution.py:151
  39.1 2.0 %collective-permute-start.11 = (bf16[32,896]{1,0:T(8,128)(2,1)S(1)}, bf16[32,896]{1,0:T(8,128)(2,1)S(1)}, u32[]{:S(2)}, u32[]{:S(2)}) collective-permute-start(bf16[32,896]{1,0:T(8,128)(2,1)S(1)} %get-tuple-element.20), channel_id=1, source_target_pairs={{0,16},{8,24},{16,0},{24,8},{32,48},{40,56},{48,32},{56,40},{64,80... | collective-permute-start | bytes 172040 | tf_op jit(solution)/shard_map/ppermute | solution.py:238
  42.6 2.2 %collective-permute-done.11._.refs_0_ = bf16[32,896]{1,0:T(8,128)(2,1)S(1)} collective-permute-done((bf16[32,896]{1,0:T(8,128)(2,1)S(1)}, bf16[32,896]{1,0:T(8,128)(2,1)S(1)}, u32[]{:S(2)}, u32[]{:S(2)}) %collective-permute-start.11) | collective-permute-done | bytes 57376 | tf_op jit(solution)/shard_map/ppermute | solution.py:238
  45.2 1.2 %collective-permute-done.12.refs_1_ = bf16[32,896]{1,0:T(8,128)(2,1)S(1)} collective-permute-done((bf16[32,896]{1,0:T(8,128)(2,1)S(1)}, bf16[32,896]{1,0:T(8,128)(2,1)S(1)}, u32[]{:S(2)}, u32[]{:S(2)}) %collective-permute-start.12) | collective-permute-done | bytes 57376 | tf_op jit(solution)/shard_map/ppermute | solution.py:238
  46.4 1.6 %collective-permute-start.14 = (bf16[32,896]{1,0:T(8,128)(2,1)S(1)}, bf16[32,896]{1,0:T(8,128)(2,1)S(1)}, u32[]{:S(2)}, u32[]{:S(2)}) collective-permute-start(bf16[32,896]{1,0:T(8,128)(2,1)S(1)} %added.10.refs_3_), channel_id=1, source_target_pairs={{0,64},{8,72},{16,80},{24,88},{32,96},{40,104},{48,112},{56,120},{... | collective-permute-start | bytes 172040 | tf_op jit(solution)/shard_map/ppermute | solution.py:238
  50.0 2.8 %collective-permute-done.14.refs_0_ = bf16[32,896]{1,0:T(8,128)(2,1)S(1)} collective-permute-done((bf16[32,896]{1,0:T(8,128)(2,1)S(1)}, bf16[32,896]{1,0:T(8,128)(2,1)S(1)}, u32[]{:S(2)}, u32[]{:S(2)}) %collective-permute-start.14) | collective-permute-done | bytes 57376 | tf_op jit(solution)/shard_map/ppermute | solution.py:238
  53.5 1.9 %collective-permute-start.19 = (bf16[32,896]{1,0:T(8,128)(2,1)S(1)}, bf16[32,896]{1,0:T(8,128)(2,1)S(1)}, u32[]{:S(2)}, u32[]{:S(2)}) collective-permute-start(bf16[32,896]{1,0:T(8,128)(2,1)S(1)} %added.11.refs_0_), channel_id=1, source_target_pairs={{0,16},{8,24},{16,0},{24,8},{32,48},{40,56},{48,32},{56,40},{64,80... | collective-permute-start | bytes 172040 | tf_op jit(solution)/shard_map/ppermute | solution.py:238
  55.4 1.2 %collective-permute-start.17 = (bf16[32,896]{1,0:T(8,128)(2,1)S(1)}, bf16[32,896]{1,0:T(8,128)(2,1)S(1)}, u32[]{:S(2)}, u32[]{:S(2)}) collective-permute-start(bf16[32,896]{1,0:T(8,128)(2,1)S(1)} %added.11.refs_0_), channel_id=1, source_target_pairs={{0,24},{8,16},{16,8},{24,0},{32,56},{40,48},{48,40},{56,32},{64,88... | collective-permute-start | bytes 172040 | tf_op jit(solution)/shard_map/ppermute | solution.py:238
  57.0 1.5 %subtract.3 = (bf16[1,1024,3584]{2,1,0:T(8,128)(2,1)}, f32[32,3584]{1,0:T(8,128)}) custom-call(bf16[32,896]{1,0:T(8,128)(2,1)S(1)} %added.11.refs_0_, bf16[32,1024]{1,0:T(8,128)(2,1)S(1)} %get-tuple-element.23.p_b.refs_1_.refs_2_, bf16[1024,3584]{1,0:T(8,128)(2,1)S(1)} %get-tuple-element.19.matrix.refs_2_.refs_3_), custom_call_target="tpu_custom_call" | custom-call | flops 58720256 | bytes 1835008 | tf_op jit(solution)/shard_map/subtract/pallas_call | solution.py:198
  59.2 1.5 %subtract.4 = (bf16[1,1024,3584]{2,1,0:T(8,128)(2,1)}, f32[32,3584]{1,0:T(8,128)}) custom-call(bf16[32,896]{1,0:T(8,128)(2,1)S(1)} %collective-permute-done.19.refs_0_, bf16[32,1024]{1,0:T(8,128)(2,1)S(1)} %get-tuple-element.23.p_b.refs_1_.refs_2_, ...), custom_call_target="tpu_custom_call", output_to_operand_aliasing={{0}: (3, {}), {1}: (4, {})} | custom-call | flops 58720256 | bytes 1835008 | tf_op jit(solution)/shard_map/subtract/pallas_call | solution.py:198
  60.8 2.3 %subtract.5 = (bf16[1,1024,3584]{2,1,0:T(8,128)(2,1)}, f32[32,3584]{1,0:T(8,128)}) custom-call(bf16[32,896]{1,0:T(8,128)(2,1)S(1)} %collective-permute-done.17.refs_0_, bf16[32,896]{1,0:T(8,128)(2,1)S(1)} %collective-permute-done.18.refs_1_, ...), custom_call_target="tpu_custom_call", output_to_operand_aliasing={{0}: (4, {}), {1}: (5, {})} | custom-call | flops 117440512 | bytes 3670016 | tf_op jit(solution)/shard_map/subtract/pallas_call | solution.py:198
  (30 shorter events, 9.1 us)
Async XLA Ops:
  0.6 1.0 %copy-start = (f32[3584,32]{0,1:T(8,128)S(1)}, f32[3584,32]{0,1:T(8,128)}, u32[]{:S(2)}) copy-start(f32[3584,32]{0,1:T(8,128)} %param.5) | copy-start | bytes 1376260
  7.3 1.3 %collective-permute-start = (f32[32,512]{1,0:T(8,128)S(1)}, f32[32,512]{1,0:T(8,128)S(1)}, u32[]{:S(2)}, u32[]{:S(2)}) collective-permute-start(f32[32,512]{1,0:T(8,128)S(1)} %get-tuple-element.18), channel_id=1, source_target_pairs={{0,1},{1,0},{2,3},{3,2},{4,5},{5,4},{6,7},{7,6},{8,9},{9,8},{10,11... | collective-permute-start | bytes 196616 | tf_op jit(solution)/shard_map/ppermute | solution.py:238
  8.7 5.8 %collective-permute-start.1 = (f32[32,512]{1,0:T(8,128)S(1)}, f32[32,512]{1,0:T(8,128)S(1)}, u32[]{:S(2)}, u32[]{:S(2)}) collective-permute-start(f32[32,512]{1,0:T(8,128)S(1)} %added.6.refs_3_), channel_id=1, source_target_pairs={{0,4},{1,5},{2,6},{3,7},{4,0},{5,1},{6,2},{7,3},{8,12},{9,13},{10,... | collective-permute-start | bytes 196616 | tf_op jit(solution)/shard_map/ppermute | solution.py:238
  11.9 5.5 %collective-permute-start.2 = (f32[32,512]{1,0:T(8,128)S(1)}, f32[32,512]{1,0:T(8,128)S(1)}, u32[]{:S(2)}, u32[]{:S(2)}) collective-permute-start(f32[32,512]{1,0:T(8,128)S(1)} %added.6.refs_3_), channel_id=1, source_target_pairs={{0,6},{1,7},{2,4},{3,5},{4,2},{5,3},{6,0},{7,1},{8,14},{9,15},{10,... | collective-permute-start | bytes 196616 | tf_op jit(solution)/shard_map/ppermute | solution.py:238
  13.0 4.3 %collective-permute-start.3 = (f32[32,512]{1,0:T(8,128)S(1)}, f32[32,512]{1,0:T(8,128)S(1)}, u32[]{:S(2)}, u32[]{:S(2)}) collective-permute-start(f32[32,512]{1,0:T(8,128)S(1)} %added.6.refs_3_), channel_id=1, source_target_pairs={{0,2},{1,3},{2,0},{3,1},{4,6},{5,7},{6,4},{7,5},{8,10},{9,11},{10,... | collective-permute-start | bytes 196616 | tf_op jit(solution)/shard_map/ppermute | solution.py:238
  17.4 5.9 %collective-permute-start.4 = (f32[32,512]{1,0:T(8,128)S(1)}, f32[32,512]{1,0:T(8,128)S(1)}, u32[]{:S(2)}, u32[]{:S(2)}) collective-permute-start(f32[32,512]{1,0:T(8,128)S(1)} %added.7.refs_3_), channel_id=1, source_target_pairs={{0,64},{8,72},{16,80},{24,88},{32,96},{40,104},{48,112},{56,120},{... | collective-permute-start | bytes 196616 | tf_op jit(solution)/shard_map/ppermute | solution.py:238
  20.6 5.5 %collective-permute-start.5 = (f32[32,512]{1,0:T(8,128)S(1)}, f32[32,512]{1,0:T(8,128)S(1)}, u32[]{:S(2)}, u32[]{:S(2)}) collective-permute-start(f32[32,512]{1,0:T(8,128)S(1)} %added.7.refs_3_), channel_id=1, source_target_pairs={{0,96},{8,104},{16,112},{24,120},{32,64},{40,72},{48,80},{56,88},{... | collective-permute-start | bytes 196616 | tf_op jit(solution)/shard_map/ppermute | solution.py:238
  21.7 4.4 %collective-permute-start.6 = (f32[32,512]{1,0:T(8,128)S(1)}, f32[32,512]{1,0:T(8,128)S(1)}, u32[]{:S(2)}, u32[]{:S(2)}) collective-permute-start(f32[32,512]{1,0:T(8,128)S(1)} %added.7.refs_3_), channel_id=1, source_target_pairs={{0,32},{8,40},{16,48},{24,56},{32,0},{40,8},{48,16},{56,24},{64,96... | collective-permute-start | bytes 196616 | tf_op jit(solution)/shard_map/ppermute | solution.py:238
  26.1 6.3 %collective-permute-start.7 = (f32[32,512]{1,0:T(8,128)S(1)}, f32[32,512]{1,0:T(8,128)S(1)}, u32[]{:S(2)}, u32[]{:S(2)}) collective-permute-start(f32[32,512]{1,0:T(8,128)S(1)} %added.8.refs_3_), channel_id=1, source_target_pairs={{0,16},{8,24},{16,0},{24,8},{32,48},{40,56},{48,32},{56,40},{64,80... | collective-permute-start | bytes 196616 | tf_op jit(solution)/shard_map/ppermute | solution.py:238
  30.1 5.5 %collective-permute-start.8 = (f32[32,512]{1,0:T(8,128)S(1)}, f32[32,512]{1,0:T(8,128)S(1)}, u32[]{:S(2)}, u32[]{:S(2)}) collective-permute-start(f32[32,512]{1,0:T(8,128)S(1)} %added.8.refs_3_), channel_id=1, source_target_pairs={{0,24},{8,16},{16,8},{24,0},{32,56},{40,48},{48,40},{56,32},{64,88... | collective-permute-start | bytes 196616 | tf_op jit(solution)/shard_map/ppermute | solution.py:238
  30.8 4.8 %collective-permute-start.9 = (f32[32,512]{1,0:T(8,128)S(1)}, f32[32,512]{1,0:T(8,128)S(1)}, u32[]{:S(2)}, u32[]{:S(2)}) collective-permute-start(f32[32,512]{1,0:T(8,128)S(1)} %added.8.refs_3_), channel_id=1, source_target_pairs={{0,8},{8,0},{16,24},{24,16},{32,40},{40,32},{48,56},{56,48},{64,72... | collective-permute-start | bytes 196616 | tf_op jit(solution)/shard_map/ppermute | solution.py:238
  35.6 1.3 %collective-permute-start.10 = (f32[32,512]{1,0:T(8,128)S(1)}, f32[32,512]{1,0:T(8,128)S(1)}, u32[]{:S(2)}, u32[]{:S(2)}) collective-permute-start(f32[32,512]{1,0:T(8,128)S(1)} %added.9.mine), channel_id=1, source_target_pairs={{0,1},{1,0},{2,3},{3,2},{4,5},{5,4},{6,7},{7,6},{8,9},{9,8},{10,11... | collective-permute-start | bytes 196616 | tf_op jit(solution)/shard_map/ppermute | solution.py:238
  39.1 5.8 %collective-permute-start.11 = (bf16[32,896]{1,0:T(8,128)(2,1)S(1)}, bf16[32,896]{1,0:T(8,128)(2,1)S(1)}, u32[]{:S(2)}, u32[]{:S(2)}) collective-permute-start(bf16[32,896]{1,0:T(8,128)(2,1)S(1)} %get-tuple-element.20), channel_id=1, source_target_pairs={{0,16},{8,24},{16,0},{24,8},{32,48},{40,56},{48,32},{56,40},{64,80... | collective-permute-start | bytes 172040 | tf_op jit(solution)/shard_map/ppermute | solution.py:238
  41.0 5.4 %collective-permute-start.12 = (bf16[32,896]{1,0:T(8,128)(2,1)S(1)}, bf16[32,896]{1,0:T(8,128)(2,1)S(1)}, u32[]{:S(2)}, u32[]{:S(2)}) collective-permute-start(bf16[32,896]{1,0:T(8,128)(2,1)S(1)} %get-tuple-element.21), channel_id=1, source_target_pairs={{0,24},{8,16},{16,8},{24,0},{32,56},{40,48},{48,40},{56,32},{64,88... | collective-permute-start | bytes 172040 | tf_op jit(solution)/shard_map/ppermute | solution.py:238
  41.6 4.8 %collective-permute-start.13 = (bf16[32,896]{1,0:T(8,128)(2,1)S(1)}, bf16[32,896]{1,0:T(8,128)(2,1)S(1)}, u32[]{:S(2)}, u32[]{:S(2)}) collective-permute-start(bf16[32,896]{1,0:T(8,128)(2,1)S(1)} %get-tuple-element.22), channel_id=1, source_target_pairs={{0,8},{8,0},{16,24},{24,16},{32,40},{40,32},{48,56},{56,48},{64,72... | collective-permute-start | bytes 172040 | tf_op jit(solution)/shard_map/ppermute | solution.py:238
  46.4 6.3 %collective-permute-start.14 = (bf16[32,896]{1,0:T(8,128)(2,1)S(1)}, bf16[32,896]{1,0:T(8,128)(2,1)S(1)}, u32[]{:S(2)}, u32[]{:S(2)}) collective-permute-start(bf16[32,896]{1,0:T(8,128)(2,1)S(1)} %added.10.refs_3_), channel_id=1, source_target_pairs={{0,64},{8,72},{16,80},{24,88},{32,96},{40,104},{48,112},{56,120},{... | collective-permute-start | bytes 172040 | tf_op jit(solution)/shard_map/ppermute | solution.py:238
  48.0 5.4 %collective-permute-start.15 = (bf16[32,896]{1,0:T(8,128)(2,1)S(1)}, bf16[32,896]{1,0:T(8,128)(2,1)S(1)}, u32[]{:S(2)}, u32[]{:S(2)}) collective-permute-start(bf16[32,896]{1,0:T(8,128)(2,1)S(1)} %added.10.refs_3_), channel_id=1, source_target_pairs={{0,96},{8,104},{16,112},{24,120},{32,64},{40,72},{48,80},{56,88},{... | collective-permute-start | bytes 172040 | tf_op jit(solution)/shard_map/ppermute | solution.py:238
  49.0 4.4 %collective-permute-start.16 = (bf16[32,896]{1,0:T(8,128)(2,1)S(1)}, bf16[32,896]{1,0:T(8,128)(2,1)S(1)}, u32[]{:S(2)}, u32[]{:S(2)}) collective-permute-start(bf16[32,896]{1,0:T(8,128)(2,1)S(1)} %added.10.refs_3_), channel_id=1, source_target_pairs={{0,32},{8,40},{16,48},{24,56},{32,0},{40,8},{48,16},{56,24},{64,96... | collective-permute-start | bytes 172040 | tf_op jit(solution)/shard_map/ppermute | solution.py:238
  53.5 5.8 %collective-permute-start.19 = (bf16[32,896]{1,0:T(8,128)(2,1)S(1)}, bf16[32,896]{1,0:T(8,128)(2,1)S(1)}, u32[]{:S(2)}, u32[]{:S(2)}) collective-permute-start(bf16[32,896]{1,0:T(8,128)(2,1)S(1)} %added.11.refs_0_), channel_id=1, source_target_pairs={{0,16},{8,24},{16,0},{24,8},{32,48},{40,56},{48,32},{56,40},{64,80... | collective-permute-start | bytes 172040 | tf_op jit(solution)/shard_map/ppermute | solution.py:238
  55.4 5.4 %collective-permute-start.17 = (bf16[32,896]{1,0:T(8,128)(2,1)S(1)}, bf16[32,896]{1,0:T(8,128)(2,1)S(1)}, u32[]{:S(2)}, u32[]{:S(2)}) collective-permute-start(bf16[32,896]{1,0:T(8,128)(2,1)S(1)} %added.11.refs_0_), channel_id=1, source_target_pairs={{0,24},{8,16},{16,8},{24,0},{32,56},{40,48},{48,40},{56,32},{64,88... | collective-permute-start | bytes 172040 | tf_op jit(solution)/shard_map/ppermute | solution.py:238
  56.6 4.2 %collective-permute-start.18 = (bf16[32,896]{1,0:T(8,128)(2,1)S(1)}, bf16[32,896]{1,0:T(8,128)(2,1)S(1)}, u32[]{:S(2)}, u32[]{:S(2)}) collective-permute-start(bf16[32,896]{1,0:T(8,128)(2,1)S(1)} %added.11.refs_0_), channel_id=1, source_target_pairs={{0,8},{8,0},{16,24},{24,16},{32,40},{40,32},{48,56},{56,48},{64,72... | collective-permute-start | bytes 172040 | tf_op jit(solution)/shard_map/ppermute | solution.py:238

commit v14 on v13

--- a/solution.py
+++ b/solution.py
@@ -254,7 +254,7 @@
     (q_own,) = rest(p_b, matrix, two)
     q_sum = summed_over_four(added(two, three, one, q_own), "dp", 4)
     mean, earlier = 1.0 / lax.axis_size("dp"), ()
-    for distances in ((0,), (2,), (3, 1)):
+    for distances in ((0,), (2, 1), (3,)):
         q_now = [swapped(q_sum, "dp", 1, distance) if distance else q_sum for distance in distances]
         earlier = subtract(q_now, p_b, matrix, mean, distances, earlier)
     new_errors, q_out = earlier

time: 63.2 us -> 67 us (1.060)
  starting transfers between devices: 24.5 us -> 27.4 us
  waiting for transfers between devices: 23.1 us -> 24 us
    ppermute x20, starting transfers between devices: 24.5 us -> 27.4 us  [swapped(): lax.ppermute(value, axis, [(i, i ^ distance * stride) for i in range(lax....]
    ppermute x20, waiting for transfers between devices: 23.1 us -> 24 us  [swapped(): lax.ppermute(value, axis, [(i, i ^ distance * stride) for i in range(lax....]
  transfers between devices with their start and end apart: 20 -> 20, of which waited for: 13 -> 14; matrix products, arithmetic and copies ran while one was open for 0% -> 0% of each run, Pallas kernels for 6% -> 6%
where the time goes in v14:
time: 67 us; the launch traced here: 66.9 us
  starting transfers between devices  27.4 us (41%)
  waiting for transfers between devices  24 us (36%)
  Pallas kernels  13.7 us (20%)
  local copies, waits for them, and re-layouts  1.01 us (2%)
  between operations  0.76 us (1%)
    ppermute x20, starting transfers between devices, swapped(): lax.ppermute(value, axis, [(i, i ^ distance * stride) for i in range(lax....  27.4 us
    ppermute x20, waiting for transfers between devices, swapped(): lax.ppermute(value, axis, [(i, i ^ distance * stride) for i in range(lax....  24 us
    pallas_call x1, Pallas kernels, merge(): pl.pallas_call(merge_kernel, out_shape=(jax.ShapeDtypeStruct((rows, cols)...  5.68 us
    pallas_call x3, Pallas kernels, subtract(): pl.pallas_call(functools.partial(subtract_kernel, mean, distances), out_s...  5.37 us
    pallas_call x1, Pallas kernels, project(): pl.pallas_call(project_kernel, out_shape=(jax.ShapeDtypeStruct((rank, LAN...  2.1 us
  transfers between devices with their start and end apart: 20, of which 14 were waited for; matrix products, arithmetic and copies ran while one was open for 0% of the time, Pallas kernels for 6%

profile of v14, /device:TPU:0, one launch (start us, length us, event | category | flops | bytes accessed | tf_op | source)
XLA Modules:
  0.0 66.9 jit_solution(6688525555947701511)
XLA Ops:
  1.6 5.7 %merge.1 = (bf16[1024,3584]{1,0:T(8,128)(2,1)S(1)}, f32[32,512]{1,0:T(8,128)S(1)}, f32[32,512]{1,0:T(8,128)S(1)}) custom-call(bf16[1,1024,3584]{2,1,0:T(8,128)(2,1)} %grads.1, bf16[1,1024,3584]{2,1,0:T(8,128)(2,1)} %errors.1, f32[32,3584]{1,0:T(8,128)S(1)} %bitcast.3), custom_call_target="tpu_custom_call" | custom-call | tf_op jit(solution)/shard_map/merge/pallas_call | solution.py:60
  7.4 1.2 %collective-permute-done.refs_1_ = f32[32,512]{1,0:T(8,128)S(1)} collective-permute-done((f32[32,512]{1,0:T(8,128)S(1)}, f32[32,512]{1,0:T(8,128)S(1)}, u32[]{:S(2)}, u32[]{:S(2)}) %collective-permute-start) | collective-permute-done | bytes 65568 | tf_op jit(solution)/shard_map/ppermute | solution.py:238
  8.7 1.7 %collective-permute-start.3 = (f32[32,512]{1,0:T(8,128)S(1)}, f32[32,512]{1,0:T(8,128)S(1)}, u32[]{:S(2)}, u32[]{:S(2)}) collective-permute-start(f32[32,512]{1,0:T(8,128)S(1)} %added.6.refs_3_), channel_id=1, source_target_pairs={{0,2},{1,3},{2,0},{3,1},{4,6},{5,7},{6,4},{7,5},{8,10},{9,11},{10,... | collective-permute-start | bytes 196616 | tf_op jit(solution)/shard_map/ppermute | solution.py:238
  10.3 2.1 %collective-permute-start.2 = (f32[32,512]{1,0:T(8,128)S(1)}, f32[32,512]{1,0:T(8,128)S(1)}, u32[]{:S(2)}, u32[]{:S(2)}) collective-permute-start(f32[32,512]{1,0:T(8,128)S(1)} %added.6.refs_3_), channel_id=1, source_target_pairs={{0,6},{1,7},{2,4},{3,5},{4,2},{5,3},{6,0},{7,1},{8,14},{9,15},{10,... | collective-permute-start | bytes 196616 | tf_op jit(solution)/shard_map/ppermute | solution.py:238
  13.1 2.7 %collective-permute-done.2.refs_1_ = f32[32,512]{1,0:T(8,128)S(1)} collective-permute-done((f32[32,512]{1,0:T(8,128)S(1)}, f32[32,512]{1,0:T(8,128)S(1)}, u32[]{:S(2)}, u32[]{:S(2)}) %collective-permute-start.2) | collective-permute-done | bytes 65568 | tf_op jit(solution)/shard_map/ppermute | solution.py:238
  15.8 2.4 %collective-permute-done.1.refs_0_ = f32[32,512]{1,0:T(8,128)S(1)} collective-permute-done((f32[32,512]{1,0:T(8,128)S(1)}, f32[32,512]{1,0:T(8,128)S(1)}, u32[]{:S(2)}, u32[]{:S(2)}) %collective-permute-start.1) | collective-permute-done | bytes 65568 | tf_op jit(solution)/shard_map/ppermute | solution.py:238
  18.2 1.7 %collective-permute-start.6 = (f32[32,512]{1,0:T(8,128)S(1)}, f32[32,512]{1,0:T(8,128)S(1)}, u32[]{:S(2)}, u32[]{:S(2)}) collective-permute-start(f32[32,512]{1,0:T(8,128)S(1)} %added.7.refs_3_), channel_id=1, source_target_pairs={{0,32},{8,40},{16,48},{24,56},{32,0},{40,8},{48,16},{56,24},{64,96... | collective-permute-start | bytes 196616 | tf_op jit(solution)/shard_map/ppermute | solution.py:238
  19.9 2.2 %collective-permute-start.5 = (f32[32,512]{1,0:T(8,128)S(1)}, f32[32,512]{1,0:T(8,128)S(1)}, u32[]{:S(2)}, u32[]{:S(2)}) collective-permute-start(f32[32,512]{1,0:T(8,128)S(1)} %added.7.refs_3_), channel_id=1, source_target_pairs={{0,96},{8,104},{16,112},{24,120},{32,64},{40,72},{48,80},{56,88},{... | collective-permute-start | bytes 196616 | tf_op jit(solution)/shard_map/ppermute | solution.py:238
  22.8 2.8 %collective-permute-done.5.refs_1_ = f32[32,512]{1,0:T(8,128)S(1)} collective-permute-done((f32[32,512]{1,0:T(8,128)S(1)}, f32[32,512]{1,0:T(8,128)S(1)}, u32[]{:S(2)}, u32[]{:S(2)}) %collective-permute-start.5) | collective-permute-done | bytes 65568 | tf_op jit(solution)/shard_map/ppermute | solution.py:238
  25.6 2.2 %collective-permute-done.4.refs_0_ = f32[32,512]{1,0:T(8,128)S(1)} collective-permute-done((f32[32,512]{1,0:T(8,128)S(1)}, f32[32,512]{1,0:T(8,128)S(1)}, u32[]{:S(2)}, u32[]{:S(2)}) %collective-permute-start.4) | collective-permute-done | bytes 65568 | tf_op jit(solution)/shard_map/ppermute | solution.py:238
  27.9 2.0 %collective-permute-start.9 = (f32[32,512]{1,0:T(8,128)S(1)}, f32[32,512]{1,0:T(8,128)S(1)}, u32[]{:S(2)}, u32[]{:S(2)}) collective-permute-start(f32[32,512]{1,0:T(8,128)S(1)} %added.8.refs_3_), channel_id=1, source_target_pairs={{0,8},{8,0},{16,24},{24,16},{32,40},{40,32},{48,56},{56,48},{64,72... | collective-permute-start | bytes 196616 | tf_op jit(solution)/shard_map/ppermute | solution.py:238
  29.9 2.5 %collective-permute-start.8 = (f32[32,512]{1,0:T(8,128)S(1)}, f32[32,512]{1,0:T(8,128)S(1)}, u32[]{:S(2)}, u32[]{:S(2)}) collective-permute-start(f32[32,512]{1,0:T(8,128)S(1)} %added.8.refs_3_), channel_id=1, source_target_pairs={{0,24},{8,16},{16,8},{24,0},{32,56},{40,48},{48,40},{56,32},{64,88... | collective-permute-start | bytes 196616 | tf_op jit(solution)/shard_map/ppermute | solution.py:238
  33.4 1.9 %collective-permute-done.8.refs_1_ = f32[32,512]{1,0:T(8,128)S(1)} collective-permute-done((f32[32,512]{1,0:T(8,128)S(1)}, f32[32,512]{1,0:T(8,128)S(1)}, u32[]{:S(2)}, u32[]{:S(2)}) %collective-permute-start.8) | collective-permute-done | bytes 65568 | tf_op jit(solution)/shard_map/ppermute | solution.py:238
  35.3 2.8 %collective-permute-done.7.refs_0_ = f32[32,512]{1,0:T(8,128)S(1)} collective-permute-done((f32[32,512]{1,0:T(8,128)S(1)}, f32[32,512]{1,0:T(8,128)S(1)}, u32[]{:S(2)}, u32[]{:S(2)}) %collective-permute-start.7) | collective-permute-done | bytes 65568 | tf_op jit(solution)/shard_map/ppermute | solution.py:238
  39.5 2.1 %project.1 = (f32[32,128]{1,0:T(8,128)}, bf16[32,1024]{1,0:T(8,128)(2,1)S(1)}, bf16[32,896]{1,0:T(8,128)(2,1)S(1)}, bf16[32,896]{1,0:T(8,128)(2,1)S(1)}, bf16[32,896]{1,0:T(8,128)(2,1)S(1)}) custom-call(f32[32,512]{1,0:T(8,128)S(1)} %added.9.mine, f32[32,512]{1,0:T(8,128)S(1)} %collective-permute-done.10.other, ...), custom_call_target="tpu_custom_call" | custom-call | tf_op jit(solution)/shard_map/project/pallas_call | solution.py:151
  42.8 2.6 %collective-permute-start.12 = (bf16[32,896]{1,0:T(8,128)(2,1)S(1)}, bf16[32,896]{1,0:T(8,128)(2,1)S(1)}, u32[]{:S(2)}, u32[]{:S(2)}) collective-permute-start(bf16[32,896]{1,0:T(8,128)(2,1)S(1)} %get-tuple-element.21), channel_id=1, source_target_pairs={{0,24},{8,16},{16,8},{24,0},{32,56},{40,48},{48,40},{56,32},{64,88... | collective-permute-start | bytes 172040 | tf_op jit(solution)/shard_map/ppermute | solution.py:238
  45.4 2.0 %collective-permute-done.11._.refs_0_ = bf16[32,896]{1,0:T(8,128)(2,1)S(1)} collective-permute-done((bf16[32,896]{1,0:T(8,128)(2,1)S(1)}, bf16[32,896]{1,0:T(8,128)(2,1)S(1)}, u32[]{:S(2)}, u32[]{:S(2)}) %collective-permute-start.11) | collective-permute-done | bytes 57376 | tf_op jit(solution)/shard_map/ppermute | solution.py:238
  51.0 2.8 %collective-permute-start.14 = (bf16[32,896]{1,0:T(8,128)(2,1)S(1)}, bf16[32,896]{1,0:T(8,128)(2,1)S(1)}, u32[]{:S(2)}, u32[]{:S(2)}) collective-permute-start(bf16[32,896]{1,0:T(8,128)(2,1)S(1)} %added.10.refs_3_), channel_id=1, source_target_pairs={{0,64},{8,72},{16,80},{24,88},{32,96},{40,104},{48,112},{56,120},{... | collective-permute-start | bytes 172040 | tf_op jit(solution)/shard_map/ppermute | solution.py:238
  54.4 1.3 %collective-permute-done.15.refs_1_ = bf16[32,896]{1,0:T(8,128)(2,1)S(1)} collective-permute-done((bf16[32,896]{1,0:T(8,128)(2,1)S(1)}, bf16[32,896]{1,0:T(8,128)(2,1)S(1)}, u32[]{:S(2)}, u32[]{:S(2)}) %collective-permute-start.15) | collective-permute-done | bytes 57376 | tf_op jit(solution)/shard_map/ppermute | solution.py:238
  56.8 2.7 %collective-permute-start.18 = (bf16[32,896]{1,0:T(8,128)(2,1)S(1)}, bf16[32,896]{1,0:T(8,128)(2,1)S(1)}, u32[]{:S(2)}, u32[]{:S(2)}) collective-permute-start(bf16[32,896]{1,0:T(8,128)(2,1)S(1)} %added.11.refs_0_), channel_id=1, source_target_pairs={{0,16},{8,24},{16,0},{24,8},{32,48},{40,56},{48,32},{56,40},{64,80... | collective-permute-start | bytes 172040 | tf_op jit(solution)/shard_map/ppermute | solution.py:238
  59.4 2.0 %collective-permute-start.17 = (bf16[32,896]{1,0:T(8,128)(2,1)S(1)}, bf16[32,896]{1,0:T(8,128)(2,1)S(1)}, u32[]{:S(2)}, u32[]{:S(2)}) collective-permute-start(bf16[32,896]{1,0:T(8,128)(2,1)S(1)} %added.11.refs_0_), channel_id=1, source_target_pairs={{0,24},{8,16},{16,8},{24,0},{32,56},{40,48},{48,40},{56,32},{64,88... | collective-permute-start | bytes 172040 | tf_op jit(solution)/shard_map/ppermute | solution.py:238
  61.5 1.5 %subtract.3 = (bf16[1,1024,3584]{2,1,0:T(8,128)(2,1)}, f32[32,3584]{1,0:T(8,128)}) custom-call(bf16[32,896]{1,0:T(8,128)(2,1)S(1)} %added.11.refs_0_, bf16[32,1024]{1,0:T(8,128)(2,1)S(1)} %get-tuple-element.23.p_b.refs_1_.refs_2_, bf16[1024,3584]{1,0:T(8,128)(2,1)S(1)} %get-tuple-element.19.matrix.refs_2_.refs_3_), custom_call_target="tpu_custom_call" | custom-call | flops 58720256 | bytes 1835008 | tf_op jit(solution)/shard_map/subtract/pallas_call | solution.py:198
  63.0 2.3 %subtract.4 = (bf16[1,1024,3584]{2,1,0:T(8,128)(2,1)}, f32[32,3584]{1,0:T(8,128)}) custom-call(bf16[32,896]{1,0:T(8,128)(2,1)S(1)} %collective-permute-done.18.refs_0_, bf16[32,896]{1,0:T(8,128)(2,1)S(1)} %collective-permute-done.19.refs_1_, ...), custom_call_target="tpu_custom_call", output_to_operand_aliasing={{0}: (4, {}), {1}: (5, {})} | custom-call | flops 117440512 | bytes 3670016 | tf_op jit(solution)/shard_map/subtract/pallas_call | solution.py:198
  65.3 1.6 %subtract.5 = (bf16[1,1024,3584]{2,1,0:T(8,128)(2,1)}, f32[32,3584]{1,0:T(8,128)}) custom-call(bf16[32,896]{1,0:T(8,128)(2,1)S(1)} %collective-permute-done.17.refs_0_, bf16[32,1024]{1,0:T(8,128)(2,1)S(1)} %get-tuple-element.23.p_b.refs_1_.refs_2_, ...), custom_call_target="tpu_custom_call", output_to_operand_aliasing={{0}: (3, {}), {1}: (4, {})} | custom-call | flops 58720256 | bytes 1835008 | tf_op jit(solution)/shard_map/subtract/pallas_call | solution.py:198
  (30 shorter events, 11.3 us)
Async XLA Ops:
  0.6 1.0 %copy-start = (f32[3584,32]{0,1:T(8,128)S(1)}, f32[3584,32]{0,1:T(8,128)}, u32[]{:S(2)}) copy-start(f32[3584,32]{0,1:T(8,128)} %param.5) | copy-start | bytes 1376260
  7.3 1.3 %collective-permute-start = (f32[32,512]{1,0:T(8,128)S(1)}, f32[32,512]{1,0:T(8,128)S(1)}, u32[]{:S(2)}, u32[]{:S(2)}) collective-permute-start(f32[32,512]{1,0:T(8,128)S(1)} %get-tuple-element.18), channel_id=1, source_target_pairs={{0,1},{1,0},{2,3},{3,2},{4,5},{5,4},{6,7},{7,6},{8,9},{9,8},{10,11... | collective-permute-start | bytes 196616 | tf_op jit(solution)/shard_map/ppermute | solution.py:238
  8.7 4.4 %collective-permute-start.3 = (f32[32,512]{1,0:T(8,128)S(1)}, f32[32,512]{1,0:T(8,128)S(1)}, u32[]{:S(2)}, u32[]{:S(2)}) collective-permute-start(f32[32,512]{1,0:T(8,128)S(1)} %added.6.refs_3_), channel_id=1, source_target_pairs={{0,2},{1,3},{2,0},{3,1},{4,6},{5,7},{6,4},{7,5},{8,10},{9,11},{10,... | collective-permute-start | bytes 196616 | tf_op jit(solution)/shard_map/ppermute | solution.py:238
  10.3 5.5 %collective-permute-start.2 = (f32[32,512]{1,0:T(8,128)S(1)}, f32[32,512]{1,0:T(8,128)S(1)}, u32[]{:S(2)}, u32[]{:S(2)}) collective-permute-start(f32[32,512]{1,0:T(8,128)S(1)} %added.6.refs_3_), channel_id=1, source_target_pairs={{0,6},{1,7},{2,4},{3,5},{4,2},{5,3},{6,0},{7,1},{8,14},{9,15},{10,... | collective-permute-start | bytes 196616 | tf_op jit(solution)/shard_map/ppermute | solution.py:238
  12.4 5.8 %collective-permute-start.1 = (f32[32,512]{1,0:T(8,128)S(1)}, f32[32,512]{1,0:T(8,128)S(1)}, u32[]{:S(2)}, u32[]{:S(2)}) collective-permute-start(f32[32,512]{1,0:T(8,128)S(1)} %added.6.refs_3_), channel_id=1, source_target_pairs={{0,4},{1,5},{2,6},{3,7},{4,0},{5,1},{6,2},{7,3},{8,12},{9,13},{10,... | collective-permute-start | bytes 196616 | tf_op jit(solution)/shard_map/ppermute | solution.py:238
  18.2 4.6 %collective-permute-start.6 = (f32[32,512]{1,0:T(8,128)S(1)}, f32[32,512]{1,0:T(8,128)S(1)}, u32[]{:S(2)}, u32[]{:S(2)}) collective-permute-start(f32[32,512]{1,0:T(8,128)S(1)} %added.7.refs_3_), channel_id=1, source_target_pairs={{0,32},{8,40},{16,48},{24,56},{32,0},{40,8},{48,16},{56,24},{64,96... | collective-permute-start | bytes 196616 | tf_op jit(solution)/shard_map/ppermute | solution.py:238
  19.9 5.7 %collective-permute-start.5 = (f32[32,512]{1,0:T(8,128)S(1)}, f32[32,512]{1,0:T(8,128)S(1)}, u32[]{:S(2)}, u32[]{:S(2)}) collective-permute-start(f32[32,512]{1,0:T(8,128)S(1)} %added.7.refs_3_), channel_id=1, source_target_pairs={{0,96},{8,104},{16,112},{24,120},{32,64},{40,72},{48,80},{56,88},{... | collective-permute-start | bytes 196616 | tf_op jit(solution)/shard_map/ppermute | solution.py:238
  22.1 5.8 %collective-permute-start.4 = (f32[32,512]{1,0:T(8,128)S(1)}, f32[32,512]{1,0:T(8,128)S(1)}, u32[]{:S(2)}, u32[]{:S(2)}) collective-permute-start(f32[32,512]{1,0:T(8,128)S(1)} %added.7.refs_3_), channel_id=1, source_target_pairs={{0,64},{8,72},{16,80},{24,88},{32,96},{40,104},{48,112},{56,120},{... | collective-permute-start | bytes 196616 | tf_op jit(solution)/shard_map/ppermute | solution.py:238
  27.9 5.6 %collective-permute-start.9 = (f32[32,512]{1,0:T(8,128)S(1)}, f32[32,512]{1,0:T(8,128)S(1)}, u32[]{:S(2)}, u32[]{:S(2)}) collective-permute-start(f32[32,512]{1,0:T(8,128)S(1)} %added.8.refs_3_), channel_id=1, source_target_pairs={{0,8},{8,0},{16,24},{24,16},{32,40},{40,32},{48,56},{56,48},{64,72... | collective-permute-start | bytes 196616 | tf_op jit(solution)/shard_map/ppermute | solution.py:238
  29.9 5.5 %collective-permute-start.8 = (f32[32,512]{1,0:T(8,128)S(1)}, f32[32,512]{1,0:T(8,128)S(1)}, u32[]{:S(2)}, u32[]{:S(2)}) collective-permute-start(f32[32,512]{1,0:T(8,128)S(1)} %added.8.refs_3_), channel_id=1, source_target_pairs={{0,24},{8,16},{16,8},{24,0},{32,56},{40,48},{48,40},{56,32},{64,88... | collective-permute-start | bytes 196616 | tf_op jit(solution)/shard_map/ppermute | solution.py:238
  32.4 5.8 %collective-permute-start.7 = (f32[32,512]{1,0:T(8,128)S(1)}, f32[32,512]{1,0:T(8,128)S(1)}, u32[]{:S(2)}, u32[]{:S(2)}) collective-permute-start(f32[32,512]{1,0:T(8,128)S(1)} %added.8.refs_3_), channel_id=1, source_target_pairs={{0,16},{8,24},{16,0},{24,8},{32,48},{40,56},{48,32},{56,40},{64,80... | collective-permute-start | bytes 196616 | tf_op jit(solution)/shard_map/ppermute | solution.py:238
  38.2 1.3 %collective-permute-start.10 = (f32[32,512]{1,0:T(8,128)S(1)}, f32[32,512]{1,0:T(8,128)S(1)}, u32[]{:S(2)}, u32[]{:S(2)}) collective-permute-start(f32[32,512]{1,0:T(8,128)S(1)} %added.9.mine), channel_id=1, source_target_pairs={{0,1},{1,0},{2,3},{3,2},{4,5},{5,4},{6,7},{7,6},{8,9},{9,8},{10,11... | collective-permute-start | bytes 196616 | tf_op jit(solution)/shard_map/ppermute | solution.py:238
  41.6 5.8 %collective-permute-start.11 = (bf16[32,896]{1,0:T(8,128)(2,1)S(1)}, bf16[32,896]{1,0:T(8,128)(2,1)S(1)}, u32[]{:S(2)}, u32[]{:S(2)}) collective-permute-start(bf16[32,896]{1,0:T(8,128)(2,1)S(1)} %get-tuple-element.20), channel_id=1, source_target_pairs={{0,16},{8,24},{16,0},{24,8},{32,48},{40,56},{48,32},{56,40},{64,80... | collective-permute-start | bytes 172040 | tf_op jit(solution)/shard_map/ppermute | solution.py:238
  42.8 5.7 %collective-permute-start.12 = (bf16[32,896]{1,0:T(8,128)(2,1)S(1)}, bf16[32,896]{1,0:T(8,128)(2,1)S(1)}, u32[]{:S(2)}, u32[]{:S(2)}) collective-permute-start(bf16[32,896]{1,0:T(8,128)(2,1)S(1)} %get-tuple-element.21), channel_id=1, source_target_pairs={{0,24},{8,16},{16,8},{24,0},{32,56},{40,48},{48,40},{56,32},{64,88... | collective-permute-start | bytes 172040 | tf_op jit(solution)/shard_map/ppermute | solution.py:238
  45.4 4.2 %collective-permute-start.13 = (bf16[32,896]{1,0:T(8,128)(2,1)S(1)}, bf16[32,896]{1,0:T(8,128)(2,1)S(1)}, u32[]{:S(2)}, u32[]{:S(2)}) collective-permute-start(bf16[32,896]{1,0:T(8,128)(2,1)S(1)} %get-tuple-element.22), channel_id=1, source_target_pairs={{0,8},{8,0},{16,24},{24,16},{32,40},{40,32},{48,56},{56,48},{64,72... | collective-permute-start | bytes 172040 | tf_op jit(solution)/shard_map/ppermute | solution.py:238
  49.6 4.8 %collective-permute-start.16 = (bf16[32,896]{1,0:T(8,128)(2,1)S(1)}, bf16[32,896]{1,0:T(8,128)(2,1)S(1)}, u32[]{:S(2)}, u32[]{:S(2)}) collective-permute-start(bf16[32,896]{1,0:T(8,128)(2,1)S(1)} %added.10.refs_3_), channel_id=1, source_target_pairs={{0,32},{8,40},{16,48},{24,56},{32,0},{40,8},{48,16},{56,24},{64,96... | collective-permute-start | bytes 172040 | tf_op jit(solution)/shard_map/ppermute | solution.py:238
  50.4 5.4 %collective-permute-start.15 = (bf16[32,896]{1,0:T(8,128)(2,1)S(1)}, bf16[32,896]{1,0:T(8,128)(2,1)S(1)}, u32[]{:S(2)}, u32[]{:S(2)}) collective-permute-start(bf16[32,896]{1,0:T(8,128)(2,1)S(1)} %added.10.refs_3_), channel_id=1, source_target_pairs={{0,96},{8,104},{16,112},{24,120},{32,64},{40,72},{48,80},{56,88},{... | collective-permute-start | bytes 172040 | tf_op jit(solution)/shard_map/ppermute | solution.py:238
  51.0 5.7 %collective-permute-start.14 = (bf16[32,896]{1,0:T(8,128)(2,1)S(1)}, bf16[32,896]{1,0:T(8,128)(2,1)S(1)}, u32[]{:S(2)}, u32[]{:S(2)}) collective-permute-start(bf16[32,896]{1,0:T(8,128)(2,1)S(1)} %added.10.refs_3_), channel_id=1, source_target_pairs={{0,64},{8,72},{16,80},{24,88},{32,96},{40,104},{48,112},{56,120},{... | collective-permute-start | bytes 172040 | tf_op jit(solution)/shard_map/ppermute | solution.py:238
  56.7 6.3 %collective-permute-start.19 = (bf16[32,896]{1,0:T(8,128)(2,1)S(1)}, bf16[32,896]{1,0:T(8,128)(2,1)S(1)}, u32[]{:S(2)}, u32[]{:S(2)}) collective-permute-start(bf16[32,896]{1,0:T(8,128)(2,1)S(1)} %added.11.refs_0_), channel_id=1, source_target_pairs={{0,8},{8,0},{16,24},{24,16},{32,40},{40,32},{48,56},{56,48},{64,72... | collective-permute-start | bytes 172040 | tf_op jit(solution)/shard_map/ppermute | solution.py:238
  56.8 6.3 %collective-permute-start.18 = (bf16[32,896]{1,0:T(8,128)(2,1)S(1)}, bf16[32,896]{1,0:T(8,128)(2,1)S(1)}, u32[]{:S(2)}, u32[]{:S(2)}) collective-permute-start(bf16[32,896]{1,0:T(8,128)(2,1)S(1)} %added.11.refs_0_), channel_id=1, source_target_pairs={{0,16},{8,24},{16,0},{24,8},{32,48},{40,56},{48,32},{56,40},{64,80... | collective-permute-start | bytes 172040 | tf_op jit(solution)/shard_map/ppermute | solution.py:238
  59.4 5.9 %collective-permute-start.17 = (bf16[32,896]{1,0:T(8,128)(2,1)S(1)}, bf16[32,896]{1,0:T(8,128)(2,1)S(1)}, u32[]{:S(2)}, u32[]{:S(2)}) collective-permute-start(bf16[32,896]{1,0:T(8,128)(2,1)S(1)} %added.11.refs_0_), channel_id=1, source_target_pairs={{0,24},{8,16},{16,8},{24,0},{32,56},{40,48},{48,40},{56,32},{64,88... | collective-permute-start | bytes 172040 | tf_op jit(solution)/shard_map/ppermute | solution.py:238
